TPU v7x, 32 devices: a whole 2x2x4 slice. The times are simulated.
32 devices in a mesh: elem: 4 (over z), span: 8 (over y, x, core).
Axes of the slice: x: 2, y: 2, z: 4, core: 2. Of those that a mesh axis runs over, the one named last changes fastest.
Arguments:
- state: float32 [4, 256, 9216], P(None, 'span', 'elem'), may hold values from -6 to 6
- metric: float32 [2, 256], P(None, 'elem'), may hold values from -40 to 40, as said below
- neighbour: int32 [256, 4], P('elem'), may hold values from 0 to 287, as said below
- orient: int32 [256, 4], P('elem'), may hold values from 0 to 1, as said below
- wall: int32 [256, 4], P('elem'), may hold values from 0 to 1, as said below
- rim: int32 [2, 64], P(None, 'elem'), may hold values from 0 to 255, as said below
Outputs:
- updated: float32 [4, 256, 9216], P(None, 'span', 'elem')
Inputs may be any that keep to these rules, and one draw needn't show every extreme that they name: neighbour[e, s] is a slot of e's element group's trace pool: e' * 4 + s' for the facing side s' of a local element e' (local index within the group), 256 + r for row r of the lower group's rim, 272 + r for row r of the upper group's rim; on a wall side it is e's own slot. Elements form a channel of 16 rows and 4 columns per group, periodic in x over the groups, in an order drawn per group; elements may be reflected in either reference direction. `orient`: 0 on wall sides. `wall`: 1 exactly on the sides of the first and last rows that face the walls. rim[0, g * 16 + r] is the local slot e * 4 + s of the side of group g's first-column element in row r that faces the lower group; rim[1] likewise for the last column and the upper group. Nonzero; the magnitude of metric[0] is equal along a global column of elements, that of metric[1] along a row; the sign is -1 where the element is reflected in that direction.
All inputs are finite; a program needn't handle non-finite values.
Results may differ from a plain program's by a relative error of at most 0.0003.
Values sent between devices are 32-bit elements; how exact they have to be, the bound alone decides.
No kernel may reach another device: no remote copies, remote signals or barrier semaphores. Data moves between devices by JAX's collectives and lax.ppermute only.
A program may use at most 64 MiB of HBM per device.

v0:
```python
import functools
import math

import jax
import jax.numpy as jnp
import numpy as np
from jax import lax
from jax.experimental import pallas as pl
from jax.experimental.pallas import tpu as pltpu
from jax.sharding import PartitionSpec as P


TIME_STEP = 0.001
VISCOSITY = 0.02
PENALTY = 1.0
HIGHEST = lax.Precision.HIGHEST
SIDE = 6
NODES = SIDE * SIDE
LANES = 128
SUB = 8
CHUNK = 3 * LANES
RIM_NODES = [p for p in range(NODES) if p // SIDE in (0, 5) or p % SIDE in (0, 5)]
CORE_NODES = [p for p in range(NODES) if p not in RIM_NODES]
PARTS = (RIM_NODES, CORE_NODES)


def gll_matrix():
    near_point = math.sqrt(1.0 / 3.0 - 2.0 * math.sqrt(7.0) / 21.0)
    far_point = math.sqrt(1.0 / 3.0 + 2.0 * math.sqrt(7.0) / 21.0)
    points = np.array([-1.0, -far_point, -near_point, near_point, far_point, 1.0])
    weights = np.array(
        [
            1.0
            / np.prod([points[column] - points[second] for second in range(6) if second != column])
            for column in range(6)
        ]
    )
    deriv = np.zeros((6, 6))
    for target in range(6):
        for source in range(6):
            if source != target:
                deriv[target, source] = (
                    weights[source] / weights[target] / (points[target] - points[source])
                )
        deriv[target, target] = -np.sum(deriv[target])
    return deriv


def basis_matrix(count):
    mode = np.arange(count)[:, None]
    plane = np.arange(count)[None, :]
    angle = (mode // 2 * plane % count) * (2.0 * math.pi / count)
    table = np.where(mode % 2 == 1, np.sin(angle), np.cos(angle)) * math.sqrt(2.0 / count)
    table = np.where(mode == 0, 1.0 / math.sqrt(count), table)
    return np.where(mode == 1, (1.0 - 2.0 * (plane % 2)) / math.sqrt(count), table)


def halves(table):
    table = np.asarray(table, np.float32)
    high = table.astype(jnp.bfloat16)
    low = (table - high.astype(np.float32)).astype(jnp.bfloat16)
    return high, low


def forward_tables(count):
    return halves(basis_matrix(count))


def backward_tables(count):
    basis = basis_matrix(count)
    wave = np.arange(count) // 2
    swapped = np.empty_like(basis)
    swapped[0::2] = wave[0::2, None] * basis[1::2]
    swapped[1::2] = -wave[1::2, None] * basis[0::2]
    damp_wave = np.where(np.arange(count) == 1, count // 2, wave).astype(np.float64)
    factor = TIME_STEP / (1.0 + TIME_STEP * VISCOSITY * damp_wave * damp_wave)
    return halves(factor[:, None] * np.concatenate([basis, -swapped], axis=1))


def split(value):
    high = value.astype(jnp.bfloat16)
    low = (value - high.astype(jnp.float32)).astype(jnp.bfloat16)
    return high, low


def mm(a, b):
    return lax.dot_general(a, b, (((1,), (0,)), ((), ())), preferred_element_type=jnp.float32)


def mm_nt(a, b):
    return lax.dot_general(a, b, (((1,), (1,)), ((), ())), preferred_element_type=jnp.float32)


def regroup(parts, lane):
    quarter = LANES // 4
    low_half = lane < 2 * quarter
    rolled = [pltpu.roll(part, 2 * quarter, 1) for part in parts]
    first = [
        jnp.where(low_half, parts[0], rolled[2]),
        jnp.where(low_half, parts[1], rolled[3]),
        jnp.where(low_half, rolled[0], parts[2]),
        jnp.where(low_half, rolled[1], parts[3]),
    ]
    even = lane // quarter % 2 == 0
    out = []
    for pair in (0, 2):
        a, b = first[pair], first[pair + 1]
        out.append(jnp.where(even, a, pltpu.roll(b, quarter, 1)))
        out.append(jnp.where(even, pltpu.roll(a, LANES - quarter, 1), b))
    return out


def spread_kernel(dims, where_ref, near_any, wall_any, rim_any, metric_any, state_any, *refs):
    rows, cols, share, span = dims
    sends = [refs[:span], refs[span : 2 * span]]
    pick_ref, facts_ref = refs[2 * span : 2 * span + 2]
    halo_ref, bends_ref, near_ref, wall_ref, rim_ref, metric_ref, state_ref, flat, sems = refs[2 * span + 2 :]
    me = where_ref[0]
    elems = rows * cols
    width = elems * NODES
    small = [
        pltpu.make_async_copy(source, target, sems.at[at])
        for at, (source, target) in enumerate(
            (
                (near_any, near_ref),
                (wall_any, wall_ref),
                (rim_any, rim_ref),
                (metric_any, metric_ref),
            )
        )
    ]
    large = [
        pltpu.make_async_copy(
            state_any.at[:, pl.ds(at, CHUNK)],
            state_ref.at[:, pl.ds(at, CHUNK)],
            sems.at[len(small) + at // CHUNK],
        )
        for at in range(0, width, CHUNK)
    ]
    for copy in small + large:
        copy.start()
    for copy in small:
        copy.wait()
    lane = lax.broadcasted_iota(jnp.int32, (1, LANES), 1) % elems
    lines = share // cols
    halo_ref[...] = jnp.zeros_like(halo_ref)
    bends_ref[...] = jnp.zeros_like(bends_ref)
    before = None
    for row in range(rows):
        cell = rim_ref[0, row] >> 2
        face = rim_ref[0, row] & 1
        here = []
        for col in range(cols):
            if row == 0:
                flip_y = wall_ref[3, cell]
            else:
                flip_y = jnp.where(near_ref[3, cell] >> 2 == before[col], 1, 0)
            here.append(cell)
            place = row * cols + col
            at = (place // share ^ me) * share + place % share
            chosen = jnp.where(lane == cell, 1.0, 0.0)
            pick_ref[pl.ds(at, 1), :] = chosen
            if row % lines == lines - 1 and row + 1 < rows:
                under = ((row // lines + 1) ^ me) * share + col
                halo_ref[pl.ds(under, 1), :] = chosen
                for kind, bend in enumerate((face, 1 - flip_y)):
                    bends_ref[kind, pl.ds(under, 1), :] = jnp.full((1, LANES), bend, jnp.int32)
            if row % lines == 0 and row > 0:
                over = ((row // lines - 1) ^ me) * share + cols + col
                halo_ref[pl.ds(over, 1), :] = chosen
                for kind, bend in enumerate((face, flip_y)):
                    bends_ref[kind, pl.ds(over, 1), :] = jnp.full((1, LANES), bend, jnp.int32)
            facts = (
                metric_ref[0, cell],
                metric_ref[1, cell],
                face.astype(jnp.float32),
                flip_y.astype(jnp.float32),
            )

            @pl.when(at < share)
            def _(at=at, facts=facts):
                for kind, fact in enumerate(facts):
                    facts_ref[kind, pl.ds(at, 1), :] = jnp.full((1, LANES), fact, jnp.float32)

            if col + 1 < cols:
                step = near_ref[face ^ 1, cell]
                cell = step >> 2
                face = step & 1
        before = here
    for at in range(0, width, LANES):
        if at % CHUNK == 0:
            large[at // CHUNK].wait()
        flat[pl.ds(at, LANES), :] = state_ref[:, pl.ds(at, LANES)].T
    pick = pick_ref[...].astype(jnp.bfloat16)
    both = jnp.concatenate([pick, halo_ref[...].astype(jnp.bfloat16)], axis=0)
    edge = {}
    for nodes, outs in zip(PARTS, sends):
        for at, node in enumerate(nodes):
            high, low = split(flat[pl.ds(node, elems, stride=NODES), :])
            wanted = node % SIDE in (0, 5)
            moved = mm(both if wanted else pick, jnp.concatenate([high, low], axis=0))
            if wanted:
                edge[divmod(node, SIDE)] = moved[elems:]
            for step in range(span):
                outs[step][pl.ds(at * share, share), :] = moved[step * share : (step + 1) * share]
    bend_x = bends_ref[0] == 1
    bend_y = bends_ref[1] == 1
    trace = [jnp.where(bend_y, edge[t, 5], edge[t, 0]) for t in range(SIDE)]
    for t in range(SIDE):
        moved = jnp.where(bend_x, trace[SIDE - 1 - t], trace[t])
        at = pl.ds((len(RIM_NODES) + t) * share, share)
        for step in range(span):
            sends[0][step][at, :] = moved[step * share : (step + 1) * share]


def along(trace, flip):
    return [jnp.where(flip, trace[SIDE - 1 - t], trace[t]) for t in range(SIDE)]


def sides_x(value, flip_x, flip_y):
    low = [jnp.where(flip_x, value(5, t), value(0, t)) for t in range(SIDE)]
    high = [jnp.where(flip_x, value(0, t), value(5, t)) for t in range(SIDE)]
    return along(low, flip_y), along(high, flip_y)


def sides_y(value, flip_x, flip_y):
    low = [jnp.where(flip_y, value(t, 5), value(t, 0)) for t in range(SIDE)]
    high = [jnp.where(flip_y, value(t, 0), value(t, 5)) for t in range(SIDE)]
    return along(low, flip_x), along(high, flip_x)


def rim_reader(ref, tile, var):
    return lambda i, j: ref[tile, var, pl.ds(RIM_NODES.index(SIDE * i + j) * SUB, SUB), :]


def back(one, two, flip, flip_along):
    return along([jnp.where(flip, two[t], one[t]) for t in range(SIDE)], flip_along)


def sign(value):
    return jnp.where(value < 0.0, -1.0, 1.0)


def to_planes(dims, me, high_ref, low_ref, takes, phys_ref):
    _, _, span, num_vars, modes = dims
    lane = lax.broadcasted_iota(jnp.int32, (1, LANES), 1)
    tables = []
    for ref in (high_ref, low_ref):
        tables.append(
            jnp.concatenate([ref[pl.ds((me ^ k) * modes, modes), :] for k in range(span)], axis=0)
        )
    pieces = []
    for group in range(span // 4):
        pieces.append(regroup([takes[4 * group + q][...] for q in range(4)], lane))
    for var in range(num_vars):
        high, low = split(jnp.concatenate([piece[var] for piece in pieces], axis=1))
        planes = mm(high, tables[0]) + mm(low, tables[0]) + mm(high, tables[1])
        for tile in range(span * modes // LANES):
            phys_ref[tile, var] = planes[:, tile * LANES : (tile + 1) * LANES]


def planes_kernel(dims, where_ref, facts_ref, high_ref, low_ref, *refs):
    cols, share, span, num_vars, modes = dims
    takes = refs[:span]
    phys_ref, one_ref, two_ref = refs[span:]
    to_planes(dims, where_ref[0], high_ref, low_ref, takes, phys_ref)
    odd = where_ref[1] == 1
    lines = share // cols
    flip_x = facts_ref[2] > 0.5
    flip_y = facts_ref[3] > 0.5
    turn_x = sign(facts_ref[0]) * (1.0 - 2.0 * facts_ref[2])
    for tile in range(span * modes // LANES):
        speed = sides_x(rim_reader(phys_ref, tile, 0), flip_x, flip_y)
        for var in range(num_vars):
            trace = sides_x(rim_reader(phys_ref, tile, var), flip_x, flip_y)
            for t in range(SIDE):
                low_x = (1.0 - turn_x * speed[0][t]) * trace[0][t]
                high_x = (1.0 + turn_x * speed[1][t]) * trace[1][t]
                for line in range(lines):
                    at = pl.ds(t * lines + line, 1)
                    up = high_x[(line + 1) * cols - 1 : (line + 1) * cols]
                    down = low_x[line * cols : line * cols + 1]
                    one_ref[tile, var, at, :] = jnp.where(odd, down, up)
                    two_ref[tile, var, at, :] = jnp.where(odd, up, down)


def to_modes(dims, me, high_ref, low_ref, rates):
    _, _, span, _, modes = dims
    lane = lax.broadcasted_iota(jnp.int32, (1, LANES), 1)
    tables = []
    for ref in (high_ref, low_ref):
        tables.append(
            jnp.concatenate([ref[pl.ds((me ^ k) * modes, modes), :] for k in range(span)], axis=0)
        )
    gains = []
    for rate in rates:
        high, low = split(rate)
        gains.append(mm_nt(high, tables[0]) + mm_nt(low, tables[0]) + mm_nt(high, tables[1]))
    out = []
    for group in range(span // 4):
        at = slice(group * LANES, (group + 1) * LANES)
        out += regroup([gain[:, at] for gain in gains], lane)
    return out


def rates_kernel(
    dims, where_ref, facts_ref, there_high, there_low, high_ref, low_ref, phys_ref, *refs
):
    cols, _, span, num_vars, modes = dims
    mid_ref, edge_ref, core_ref, rate_ref = refs[span:]
    me = where_ref[0]
    to_planes(dims, me, there_high, there_low, refs[:span], core_ref)
    count = span * modes
    deriv = np.asarray(gll_matrix(), np.float32)
    slot = lax.broadcasted_iota(jnp.int32, (SUB, LANES), 0)
    flip_x = facts_ref[2] > 0.5
    flip_y = facts_ref[3] > 0.5
    scale_x = facts_ref[0]
    scale_y = facts_ref[1]
    turn_x = sign(scale_x) * (1.0 - 2.0 * facts_ref[2])
    turn_y = sign(scale_y) * (1.0 - 2.0 * facts_ref[3])
    weight_x = 7.5 * jnp.abs(scale_x)
    weight_y = 7.5 * jnp.abs(scale_y)
    first_col = slot % cols == 0
    last_col = slot % cols == cols - 1
    first_line = slot < cols
    turn_halo = jnp.where(first_line, turn_y, -turn_y)
    floor = jnp.logical_and(first_line, me == 0)
    roof = jnp.logical_and(jnp.logical_not(first_line), me == span - 1)

    for tile in range(count // LANES):

        def reader(var, tile=tile):
            def read(i, j):
                node = SIDE * i + j
                ref = phys_ref if node in RIM_NODES else core_ref
                nodes = RIM_NODES if node in RIM_NODES else CORE_NODES
                return ref[tile, var, pl.ds(nodes.index(node) * SUB, SUB), :]

            return read

        def halo(var, t, tile=tile):
            return phys_ref[tile, var, pl.ds((len(RIM_NODES) + t) * SUB, SUB), :]

        speed_x = sides_x(reader(0), flip_x, flip_y)
        speed_y = sides_y(reader(1), flip_x, flip_y)
        pace_x = [[turn_x * speed for speed in side] for side in speed_x]
        pace_y = [[turn_y * speed for speed in side] for side in speed_y]
        for var in range(num_vars):
            q = reader(var)
            mirror = 1.0 if var == num_vars - 1 else -1.0
            total = {}
            for j in range(SIDE):
                flux = [q(i, j) * reader(0)(i, j) for i in range(SIDE)]
                for i in range(SIDE):
                    acc = None
                    for s in range(SIDE):
                        if abs(deriv[i, s]) > 1e-6:
                            term = flux[s] * float(deriv[i, s])
                            acc = term if acc is None else acc + term
                    total[i, j] = -scale_x * acc
            for i in range(SIDE):
                flux = [q(i, j) * reader(1)(i, j) for j in range(SIDE)]
                for j in range(SIDE):
                    acc = None
                    for s in range(SIDE):
                        if abs(deriv[j, s]) > 1e-6:
                            term = flux[s] * float(deriv[j, s])
                            acc = term if acc is None else acc + term
                    total[i, j] = total[i, j] - scale_y * acc
            trace = sides_x(q, flip_x, flip_y)
            low, high = [], []
            for t in range(SIDE):
                pace, value = pace_x[0][t], trace[0][t]
                own_low, give_low = -(pace + 1.0) * value, (1.0 - pace) * value
                pace, value = pace_x[1][t], trace[1][t]
                own_high, give_high = (pace - 1.0) * value, (1.0 + pace) * value
                from_low = jnp.where(first_col, 0.0, pltpu.roll(give_high, 1, 0))
                from_high = jnp.where(last_col, 0.0, pltpu.roll(give_low, SUB - 1, 0))
                low.append(weight_x * (own_low + from_low))
                high.append(weight_x * (own_high + from_high))
            for i, side in (
                (0, back(low, high, flip_x, flip_y)),
                (5, back(high, low, flip_x, flip_y)),
            ):
                for t in range(SIDE):
                    total[i, t] = total[i, t] + side[t]
            trace = sides_y(q, flip_x, flip_y)
            low, high = [], []
            for t in range(SIDE):
                pace, value = pace_y[0][t], trace[0][t]
                own_low, give_low = -(pace + 1.0) * value, (1.0 - pace) * value
                pace, value = pace_y[1][t], trace[1][t]
                own_high, give_high = (pace - 1.0) * value, (1.0 + pace) * value
                outside = (1.0 + turn_halo * halo(1, t)) * halo(var, t)
                outside = jnp.where(floor, mirror * give_low, outside)
                outside = jnp.where(roof, mirror * give_high, outside)
                from_low = jnp.where(first_line, outside, pltpu.roll(give_high, cols, 0))
                from_high = jnp.where(first_line, pltpu.roll(give_low, SUB - cols, 0), outside)
                low.append(weight_y * (own_low + from_low))
                high.append(weight_y * (own_high + from_high))
            for j, side in (
                (0, back(low, high, flip_y, flip_x)),
                (5, back(high, low, flip_y, flip_x)),
            ):
                for t in range(SIDE):
                    total[t, j] = total[t, j] + side[t]
            for i in range(SIDE):
                for j in range(SIDE):
                    if i in (0, 5):
                        ref, node = edge_ref, i // 5 * SIDE + j
                    else:
                        ref, node = rate_ref, SIDE * (i - 1) + j
                    at = pl.ds(node * SUB, SUB)
                    ref[var, at, pl.ds(tile * LANES, LANES)] = total[i, j]
                    ref[var, at, pl.ds(count + tile * LANES, LANES)] = q(i, j) * reader(2)(i, j)
    parts = to_modes(dims, me, high_ref, low_ref, [rate_ref[var] for var in range(num_vars)])
    for k in range(span):
        mid_ref[k] = parts[k]


def edges_kernel(
    dims, where_ref, facts_ref, high_ref, low_ref, mid_ref, edge_ref, one_ref, two_ref, *refs
):
    cols, share, span, num_vars, modes = dims
    outs = refs[:span]
    rate_ref = refs[span]
    count = span * modes
    lines = share // cols
    odd = where_ref[1] == 1
    slot = lax.broadcasted_iota(jnp.int32, (SUB, LANES), 0)
    flip_x = facts_ref[2] > 0.5
    flip_y = facts_ref[3] > 0.5
    weight = 7.5 * jnp.abs(facts_ref[0])
    for tile in range(count // LANES):
        for var in range(num_vars):
            low, high = [], []
            for t in range(SIDE):
                below, above = jnp.zeros((SUB, LANES)), jnp.zeros((SUB, LANES))
                for line in range(lines):
                    at = pl.ds(t * lines + line, 1)
                    one, two = one_ref[tile, var, at, :], two_ref[tile, var, at, :]
                    below = jnp.where(slot == line * cols, jnp.where(odd, one, two), below)
                    above = jnp.where(
                        slot == (line + 1) * cols - 1, jnp.where(odd, two, one), above
                    )
                low.append(weight * below)
                high.append(weight * above)
            for i, side in enumerate(
                (back(low, high, flip_x, flip_y), back(high, low, flip_x, flip_y))
            ):
                for t in range(SIDE):
                    at = (pl.ds((i * SIDE + t) * SUB, SUB), pl.ds(tile * LANES, LANES))
                    rate_ref[var, at[0], at[1]] = edge_ref[var, at[0], at[1]] + side[t]
    rates = [
        jnp.concatenate([rate_ref[var], edge_ref[var, :, count:]], axis=1)
        for var in range(num_vars)
    ]
    parts = to_modes(dims, where_ref[0], high_ref, low_ref, rates)
    half = SIDE * share
    for k in range(span):
        outs[k][:half] = parts[k][:half]
        outs[k][half : (NODES - SIDE) * share] = mid_ref[k]
        outs[k][(NODES - SIDE) * share :] = parts[k][half:]


def gather_kernel(dims, where_ref, pick_ref, state_ref, *refs):
    rows, cols, share, span, modes = dims
    takes = refs[:span]
    out_any, flat, out_ref, sems = refs[span:]
    elems = rows * cols
    count = span * modes
    turned = pick_ref[...].T[:elems]
    pick = jnp.concatenate([turned] * (LANES // elems), axis=1).astype(jnp.bfloat16)
    for node in range(NODES):
        part = jnp.concatenate([take[pl.ds(node * share, share), :] for take in takes], axis=0)
        high, low = split(part)
        flat[pl.ds(node, elems, stride=NODES), :] = mm(pick, jnp.concatenate([high, low], axis=0))
    index = where_ref[0] * modes + lax.broadcasted_iota(jnp.int32, (LANES, 1), 0) % modes
    wave = jnp.where(index == 1, count // 2, index // 2).astype(jnp.float32)
    damping = 1.0 / (1.0 + TIME_STEP * VISCOSITY * wave * wave)
    copies = []
    for start in range(0, elems * NODES, CHUNK):
        for block in range(start, start + CHUNK, LANES):
            at = pl.ds(block, LANES)
            out_ref[:, at] = state_ref[:, at] * damping + flat[at, :].T
        at = pl.ds(start, CHUNK)
        copies.append(
            pltpu.make_async_copy(out_ref.at[:, at], out_any.at[:, at], sems.at[start // CHUNK])
        )
        copies[-1].start()
    for copy in copies:
        copy.wait()


def smem():
    return pl.BlockSpec(memory_space=pltpu.SMEM)


def in_hbm(array):
    return pltpu.with_memory_space_constraint(array, pltpu.HBM)


def anywhere(count):
    return [pl.BlockSpec(memory_space=pltpu.HBM)] * count


def vmem(count):
    return [pl.BlockSpec(memory_space=pltpu.VMEM)] * count


PARAMS = pltpu.CompilerParams(vmem_limit_bytes=24 * 1024 * 1024)


def exchange(blocks, span):
    taken = {0: blocks[0]}
    for k in range(1, span):
        taken[k] = lax.ppermute(blocks[k], "span", [(s, s ^ k) for s in range(span)])
    return [taken[k] for k in range(span)]


def ordered_body(state, metric, neighbour, wall, rim):
    num_vars, modes, flat_size = state.shape
    elems = flat_size // NODES
    span = lax.axis_size("span")
    groups = lax.axis_size("elem")
    share = elems // span
    rows = rim.shape[1]
    cols = elems // rows
    count = modes * span
    tiles = count // LANES
    lines = share // cols
    me = jnp.stack([lax.axis_index("span"), lax.axis_index("elem") % 2])
    flat_state = state.reshape(num_vars * modes, flat_size)
    f32 = jnp.float32
    whole, rim_part, core_part = (
        jax.ShapeDtypeStruct((nodes * share, LANES), f32)
        for nodes in (NODES, len(RIM_NODES) + SIDE, len(CORE_NODES))
    )
    chunks = flat_size // CHUNK
    first = pl.pallas_call(
        functools.partial(spread_kernel, (rows, cols, share, span)),
        out_shape=[rim_part] * span
        + [core_part] * span
        + [
            jax.ShapeDtypeStruct((elems, LANES), f32),
            jax.ShapeDtypeStruct((4, share, LANES), f32),
        ],
        in_specs=[smem()] + anywhere(5),
        out_specs=vmem(2 * span + 2),
        scratch_shapes=[
            pltpu.VMEM((elems, LANES), f32),
            pltpu.VMEM((2, elems, LANES), jnp.int32),
            pltpu.SMEM(neighbour.T.shape, jnp.int32),
            pltpu.SMEM(wall.T.shape, jnp.int32),
            pltpu.SMEM(rim.shape, jnp.int32),
            pltpu.SMEM(metric.shape, f32),
            pltpu.VMEM(flat_state.shape, f32),
            pltpu.VMEM((flat_size, LANES), f32),
            pltpu.SemaphoreType.DMA((4 + chunks,)),
        ],
        compiler_params=PARAMS,
        name="spread",
    )(me, *[in_hbm(x) for x in (neighbour.T, wall.T, rim, metric, flat_state)])
    rim_takes = exchange(first[:span], span)
    core_takes = exchange(first[span : 2 * span], span)
    pick, facts = first[2 * span :]

    dims = (cols, share, span, num_vars, modes)
    forward = [jnp.asarray(t) for t in forward_tables(count)]
    backward = [jnp.asarray(t) for t in backward_tables(count)]
    line_shape = jax.ShapeDtypeStruct((tiles, num_vars, SIDE * lines, LANES), f32)
    planes = pl.pallas_call(
        functools.partial(planes_kernel, dims),
        out_shape=[
            jax.ShapeDtypeStruct((tiles, num_vars, (len(RIM_NODES) + SIDE) * share, LANES), f32),
            line_shape,
            line_shape,
        ],
        in_specs=[smem()] + vmem(3 + span),
        out_specs=vmem(3),
        compiler_params=PARAMS,
        name="planes",
    )
    phys, one, two = planes(me, facts, *forward, *rim_takes)
    one = lax.ppermute(one, "elem", [(g, g ^ 1) for g in range(groups)])
    two = lax.ppermute(
        two, "elem", [(g, (g - 1 if g % 2 == 0 else g + 1) % groups) for g in range(groups)]
    )

    middle = NODES - 2 * SIDE
    rates = pl.pallas_call(
        functools.partial(rates_kernel, dims),
        out_shape=[
            jax.ShapeDtypeStruct((span, middle * share, LANES), f32),
            jax.ShapeDtypeStruct((num_vars, 2 * SIDE * share, 2 * count), f32),
        ],
        in_specs=[smem()] + vmem(6 + span),
        out_specs=vmem(2),
        scratch_shapes=[
            pltpu.VMEM((tiles, num_vars, len(CORE_NODES) * share, LANES), f32),
            pltpu.VMEM((num_vars, middle * share, 2 * count), f32),
        ],
        compiler_params=PARAMS,
        name="rates",
    )
    mid, edge = rates(me, facts, *forward, *backward, phys, *core_takes)
    gains = pl.pallas_call(
        functools.partial(edges_kernel, dims),
        out_shape=[whole] * span,
        in_specs=[smem()] + vmem(7),
        out_specs=vmem(span),
        scratch_shapes=[pltpu.VMEM((num_vars, 2 * SIDE * share, count), f32)],
        compiler_params=PARAMS,
        name="edges",
    )(me, facts, *backward, mid, edge, one, two)
    takes = exchange(gains, span)

    out = pl.pallas_call(
        functools.partial(gather_kernel, (rows, cols, share, span, modes)),
        out_shape=jax.ShapeDtypeStruct((num_vars * modes, flat_size), f32),
        in_specs=[smem()] + vmem(2 + span),
        out_specs=pl.BlockSpec(memory_space=pltpu.HBM),
        scratch_shapes=[
            pltpu.VMEM((flat_size, LANES), f32),
            pltpu.VMEM(flat_state.shape, f32),
            pltpu.SemaphoreType.DMA((chunks,)),
        ],
        compiler_params=PARAMS,
        name="collect",
    )(me, pick, flat_state, *takes)
    return out.reshape(state.shape)


def from_behind(value, axis, steps):
    count = lax.axis_size(axis)
    pairs = [(source, (source + steps) % count) for source in range(count)]
    return lax.ppermute(value, axis, pairs)


def gll_tables():
    near_point = math.sqrt(1.0 / 3.0 - 2.0 * math.sqrt(7.0) / 21.0)
    far_point = math.sqrt(1.0 / 3.0 + 2.0 * math.sqrt(7.0) / 21.0)
    points = np.array([-1.0, -far_point, -near_point, near_point, far_point, 1.0])
    weights = np.array(
        [
            1.0
            / np.prod([points[column] - points[second] for second in range(6) if second != column])
            for column in range(6)
        ]
    )
    deriv = np.zeros((6, 6))
    for target in range(6):
        for source in range(6):
            if source != target:
                deriv[target, source] = (
                    weights[source] / weights[target] / (points[target] - points[source])
                )
        deriv[target, target] = -np.sum(deriv[target])
    identity = np.eye(6)
    along_x = np.kron(deriv, identity)
    along_y = np.kron(identity, deriv)
    edge_nodes = np.array(
        [
            [offset for offset in range(6)],
            [30 + offset for offset in range(6)],
            [6 * offset for offset in range(6)],
            [6 * offset + 5 for offset in range(6)],
        ]
    ).reshape(-1)
    lifting = np.zeros((36, 24))
    lifting[edge_nodes, np.arange(24)] = 1.0
    return (
        jnp.asarray(along_x, jnp.float32),
        jnp.asarray(along_y, jnp.float32),
        edge_nodes,
        jnp.asarray(lifting, jnp.float32),
    )


def spanwise_basis(count):
    mode_index = jnp.arange(count, dtype=jnp.int32)
    planes = jnp.arange(count, dtype=jnp.int32)
    phase = mode_index[:, None] // 2 * planes[None, :] % count
    phase_angle = phase.astype(jnp.float32) * (2.0 * math.pi / count)
    odd_rows = (mode_index % 2 == 1)[:, None]
    basis_table = jnp.where(odd_rows, jnp.sin(phase_angle), jnp.cos(phase_angle)) * math.sqrt(
        2.0 / count
    )
    alternate = (1 - 2 * (planes % 2)).astype(jnp.float32) / math.sqrt(count)
    constant = jnp.ones((count,), jnp.float32) / math.sqrt(count)
    basis_table = jnp.where(mode_index[:, None] == 0, constant[None, :], basis_table)
    basis_table = jnp.where(mode_index[:, None] == 1, alternate[None, :], basis_table)
    return basis_table


def spanwise_derivative(modal):
    shape_in = modal.shape
    paired = modal.reshape(shape_in[0], shape_in[1] // 2, 2, shape_in[2])
    wavenumber = jnp.arange(shape_in[1] // 2, dtype=jnp.int32).astype(jnp.float32)[None, :, None]
    return jnp.stack([wavenumber * paired[:, :, 1], -wavenumber * paired[:, :, 0]], axis=2).reshape(
        shape_in
    )


def planar_terms(flux_x, flux_y, metric_part):
    along_x, along_y, edge_nodes, _ = gll_tables()
    scale_x = metric_part[0][:, None]
    scale_y = metric_part[1][:, None]
    grad_x = jnp.einsum("pq,vmeq->vmep", along_x, flux_x, precision=HIGHEST)
    grad_y = jnp.einsum("pq,vmeq->vmep", along_y, flux_y, precision=HIGHEST)
    planar = scale_x * grad_x + scale_y * grad_y
    sign_x = jnp.sign(scale_x)
    sign_y = jnp.sign(scale_y)
    edge_flux = jnp.concatenate(
        [
            -sign_x * flux_x[:, :, :, edge_nodes[0:6]],
            sign_x * flux_x[:, :, :, edge_nodes[6:12]],
            -sign_y * flux_y[:, :, :, edge_nodes[12:18]],
            sign_y * flux_y[:, :, :, edge_nodes[18:24]],
        ],
        axis=3,
    )
    return (planar, edge_flux)


def node_major(flat, num_vars, local_modes, nodes, local_elems):
    return jnp.transpose(flat.reshape(num_vars, local_modes, local_elems, nodes), (0, 1, 3, 2))


def trace_pool(traces):
    shape_in = traces.shape
    return (
        traces.reshape(shape_in[0], shape_in[1], 4, 6, shape_in[3])
        .transpose(0, 1, 3, 4, 2)
        .reshape(shape_in[0], shape_in[1], 6, 4 * shape_in[3])
    )


def own_pools(state_local, normal_flux):
    edge_nodes = gll_tables()[2]
    return (trace_pool(state_local[:, :, edge_nodes, :]), trace_pool(normal_flux))


def update(
    state_local,
    divergence,
    own_q,
    own_flux,
    from_lower,
    from_upper,
    neighbour,
    orient,
    wall,
    metric_local,
    first_mode,
    total_modes,
):
    lifting = gll_tables()[3]
    num_vars, modes_here, _, count = state_local.shape
    pool_q = jnp.concatenate([own_q, from_lower[0], from_upper[0]], axis=3)
    pool_flux = jnp.concatenate([own_flux, from_lower[1], from_upper[1]], axis=3)
    flat_index = neighbour.reshape(-1)
    other_q = jnp.take(pool_q, flat_index, axis=3)
    other_flux = jnp.take(pool_flux, flat_index, axis=3)
    flipped = orient.reshape(-1) == 1
    other_q = jnp.where(flipped, other_q[:, :, ::-1, :], other_q)
    other_flux = jnp.where(flipped, other_flux[:, :, ::-1, :], other_flux)
    mirror = jnp.array([-1.0, -1.0, -1.0, 1.0], jnp.float32).reshape(4, 1, 1, 1)
    walled = wall.reshape(-1) == 1
    other_q = jnp.where(walled, mirror * own_q, other_q)
    other_flux = jnp.where(walled, mirror * own_flux, other_flux)
    magnitude = (
        jnp.abs(
            jnp.stack([metric_local[0], metric_local[0], metric_local[1], metric_local[1]], axis=1)
        ).reshape(-1)
        * 15.0
    )
    surface_jump = magnitude * (0.5 * (own_flux + other_flux) - 0.5 * PENALTY * (own_q - other_q))
    unpooled = (
        surface_jump.reshape(num_vars, modes_here, 6, count, 4)
        .transpose(0, 1, 4, 2, 3)
        .reshape(num_vars, modes_here, 24, count)
    )
    surface = jnp.einsum("pq,vmqe->vmpe", lifting, unpooled, precision=HIGHEST)
    mode_index = first_mode + jnp.arange(modes_here, dtype=jnp.int32)
    wavenumber = jnp.where(mode_index == 1, total_modes // 2, mode_index // 2).astype(jnp.float32)
    damping = 1.0 + TIME_STEP * VISCOSITY * wavenumber * wavenumber
    return (state_local + TIME_STEP * (surface - divergence)) / damping[None, :, None, None]


def plain_body(state, metric, neighbour, orient, wall, rim):
    num_vars, local_modes, flat_size = state.shape
    num_nodes = 36
    local_elems = flat_size // num_nodes
    span_size = lax.axis_size("span")
    total_modes = local_modes * span_size
    share = local_elems // span_size
    state_nodes = node_major(state, num_vars, local_modes, num_nodes, local_elems)
    planes_in = lax.all_to_all(state, "span", split_axis=2, concat_axis=1, tiled=True)
    basis_table = spanwise_basis(total_modes)
    physical = jnp.einsum("mn,vmk->vnk", basis_table, planes_in, precision=HIGHEST)
    metric_part = lax.dynamic_slice_in_dim(metric, lax.axis_index("span") * share, share, axis=1)
    shape_here = (num_vars, total_modes, share, num_nodes)
    planar_div, edge_flux = planar_terms(
        (physical[0:1] * physical).reshape(shape_here),
        (physical[1:2] * physical).reshape(shape_here),
        metric_part,
    )
    volume_fields = jnp.concatenate(
        [planar_div.reshape(num_vars, total_modes, share * num_nodes), physical[2:3] * physical],
        axis=0,
    )
    volume_modal = jnp.einsum("mn,vnk->vmk", basis_table, volume_fields, precision=HIGHEST)
    edge_modal = jnp.einsum(
        "mn,vnk->vmk",
        basis_table,
        edge_flux.reshape(num_vars, total_modes, share * 24),
        precision=HIGHEST,
    )
    combined = volume_modal[0:4] + spanwise_derivative(volume_modal[4:8])
    div_flat, flux_flat = (
        lax.all_to_all(combined, "span", split_axis=1, concat_axis=2, tiled=True),
        lax.all_to_all(edge_modal, "span", split_axis=1, concat_axis=2, tiled=True),
    )
    divergence = node_major(div_flat, num_vars, local_modes, num_nodes, local_elems)
    normal_flux = node_major(flux_flat, num_vars, local_modes, 24, local_elems)
    own_q, own_flux = own_pools(state_nodes, normal_flux)
    upper_rim = jnp.stack([jnp.take(own_q, rim[1], axis=3), jnp.take(own_flux, rim[1], axis=3)])
    lower_rim = jnp.stack([jnp.take(own_q, rim[0], axis=3), jnp.take(own_flux, rim[0], axis=3)])
    from_lower = from_behind(upper_rim, "elem", 1)
    from_upper = from_behind(lower_rim, "elem", -1)
    first_mode = lax.axis_index("span") * local_modes
    result = update(
        state_nodes,
        divergence,
        own_q,
        own_flux,
        from_lower,
        from_upper,
        neighbour,
        orient,
        wall,
        metric,
        first_mode,
        total_modes,
    )
    return jnp.transpose(result, (0, 1, 3, 2)).reshape(num_vars, local_modes, flat_size)


def body(state, metric, neighbour, orient, wall, rim):
    num_vars, modes, flat_size = state.shape
    span = lax.axis_size("span")
    groups = lax.axis_size("elem")
    elems = flat_size // NODES
    rows = rim.shape[1]
    fits = (
        groups % 2 == 0
        and rows % span == 0
        and SUB == 2 * (elems // rows)
        and num_vars * modes == LANES
        and modes * 4 == LANES
        and span % 4 == 0
        and span & (span - 1) == 0
        and LANES % elems == 0
        and elems == SUB * span
        and elems % rows == 0
        and SUB % (elems // rows) == 0
        and flat_size % CHUNK == 0
    )
    if not fits:
        return plain_body(state, metric, neighbour, orient, wall, rim)
    return ordered_body(state, metric, neighbour, wall, rim)


def solution(mesh):
    placed = (
        P(None, "span", "elem"),
        P(None, "elem"),
        P("elem", None),
        P("elem", None),
        P("elem", None),
        P(None, "elem"),
    )
    return jax.shard_map(
        body, mesh=mesh, in_specs=placed, out_specs=P(None, "span", "elem"), check_vma=False
    )
```

profile of v0, /device:TPU:0, one launch (start us, length us, event | category | flops | bytes accessed | tf_op | source)
XLA Modules:
  0.0 56.2 jit_solution(1734405803678344086)
XLA Ops:
  0.0 0.0 copy-start.3
  0.0 0.0 copy-start.4
  0.0 0.1 pad_add_fusion.where_ref
  0.1 0.0 copy-start.1
  0.1 0.0 copy-start.2
  0.1 3.6 %spread.1 = (f32[208,128]{1,0:T(8,128)S(1)}, f32[208,128]{1,0:T(8,128)S(1)}, f32[208,128]{1,0:T(8,128)S(1)}, f32[208,128]{1,0:T(8,128)S(1)}, f32[208,128]{1,0:T(...) custom-call(s32[2]{0:T(128)S(1)} %pad_add_fusion.where_ref, ...), custom_call_target="tpu_custom_call" | custom-call | tf_op jit(solution)/shard_map/spread/pallas_call | solution.py:541
  3.7 0.6 collective-permute-start.7
  4.3 0.1 collective-permute-start
  4.3 2.9 %collective-permute-start.1 = (f32[208,128]{1,0:T(8,128)S(1)}, f32[208,128]{1,0:T(8,128)S(1)}, u32[]{:S(2)}, u32[]{:S(2)}) collective-permute-start(f32[208,128]{1,0:T(8,128)S(1)} %get-tuple-element.40), channel_id=1, source_target_pairs={{0,2},{1,3},{2,0},{3,1},{4,6},{5,7},{6,4},{7,5},{8,10},{9,11},{10,... | collective-permute-start | bytes 319496 | tf_op jit(solution)/shard_map/ppermute | solution.py:518
  7.3 0.0 collective-permute-start.8
  7.3 1.1 %collective-permute-start.2 = (f32[208,128]{1,0:T(8,128)S(1)}, f32[208,128]{1,0:T(8,128)S(1)}, u32[]{:S(2)}, u32[]{:S(2)}) collective-permute-start(f32[208,128]{1,0:T(8,128)S(1)} %get-tuple-element.41), channel_id=1, source_target_pairs={{0,3},{1,2},{2,1},{3,0},{4,7},{5,6},{6,5},{7,4},{8,11},{9,10},{10,... | collective-permute-start | bytes 319496 | tf_op jit(solution)/shard_map/ppermute | solution.py:518
  8.4 0.0 collective-permute-done.7.refs_1_
  8.4 1.5 %collective-permute-start.3 = (f32[208,128]{1,0:T(8,128)S(1)}, f32[208,128]{1,0:T(8,128)S(1)}, u32[]{:S(2)}, u32[]{:S(2)}) collective-permute-start(f32[208,128]{1,0:T(8,128)S(1)} %get-tuple-element.42), channel_id=1, source_target_pairs={{0,4},{1,5},{2,6},{3,7},{4,0},{5,1},{6,2},{7,3},{8,12},{9,13},{10,... | collective-permute-start | bytes 319496 | tf_op jit(solution)/shard_map/ppermute | solution.py:518
  9.9 2.6 %collective-permute-done.8.refs_2_ = f32[128,128]{1,0:T(8,128)S(1)} collective-permute-done((f32[128,128]{1,0:T(8,128)S(1)}, f32[128,128]{1,0:T(8,128)S(1)}, u32[]{:S(2)}, u32[]{:S(2)}) %collective-permute-start.8) | collective-permute-done | bytes 65568 | tf_op jit(solution)/shard_map/ppermute | solution.py:518
  12.5 0.0 collective-permute-start.4
  12.5 0.0 collective-permute-done.refs_1_
  12.5 3.0 %collective-permute-start.5 = (f32[208,128]{1,0:T(8,128)S(1)}, f32[208,128]{1,0:T(8,128)S(1)}, u32[]{:S(2)}, u32[]{:S(2)}) collective-permute-start(f32[208,128]{1,0:T(8,128)S(1)} %get-tuple-element.44), channel_id=1, source_target_pairs={{0,6},{1,7},{2,4},{3,5},{4,2},{5,3},{6,0},{7,1},{8,14},{9,15},{10,... | collective-permute-start | bytes 319496 | tf_op jit(solution)/shard_map/ppermute | solution.py:518
  15.5 0.0 collective-permute-done.1.refs_2_
  15.5 1.4 %collective-permute-start.6 = (f32[208,128]{1,0:T(8,128)S(1)}, f32[208,128]{1,0:T(8,128)S(1)}, u32[]{:S(2)}, u32[]{:S(2)}) collective-permute-start(f32[208,128]{1,0:T(8,128)S(1)} %get-tuple-element.45), channel_id=1, source_target_pairs={{0,7},{1,6},{2,5},{3,4},{4,3},{5,2},{6,1},{7,0},{8,15},{9,14},{10,... | collective-permute-start | bytes 319496 | tf_op jit(solution)/shard_map/ppermute | solution.py:518
  16.9 0.0 collective-permute-done.2.refs_3_
  16.9 0.3 collective-permute-start.9
  17.2 0.0 collective-permute-done.3.refs_4_
  17.2 1.5 %collective-permute-start.10 = (f32[128,128]{1,0:T(8,128)S(1)}, f32[128,128]{1,0:T(8,128)S(1)}, u32[]{:S(2)}, u32[]{:S(2)}) collective-permute-start(f32[128,128]{1,0:T(8,128)S(1)} %get-tuple-element.51), channel_id=1, source_target_pairs={{0,4},{1,5},{2,6},{3,7},{4,0},{5,1},{6,2},{7,3},{8,12},{9,13},{10,... | collective-permute-start | bytes 196616 | tf_op jit(solution)/shard_map/ppermute | solution.py:518
  18.7 2.6 %collective-permute-done.4.refs_5_ = f32[208,128]{1,0:T(8,128)S(1)} collective-permute-done((f32[208,128]{1,0:T(8,128)S(1)}, f32[208,128]{1,0:T(8,128)S(1)}, u32[]{:S(2)}, u32[]{:S(2)}) %collective-permute-start.4) | collective-permute-done | bytes 106528 | tf_op jit(solution)/shard_map/ppermute | solution.py:518
  21.2 0.0 collective-permute-start.11
  21.2 0.0 collective-permute-done.5.refs_6_
  21.3 4.3 %collective-permute-start.12 = (f32[128,128]{1,0:T(8,128)S(1)}, f32[128,128]{1,0:T(8,128)S(1)}, u32[]{:S(2)}, u32[]{:S(2)}) collective-permute-start(f32[128,128]{1,0:T(8,128)S(1)} %get-tuple-element.53), channel_id=1, source_target_pairs={{0,6},{1,7},{2,4},{3,5},{4,2},{5,3},{6,0},{7,1},{8,14},{9,15},{10,... | collective-permute-start | bytes 196616 | tf_op jit(solution)/shard_map/ppermute | solution.py:518
  25.5 0.0 collective-permute-done.6.refs_7_
  25.5 0.0 collective-permute-start.13
  25.5 0.0 copy-done.3
  25.5 0.0 copy-done.4
  25.6 1.4 %planes.1 = (f32[2,4,208,128]{3,2,1,0:T(8,128)S(1)}, f32[2,4,12,128]{3,2,1,0:T(8,128)S(1)}, f32[2,4,12,128]{3,2,1,0:T(8,128)S(1)}) custom-call(s32[2]{0:T(128)S(1)} %pad_add_fusion.where_ref, f32[4,8,128]{2,1,0:T(8,128)S(1)} %get-tuple-element.37.facts_ref, bf16[256,256]{1,0:T(8,128)(2,1)S(1)} %copy-done.4, bf16[256,256]{1,0:T(8,128)(2,1)S(1)} %copy-done.3, ...), custom_call_target="tpu_custom_call" | custom-call | tf_op jit(solution)/shard_map/planes/pallas_call | solution.py:585
  26.9 0.0 collective-permute-done.9.refs_3_
  27.0 1.8 %collective-permute-start.14 = (f32[2,4,12,128]{3,2,1,0:T(8,128)S(1)}, f32[2,4,12,128]{3,2,1,0:T(8,128)S(1)}, u32[]{:S(2)}, u32[]{:S(2)}) collective-permute-start(f32[2,4,12,128]{3,2,1,0:T(8,128)S(1)} %get-tuple-element.57), channel_id=1, source_target_pairs={{0,8},{8,0},{16,24},{24,16},{1,9},{9,1},{17,25},{25,17},{2,10},{10... | collective-permute-start | bytes 147464 | tf_op jit(solution)/shard_map/ppermute | solution.py:586
  28.8 0.0 collective-permute-done.10.refs_4_
  28.8 2.5 %collective-permute-start.15 = (f32[2,4,12,128]{3,2,1,0:T(8,128)S(1)}, f32[2,4,12,128]{3,2,1,0:T(8,128)S(1)}, u32[]{:S(2)}, u32[]{:S(2)}) collective-permute-start(f32[2,4,12,128]{3,2,1,0:T(8,128)S(1)} %get-tuple-element.58), channel_id=1, source_target_pairs={{0,24},{8,16},{16,8},{24,0},{1,25},{9,17},{17,9},{25,1},{2,26},{10... | collective-permute-start | bytes 147464 | tf_op jit(solution)/shard_map/ppermute | solution.py:587
  31.3 0.0 collective-permute-done.11.refs_5_
  31.3 0.0 collective-permute-done.12.refs_6_
  31.3 0.0 collective-permute-done.13.refs_7_
  31.3 0.0 copy-done.1
  31.3 0.0 copy-done.2
  31.3 3.4 %rates.1 = (f32[8,192,128]{2,1,0:T(8,128)S(1)}, f32[4,96,512]{2,1,0:T(8,128)S(1)}) custom-call(s32[2]{0:T(128)S(1)} %pad_add_fusion.where_ref, f32[4,8,128]{2,1,0:T(8,128)S(1)} %get-tuple-element.37.facts_ref, bf16[256,256]{1,0:T(8,128)(2,1)S(1)} %copy-done.4, bf16[256,256]{1,0:T(8,128)(2,1)S(1)} %copy-done.3, bf16[256,512]{1,0:T(8,128)(2,1)S(1)} %copy-done.2, ...), custom_call_target="tpu_custom_call" | custom-call | tf_op jit(solution)/shard_map/rates/pallas_call | solution.py:607
  34.7 0.0 copy-start
  34.7 0.0 collective-permute-done.14.one_ref
  34.8 0.2 collective-permute-done.15.two_ref
  35.0 1.8 %edges.1 = (f32[288,128]{1,0:T(8,128)S(1)}, f32[288,128]{1,0:T(8,128)S(1)}, f32[288,128]{1,0:T(8,128)S(1)}, f32[288,128]{1,0:T(8,128)S(1)}, f32[288,128]{1,0:T(8...) custom-call(s32[2]{0:T(128)S(1)} %pad_add_fusion.where_ref, ...), custom_call_target="tpu_custom_call" | custom-call | tf_op jit(solution)/shard_map/edges/pallas_call | solution.py:608
  36.8 0.1 collective-permute-start.16
  36.9 1.7 %collective-permute-start.17 = (f32[288,128]{1,0:T(8,128)S(1)}, f32[288,128]{1,0:T(8,128)S(1)}, u32[]{:S(2)}, u32[]{:S(2)}) collective-permute-start(f32[288,128]{1,0:T(8,128)S(1)} %get-tuple-element.61), channel_id=1, source_target_pairs={{0,2},{1,3},{2,0},{3,1},{4,6},{5,7},{6,4},{7,5},{8,10},{9,11},{10,... | collective-permute-start | bytes 442376 | tf_op jit(solution)/shard_map/ppermute | solution.py:518
  38.6 0.2 collective-permute-start.18
  38.8 1.6 %collective-permute-start.19 = (f32[288,128]{1,0:T(8,128)S(1)}, f32[288,128]{1,0:T(8,128)S(1)}, u32[]{:S(2)}, u32[]{:S(2)}) collective-permute-start(f32[288,128]{1,0:T(8,128)S(1)} %get-tuple-element.63), channel_id=1, source_target_pairs={{0,4},{1,5},{2,6},{3,7},{4,0},{5,1},{6,2},{7,3},{8,12},{9,13},{10,... | collective-permute-start | bytes 442376 | tf_op jit(solution)/shard_map/ppermute | solution.py:518
  40.3 0.2 collective-permute-start.20
  40.5 0.0 collective-permute-done.16.refs_1_
  40.5 2.6 %collective-permute-start.21 = (f32[288,128]{1,0:T(8,128)S(1)}, f32[288,128]{1,0:T(8,128)S(1)}, u32[]{:S(2)}, u32[]{:S(2)}) collective-permute-start(f32[288,128]{1,0:T(8,128)S(1)} %get-tuple-element.65), channel_id=1, source_target_pairs={{0,6},{1,7},{2,4},{3,5},{4,2},{5,3},{6,0},{7,1},{8,14},{9,15},{10,... | collective-permute-start | bytes 442376 | tf_op jit(solution)/shard_map/ppermute | solution.py:518
  43.1 0.7 %collective-permute-done.17.refs_2_ = f32[288,128]{1,0:T(8,128)S(1)} collective-permute-done((f32[288,128]{1,0:T(8,128)S(1)}, f32[288,128]{1,0:T(8,128)S(1)}, u32[]{:S(2)}, u32[]{:S(2)}) %collective-permute-start.17) | collective-permute-done | bytes 147488 | tf_op jit(solution)/shard_map/ppermute | solution.py:518
  43.7 1.2 %collective-permute-start.22 = (f32[288,128]{1,0:T(8,128)S(1)}, f32[288,128]{1,0:T(8,128)S(1)}, u32[]{:S(2)}, u32[]{:S(2)}) collective-permute-start(f32[288,128]{1,0:T(8,128)S(1)} %get-tuple-element.66), channel_id=1, source_target_pairs={{0,7},{1,6},{2,5},{3,4},{4,3},{5,2},{6,1},{7,0},{8,15},{9,14},{10,... | collective-permute-start | bytes 442376 | tf_op jit(solution)/shard_map/ppermute | solution.py:518
  44.9 1.1 %collective-permute-done.18.refs_3_ = f32[288,128]{1,0:T(8,128)S(1)} collective-permute-done((f32[288,128]{1,0:T(8,128)S(1)}, f32[288,128]{1,0:T(8,128)S(1)}, u32[]{:S(2)}, u32[]{:S(2)}) %collective-permute-start.18) | collective-permute-done | bytes 147488 | tf_op jit(solution)/shard_map/ppermute | solution.py:518
  46.0 0.0 collective-permute-done.19.refs_4_
  46.0 7.8 %collective-permute-done.20.refs_5_ = f32[288,128]{1,0:T(8,128)S(1)} collective-permute-done((f32[288,128]{1,0:T(8,128)S(1)}, f32[288,128]{1,0:T(8,128)S(1)}, u32[]{:S(2)}, u32[]{:S(2)}) %collective-permute-start.20) | collective-permute-done | bytes 147488 | tf_op jit(solution)/shard_map/ppermute | solution.py:518
  53.8 0.0 collective-permute-done.21.refs_6_
  53.8 0.0 collective-permute-done.22.refs_7_
  53.8 0.0 copy-done
  53.8 2.4 %collect.1 = f32[128,2304]{1,0:T(8,128)} custom-call(s32[2]{0:T(128)S(1)} %pad_add_fusion.where_ref, f32[64,128]{1,0:T(8,128)S(1)} %get-tuple-element.36.pick_ref, f32[128,2304]{1,0:T(8,128)S(1)} %bitcast.7, f32[288,128]{1,0:T(8,128)S(1)} %get-tuple-element.59.refs_0_, f32[288,128]{1,0:T(8,128)S(1)} %collective-permute-done.16.refs_1_, ...), custom_call_target="tpu_custom_call" | custom-call | tf_op jit(solution)/shard_map/collect/pallas_call | solution.py:619
Async XLA Ops:
  0.0 25.5 %copy-start.3 = (bf16[256,256]{1,0:T(8,128)(2,1)S(1)}, bf16[256,256]{1,0:T(8,128)(2,1)}, u32[]{:S(2)}) copy-start(bf16[256,256]{1,0:T(8,128)(2,1)} %constant.30.clone.low_ref.there_low) | copy-start | bytes 393220
  0.0 25.5 %copy-start.4 = (bf16[256,256]{1,0:T(8,128)(2,1)S(1)}, bf16[256,256]{1,0:T(8,128)(2,1)}, u32[]{:S(2)}) copy-start(bf16[256,256]{1,0:T(8,128)(2,1)} %constant.29.clone.high_ref.there_high) | copy-start | bytes 393220
  0.1 31.2 %copy-start.1 = (bf16[256,512]{1,0:T(8,128)(2,1)S(1)}, bf16[256,512]{1,0:T(8,128)(2,1)}, u32[]{:S(2)}) copy-start(bf16[256,512]{1,0:T(8,128)(2,1)} %constant.32.clone.low_ref) | copy-start | bytes 786436
  0.1 31.2 %copy-start.2 = (bf16[256,512]{1,0:T(8,128)(2,1)S(1)}, bf16[256,512]{1,0:T(8,128)(2,1)}, u32[]{:S(2)}) copy-start(bf16[256,512]{1,0:T(8,128)(2,1)} %constant.31.clone.high_ref) | copy-start | bytes 786436
  3.7 4.7 %collective-permute-start.7 = (f32[128,128]{1,0:T(8,128)S(1)}, f32[128,128]{1,0:T(8,128)S(1)}, u32[]{:S(2)}, u32[]{:S(2)}) collective-permute-start(f32[128,128]{1,0:T(8,128)S(1)} %get-tuple-element.48), channel_id=1, source_target_pairs={{0,1},{1,0},{2,3},{3,2},{4,5},{5,4},{6,7},{7,6},{8,9},{9,8},{10,11... | collective-permute-start | bytes 196616 | tf_op jit(solution)/shard_map/ppermute | solution.py:518
  4.3 8.2 %collective-permute-start = (f32[208,128]{1,0:T(8,128)S(1)}, f32[208,128]{1,0:T(8,128)S(1)}, u32[]{:S(2)}, u32[]{:S(2)}) collective-permute-start(f32[208,128]{1,0:T(8,128)S(1)} %get-tuple-element.39), channel_id=1, source_target_pairs={{0,1},{1,0},{2,3},{3,2},{4,5},{5,4},{6,7},{7,6},{8,9},{9,8},{10,11... | collective-permute-start | bytes 319496 | tf_op jit(solution)/shard_map/ppermute | solution.py:518
  4.3 11.1 %collective-permute-start.1 = (f32[208,128]{1,0:T(8,128)S(1)}, f32[208,128]{1,0:T(8,128)S(1)}, u32[]{:S(2)}, u32[]{:S(2)}) collective-permute-start(f32[208,128]{1,0:T(8,128)S(1)} %get-tuple-element.40), channel_id=1, source_target_pairs={{0,2},{1,3},{2,0},{3,1},{4,6},{5,7},{6,4},{7,5},{8,10},{9,11},{10,... | collective-permute-start | bytes 319496 | tf_op jit(solution)/shard_map/ppermute | solution.py:518
  7.3 5.2 %collective-permute-start.8 = (f32[128,128]{1,0:T(8,128)S(1)}, f32[128,128]{1,0:T(8,128)S(1)}, u32[]{:S(2)}, u32[]{:S(2)}) collective-permute-start(f32[128,128]{1,0:T(8,128)S(1)} %get-tuple-element.49), channel_id=1, source_target_pairs={{0,2},{1,3},{2,0},{3,1},{4,6},{5,7},{6,4},{7,5},{8,10},{9,11},{10,... | collective-permute-start | bytes 196616 | tf_op jit(solution)/shard_map/ppermute | solution.py:518
  7.3 9.6 %collective-permute-start.2 = (f32[208,128]{1,0:T(8,128)S(1)}, f32[208,128]{1,0:T(8,128)S(1)}, u32[]{:S(2)}, u32[]{:S(2)}) collective-permute-start(f32[208,128]{1,0:T(8,128)S(1)} %get-tuple-element.41), channel_id=1, source_target_pairs={{0,3},{1,2},{2,1},{3,0},{4,7},{5,6},{6,5},{7,4},{8,11},{9,10},{10,... | collective-permute-start | bytes 319496 | tf_op jit(solution)/shard_map/ppermute | solution.py:518
  8.4 8.8 %collective-permute-start.3 = (f32[208,128]{1,0:T(8,128)S(1)}, f32[208,128]{1,0:T(8,128)S(1)}, u32[]{:S(2)}, u32[]{:S(2)}) collective-permute-start(f32[208,128]{1,0:T(8,128)S(1)} %get-tuple-element.42), channel_id=1, source_target_pairs={{0,4},{1,5},{2,6},{3,7},{4,0},{5,1},{6,2},{7,3},{8,12},{9,13},{10,... | collective-permute-start | bytes 319496 | tf_op jit(solution)/shard_map/ppermute | solution.py:518
  12.5 8.8 %collective-permute-start.4 = (f32[208,128]{1,0:T(8,128)S(1)}, f32[208,128]{1,0:T(8,128)S(1)}, u32[]{:S(2)}, u32[]{:S(2)}) collective-permute-start(f32[208,128]{1,0:T(8,128)S(1)} %get-tuple-element.43), channel_id=1, source_target_pairs={{0,5},{1,4},{2,7},{3,6},{4,1},{5,0},{6,3},{7,2},{8,13},{9,12},{10,... | collective-permute-start | bytes 319496 | tf_op jit(solution)/shard_map/ppermute | solution.py:518
  12.5 8.8 %collective-permute-start.5 = (f32[208,128]{1,0:T(8,128)S(1)}, f32[208,128]{1,0:T(8,128)S(1)}, u32[]{:S(2)}, u32[]{:S(2)}) collective-permute-start(f32[208,128]{1,0:T(8,128)S(1)} %get-tuple-element.44), channel_id=1, source_target_pairs={{0,6},{1,7},{2,4},{3,5},{4,2},{5,3},{6,0},{7,1},{8,14},{9,15},{10,... | collective-permute-start | bytes 319496 | tf_op jit(solution)/shard_map/ppermute | solution.py:518
  15.5 10.1 %collective-permute-start.6 = (f32[208,128]{1,0:T(8,128)S(1)}, f32[208,128]{1,0:T(8,128)S(1)}, u32[]{:S(2)}, u32[]{:S(2)}) collective-permute-start(f32[208,128]{1,0:T(8,128)S(1)} %get-tuple-element.45), channel_id=1, source_target_pairs={{0,7},{1,6},{2,5},{3,4},{4,3},{5,2},{6,1},{7,0},{8,15},{9,14},{10,... | collective-permute-start | bytes 319496 | tf_op jit(solution)/shard_map/ppermute | solution.py:518
  16.9 10.0 %collective-permute-start.9 = (f32[128,128]{1,0:T(8,128)S(1)}, f32[128,128]{1,0:T(8,128)S(1)}, u32[]{:S(2)}, u32[]{:S(2)}) collective-permute-start(f32[128,128]{1,0:T(8,128)S(1)} %get-tuple-element.50), channel_id=1, source_target_pairs={{0,3},{1,2},{2,1},{3,0},{4,7},{5,6},{6,5},{7,4},{8,11},{9,10},{10,... | collective-permute-start | bytes 196616 | tf_op jit(solution)/shard_map/ppermute | solution.py:518
  17.2 11.6 %collective-permute-start.10 = (f32[128,128]{1,0:T(8,128)S(1)}, f32[128,128]{1,0:T(8,128)S(1)}, u32[]{:S(2)}, u32[]{:S(2)}) collective-permute-start(f32[128,128]{1,0:T(8,128)S(1)} %get-tuple-element.51), channel_id=1, source_target_pairs={{0,4},{1,5},{2,6},{3,7},{4,0},{5,1},{6,2},{7,3},{8,12},{9,13},{10,... | collective-permute-start | bytes 196616 | tf_op jit(solution)/shard_map/ppermute | solution.py:518
  21.2 10.0 %collective-permute-start.11 = (f32[128,128]{1,0:T(8,128)S(1)}, f32[128,128]{1,0:T(8,128)S(1)}, u32[]{:S(2)}, u32[]{:S(2)}) collective-permute-start(f32[128,128]{1,0:T(8,128)S(1)} %get-tuple-element.52), channel_id=1, source_target_pairs={{0,5},{1,4},{2,7},{3,6},{4,1},{5,0},{6,3},{7,2},{8,13},{9,12},{10,... | collective-permute-start | bytes 196616 | tf_op jit(solution)/shard_map/ppermute | solution.py:518
  21.3 10.0 %collective-permute-start.12 = (f32[128,128]{1,0:T(8,128)S(1)}, f32[128,128]{1,0:T(8,128)S(1)}, u32[]{:S(2)}, u32[]{:S(2)}) collective-permute-start(f32[128,128]{1,0:T(8,128)S(1)} %get-tuple-element.53), channel_id=1, source_target_pairs={{0,6},{1,7},{2,4},{3,5},{4,2},{5,3},{6,0},{7,1},{8,14},{9,15},{10,... | collective-permute-start | bytes 196616 | tf_op jit(solution)/shard_map/ppermute | solution.py:518
  25.5 5.7 %collective-permute-start.13 = (f32[128,128]{1,0:T(8,128)S(1)}, f32[128,128]{1,0:T(8,128)S(1)}, u32[]{:S(2)}, u32[]{:S(2)}) collective-permute-start(f32[128,128]{1,0:T(8,128)S(1)} %get-tuple-element.54), channel_id=1, source_target_pairs={{0,7},{1,6},{2,5},{3,4},{4,3},{5,2},{6,1},{7,0},{8,15},{9,14},{10,... | collective-permute-start | bytes 196616 | tf_op jit(solution)/shard_map/ppermute | solution.py:518
  27.0 7.8 %collective-permute-start.14 = (f32[2,4,12,128]{3,2,1,0:T(8,128)S(1)}, f32[2,4,12,128]{3,2,1,0:T(8,128)S(1)}, u32[]{:S(2)}, u32[]{:S(2)}) collective-permute-start(f32[2,4,12,128]{3,2,1,0:T(8,128)S(1)} %get-tuple-element.57), channel_id=1, source_target_pairs={{0,8},{8,0},{16,24},{24,16},{1,9},{9,1},{17,25},{25,17},{2,10},{10... | collective-permute-start | bytes 147464 | tf_op jit(solution)/shard_map/ppermute | solution.py:586
  28.8 6.2 %collective-permute-start.15 = (f32[2,4,12,128]{3,2,1,0:T(8,128)S(1)}, f32[2,4,12,128]{3,2,1,0:T(8,128)S(1)}, u32[]{:S(2)}, u32[]{:S(2)}) collective-permute-start(f32[2,4,12,128]{3,2,1,0:T(8,128)S(1)} %get-tuple-element.58), channel_id=1, source_target_pairs={{0,24},{8,16},{16,8},{24,0},{1,25},{9,17},{17,9},{25,1},{2,26},{10... | collective-permute-start | bytes 147464 | tf_op jit(solution)/shard_map/ppermute | solution.py:587
  34.7 19.0 %copy-start = (f32[4,32,2304]{2,1,0:T(8,128)S(1)}, f32[4,32,2304]{2,1,0:T(8,128)}, u32[]{:S(2)}) copy-start(f32[4,32,2304]{2,1,0:T(8,128)} %param.10) | copy-start | bytes 3538948
  36.8 3.6 %collective-permute-start.16 = (f32[288,128]{1,0:T(8,128)S(1)}, f32[288,128]{1,0:T(8,128)S(1)}, u32[]{:S(2)}, u32[]{:S(2)}) collective-permute-start(f32[288,128]{1,0:T(8,128)S(1)} %get-tuple-element.60), channel_id=1, source_target_pairs={{0,1},{1,0},{2,3},{3,2},{4,5},{5,4},{6,7},{7,6},{8,9},{9,8},{10,11... | collective-permute-start | bytes 442376 | tf_op jit(solution)/shard_map/ppermute | solution.py:518
  36.9 6.8 %collective-permute-start.17 = (f32[288,128]{1,0:T(8,128)S(1)}, f32[288,128]{1,0:T(8,128)S(1)}, u32[]{:S(2)}, u32[]{:S(2)}) collective-permute-start(f32[288,128]{1,0:T(8,128)S(1)} %get-tuple-element.61), channel_id=1, source_target_pairs={{0,2},{1,3},{2,0},{3,1},{4,6},{5,7},{6,4},{7,5},{8,10},{9,11},{10,... | collective-permute-start | bytes 442376 | tf_op jit(solution)/shard_map/ppermute | solution.py:518
  38.6 7.4 %collective-permute-start.18 = (f32[288,128]{1,0:T(8,128)S(1)}, f32[288,128]{1,0:T(8,128)S(1)}, u32[]{:S(2)}, u32[]{:S(2)}) collective-permute-start(f32[288,128]{1,0:T(8,128)S(1)} %get-tuple-element.62), channel_id=1, source_target_pairs={{0,3},{1,2},{2,1},{3,0},{4,7},{5,6},{6,5},{7,4},{8,11},{9,10},{10,... | collective-permute-start | bytes 442376 | tf_op jit(solution)/shard_map/ppermute | solution.py:518
  38.8 7.2 %collective-permute-start.19 = (f32[288,128]{1,0:T(8,128)S(1)}, f32[288,128]{1,0:T(8,128)S(1)}, u32[]{:S(2)}, u32[]{:S(2)}) collective-permute-start(f32[288,128]{1,0:T(8,128)S(1)} %get-tuple-element.63), channel_id=1, source_target_pairs={{0,4},{1,5},{2,6},{3,7},{4,0},{5,1},{6,2},{7,3},{8,12},{9,13},{10,... | collective-permute-start | bytes 442376 | tf_op jit(solution)/shard_map/ppermute | solution.py:518
  40.3 13.4 %collective-permute-start.20 = (f32[288,128]{1,0:T(8,128)S(1)}, f32[288,128]{1,0:T(8,128)S(1)}, u32[]{:S(2)}, u32[]{:S(2)}) collective-permute-start(f32[288,128]{1,0:T(8,128)S(1)} %get-tuple-element.64), channel_id=1, source_target_pairs={{0,5},{1,4},{2,7},{3,6},{4,1},{5,0},{6,3},{7,2},{8,13},{9,12},{10,... | collective-permute-start | bytes 442376 | tf_op jit(solution)/shard_map/ppermute | solution.py:518
  40.5 13.3 %collective-permute-start.21 = (f32[288,128]{1,0:T(8,128)S(1)}, f32[288,128]{1,0:T(8,128)S(1)}, u32[]{:S(2)}, u32[]{:S(2)}) collective-permute-start(f32[288,128]{1,0:T(8,128)S(1)} %get-tuple-element.65), channel_id=1, source_target_pairs={{0,6},{1,7},{2,4},{3,5},{4,2},{5,3},{6,0},{7,1},{8,14},{9,15},{10,... | collective-permute-start | bytes 442376 | tf_op jit(solution)/shard_map/ppermute | solution.py:518
  43.7 10.0 %collective-permute-start.22 = (f32[288,128]{1,0:T(8,128)S(1)}, f32[288,128]{1,0:T(8,128)S(1)}, u32[]{:S(2)}, u32[]{:S(2)}) collective-permute-start(f32[288,128]{1,0:T(8,128)S(1)} %get-tuple-element.66), channel_id=1, source_target_pairs={{0,7},{1,6},{2,5},{3,4},{4,3},{5,2},{6,1},{7,0},{8,15},{9,14},{10,... | collective-permute-start | bytes 442376 | tf_op jit(solution)/shard_map/ppermute | solution.py:518
where the time goes:
time: 56.3 us; the launch traced here: 56.2 us
  starting transfers between devices  28.4 us (50%)
  waiting for transfers between devices  14.9 us (26%)
  Pallas kernels  12.7 us (23%)
    ppermute x21, starting transfers between devices, exchange(): lax.ppermute(blocks[k], 'span', [(s, s ^ k) for s in range(span)])  24.1 us
    ppermute x21, waiting for transfers between devices, exchange(): lax.ppermute(blocks[k], 'span', [(s, s ^ k) for s in range(span)])  14.6 us
    pallas_call x1, Pallas kernels, ordered_body(): pl.pallas_call(functools.partial(spread_kernel, (rows, cols, share, span)...  3.61 us
    pallas_call x1, Pallas kernels, ordered_body(): mid, edge = rates(me, facts, *forward, *backward, phys, *core_takes)  3.44 us
    ppermute x1, starting transfers between devices, ordered_body(): lax.ppermute(two, 'elem', [(g, (g - 1 if g % 2 == 0 else g + 1) % groups)...  2.45 us
    pallas_call x1, Pallas kernels, ordered_body(): pl.pallas_call(functools.partial(gather_kernel, (rows, cols, share, span,...  2.41 us
    ppermute x1, starting transfers between devices, ordered_body(): one = lax.ppermute(one, 'elem', [(g, g ^ 1) for g in range(groups)])  1.85 us
    pallas_call x1, Pallas kernels, ordered_body(): pl.pallas_call(functools.partial(edges_kernel, dims), out_shape=[whole] *...  1.84 us
  transfers between devices with their start and end apart: 23, of which 6 were waited for; matrix products, arithmetic and copies ran while one was open for 0% of the time, Pallas kernels for 9%

commit v1 on v0

--- a/solution.py
+++ b/solution.py
@@ -21,7 +21,8 @@
 CHUNK = 3 * LANES
 RIM_NODES = [p for p in range(NODES) if p // SIDE in (0, 5) or p % SIDE in (0, 5)]
 CORE_NODES = [p for p in range(NODES) if p not in RIM_NODES]
-PARTS = (RIM_NODES, CORE_NODES)
+MID_NODES = [p for p in range(NODES) if p // SIDE not in (0, 5)]
+END_NODES = [p for p in range(NODES) if p // SIDE in (0, 5)]
 
 
 def gll_matrix():
@@ -110,12 +111,25 @@
     return out
 
 
-def spread_kernel(dims, where_ref, near_any, wall_any, rim_any, metric_any, state_any, *refs):
+def move_nodes(nodes, elems, flat, pick, pick_sides, put):
+    for at in range(0, len(nodes), 2):
+        pair = nodes[at : at + 2]
+        columns = [
+            jnp.concatenate(split(flat[pl.ds(node, elems, stride=NODES), :]), axis=0)
+            for node in pair
+        ]
+        chosen = pick_sides if any(node % SIDE in (0, 5) for node in pair) else pick
+        moved = mm(chosen, jnp.concatenate(columns, axis=1))
+        for half, node in enumerate(pair):
+            put(at + half, node, moved[:, half * LANES : (half + 1) * LANES])
+
+
+def spread_kernel(dims, near_any, wall_any, rim_any, metric_any, state_any, *refs):
     rows, cols, share, span = dims
-    sends = [refs[:span], refs[span : 2 * span]]
-    pick_ref, facts_ref = refs[2 * span : 2 * span + 2]
-    halo_ref, bends_ref, near_ref, wall_ref, rim_ref, metric_ref, state_ref, flat, sems = refs[2 * span + 2 :]
-    me = where_ref[0]
+    sends = refs[:span]
+    pick_ref, facts_ref, flat, all_ref = refs[span : span + 4]
+    halo_ref, bends_ref, near_ref, wall_ref, rim_ref, metric_ref, state_ref, sems = refs[span + 4 :]
+    me = lax.axis_index("span")
     elems = rows * cols
     width = elems * NODES
     small = [
@@ -176,12 +190,8 @@
                 face.astype(jnp.float32),
                 flip_y.astype(jnp.float32),
             )
-
-            @pl.when(at < share)
-            def _(at=at, facts=facts):
-                for kind, fact in enumerate(facts):
-                    facts_ref[kind, pl.ds(at, 1), :] = jnp.full((1, LANES), fact, jnp.float32)
-
+            for kind, fact in enumerate(facts):
+                all_ref[kind, pl.ds(at, 1), :] = jnp.full((1, LANES), fact, jnp.float32)
             if col + 1 < cols:
                 step = near_ref[face ^ 1, cell]
                 cell = step >> 2
@@ -191,18 +201,18 @@
         if at % CHUNK == 0:
             large[at // CHUNK].wait()
         flat[pl.ds(at, LANES), :] = state_ref[:, pl.ds(at, LANES)].T
+    facts_ref[...] = all_ref[:, :share]
     pick = pick_ref[...].astype(jnp.bfloat16)
     both = jnp.concatenate([pick, halo_ref[...].astype(jnp.bfloat16)], axis=0)
     edge = {}
-    for nodes, outs in zip(PARTS, sends):
-        for at, node in enumerate(nodes):
-            high, low = split(flat[pl.ds(node, elems, stride=NODES), :])
-            wanted = node % SIDE in (0, 5)
-            moved = mm(both if wanted else pick, jnp.concatenate([high, low], axis=0))
-            if wanted:
-                edge[divmod(node, SIDE)] = moved[elems:]
-            for step in range(span):
-                outs[step][pl.ds(at * share, share), :] = moved[step * share : (step + 1) * share]
+
+    def put(at, node, mine):
+        if node % SIDE in (0, 5):
+            edge[divmod(node, SIDE)] = mine[elems:]
+        for step in range(span):
+            sends[step][pl.ds(at * share, share), :] = mine[step * share : (step + 1) * share]
+
+    move_nodes(RIM_NODES, elems, flat, pick, both, put)
     bend_x = bends_ref[0] == 1
     bend_y = bends_ref[1] == 1
     trace = [jnp.where(bend_y, edge[t, 5], edge[t, 0]) for t in range(SIDE)]
@@ -210,22 +220,37 @@
         moved = jnp.where(bend_x, trace[SIDE - 1 - t], trace[t])
         at = pl.ds((len(RIM_NODES) + t) * share, share)
         for step in range(span):
-            sends[0][step][at, :] = moved[step * share : (step + 1) * share]
+            sends[step][at, :] = moved[step * share : (step + 1) * share]
+
+
+def spread_core_kernel(share, span, pick_ref, flat, odd_ref, *evens):
+    pick = pick_ref[...].astype(jnp.bfloat16)
+    size = len(CORE_NODES) * share
+
+    def put(at, node, mine):
+        for step in range(span):
+            value = mine[step * share : (step + 1) * share]
+            if step % 2:
+                odd_ref[pl.ds(step // 2 * size + at * share, share), :] = value
+            else:
+                evens[step // 2][pl.ds(at * share, share), :] = value
+
+    move_nodes(CORE_NODES, pick.shape[0], flat, pick, pick, put)
 
 
 def along(trace, flip):
-    return [jnp.where(flip, trace[SIDE - 1 - t], trace[t]) for t in range(SIDE)]
+    return {t: jnp.where(flip, trace[SIDE - 1 - t], trace[t]) for t in trace}
 
 
 def sides_x(value, flip_x, flip_y):
-    low = [jnp.where(flip_x, value(5, t), value(0, t)) for t in range(SIDE)]
-    high = [jnp.where(flip_x, value(0, t), value(5, t)) for t in range(SIDE)]
+    low = {t: jnp.where(flip_x, value(5, t), value(0, t)) for t in range(SIDE)}
+    high = {t: jnp.where(flip_x, value(0, t), value(5, t)) for t in range(SIDE)}
     return along(low, flip_y), along(high, flip_y)
 
 
-def sides_y(value, flip_x, flip_y):
-    low = [jnp.where(flip_y, value(t, 5), value(t, 0)) for t in range(SIDE)]
-    high = [jnp.where(flip_y, value(t, 0), value(t, 5)) for t in range(SIDE)]
+def sides_y(value, flip_x, flip_y, wanted):
+    low = {t: jnp.where(flip_y, value(t, 5), value(t, 0)) for t in wanted}
+    high = {t: jnp.where(flip_y, value(t, 0), value(t, 5)) for t in wanted}
     return along(low, flip_x), along(high, flip_x)
 
 
@@ -234,7 +259,7 @@
 
 
 def back(one, two, flip, flip_along):
-    return along([jnp.where(flip, two[t], one[t]) for t in range(SIDE)], flip_along)
+    return along({t: jnp.where(flip, two[t], one[t]) for t in one}, flip_along)
 
 
 def sign(value):
@@ -252,19 +277,23 @@
     pieces = []
     for group in range(span // 4):
         pieces.append(regroup([takes[4 * group + q][...] for q in range(4)], lane))
+    stack = [jnp.concatenate([piece[var] for piece in pieces], axis=1) for var in range(num_vars)]
+    high, low = split(jnp.concatenate(stack, axis=0))
+    planes = mm(high, tables[0]) + mm(low, tables[0]) + mm(high, tables[1])
+    size = takes[0].shape[0]
     for var in range(num_vars):
-        high, low = split(jnp.concatenate([piece[var] for piece in pieces], axis=1))
-        planes = mm(high, tables[0]) + mm(low, tables[0]) + mm(high, tables[1])
         for tile in range(span * modes // LANES):
-            phys_ref[tile, var] = planes[:, tile * LANES : (tile + 1) * LANES]
-
-
-def planes_kernel(dims, where_ref, facts_ref, high_ref, low_ref, *refs):
+            phys_ref[tile, var] = planes[
+                var * size : (var + 1) * size, tile * LANES : (tile + 1) * LANES
+            ]
+
+
+def planes_kernel(dims, facts_ref, high_ref, low_ref, *refs):
     cols, share, span, num_vars, modes = dims
     takes = refs[:span]
     phys_ref, one_ref, two_ref = refs[span:]
-    to_planes(dims, where_ref[0], high_ref, low_ref, takes, phys_ref)
-    odd = where_ref[1] == 1
+    to_planes(dims, lax.axis_index("span"), high_ref, low_ref, takes, phys_ref)
+    odd = lax.axis_index("elem") % 2 == 1
     lines = share // cols
     flip_x = facts_ref[2] > 0.5
     flip_y = facts_ref[3] > 0.5
@@ -285,17 +314,17 @@
 
 
 def to_modes(dims, me, high_ref, low_ref, rates):
-    _, _, span, _, modes = dims
+    _, _, span, num_vars, modes = dims
     lane = lax.broadcasted_iota(jnp.int32, (1, LANES), 1)
     tables = []
     for ref in (high_ref, low_ref):
         tables.append(
             jnp.concatenate([ref[pl.ds((me ^ k) * modes, modes), :] for k in range(span)], axis=0)
         )
-    gains = []
-    for rate in rates:
-        high, low = split(rate)
-        gains.append(mm_nt(high, tables[0]) + mm_nt(low, tables[0]) + mm_nt(high, tables[1]))
+    size = rates[0].shape[0]
+    high, low = split(jnp.concatenate(rates, axis=0))
+    gain = mm_nt(high, tables[0]) + mm_nt(low, tables[0]) + mm_nt(high, tables[1])
+    gains = [gain[var * size : (var + 1) * size] for var in range(num_vars)]
     out = []
     for group in range(span // 4):
         at = slice(group * LANES, (group + 1) * LANES)
@@ -303,180 +332,227 @@
     return out
 
 
+def derivative(values, wanted=tuple(range(SIDE))):
+    deriv = gll_matrix()
+    last = SIDE - 1
+    plus = [values[j] + values[last - j] for j in range(SIDE // 2)]
+    minus = [values[j] - values[last - j] for j in range(SIDE // 2)]
+    out = [None] * SIDE
+    for i in range(SIDE // 2):
+        if i not in wanted:
+            continue
+        even, odd = None, None
+        for j in range(SIDE // 2):
+            a = minus[j] * float(0.5 * (deriv[i, j] - deriv[i, last - j]))
+            b = plus[j] * float(0.5 * (deriv[i, j] + deriv[i, last - j]))
+            even = a if even is None else even + a
+            odd = b if odd is None else odd + b
+        out[i] = even + odd
+        out[last - i] = even - odd
+    return out
+
+
+class Faces:
+    def __init__(self, dims, facts_ref, phys_ref, core_ref):
+        cols, share, span, self.num_vars, modes = dims
+        self.cols = cols
+        self.phys_ref, self.core_ref = phys_ref, core_ref
+        me = lax.axis_index("span")
+        slot = lax.broadcasted_iota(jnp.int32, (SUB, LANES), 0)
+        self.slot = slot
+        self.flip_x = facts_ref[2] > 0.5
+        self.flip_y = facts_ref[3] > 0.5
+        self.scale_x = -facts_ref[0]
+        self.scale_y = facts_ref[1]
+        self.turn_x = sign(facts_ref[0]) * (1.0 - 2.0 * facts_ref[2])
+        self.turn_y = sign(facts_ref[1]) * (1.0 - 2.0 * facts_ref[3])
+        self.weight_x = 7.5 * jnp.abs(facts_ref[0])
+        self.weight_y = 7.5 * jnp.abs(facts_ref[1])
+        self.first_line = slot < cols
+        self.turn_halo = jnp.where(self.first_line, self.turn_y, -self.turn_y)
+        self.floor = jnp.logical_and(self.first_line, me == 0)
+        self.roof = jnp.logical_and(jnp.logical_not(self.first_line), me == span - 1)
+
+    def reader(self, tile, var):
+        def read(i, j):
+            node = SIDE * i + j
+            ref = self.phys_ref if node in RIM_NODES else self.core_ref
+            nodes = RIM_NODES if node in RIM_NODES else CORE_NODES
+            return ref[tile, var, pl.ds(nodes.index(node) * SUB, SUB), :]
+
+        return read
+
+    def volume(self, tile, var, wanted):
+        q, u, v = (self.reader(tile, at) for at in (var, 0, 1))
+        total = {}
+        for j in range(SIDE):
+            slope = derivative([q(i, j) * u(i, j) for i in range(SIDE)], wanted)
+            for i in wanted:
+                total[i, j] = self.scale_x * slope[i]
+        for i in wanted:
+            slope = derivative([q(i, j) * v(i, j) for j in range(SIDE)])
+            for j in range(SIDE):
+                total[i, j] = total[i, j] - self.scale_y * slope[j]
+        return total
+
+    def pace_y(self, tile, wanted):
+        speed = sides_y(self.reader(tile, 1), self.flip_x, self.flip_y, wanted)
+        return [{t: self.turn_y * side[t] for t in wanted} for side in speed]
+
+    def faces_y(self, tile, var, pace, wanted, total):
+        mirror = 1.0 if var == self.num_vars - 1 else -1.0
+        trace = sides_y(self.reader(tile, var), self.flip_x, self.flip_y, wanted)
+        low, high = {}, {}
+        for t in wanted:
+            at = pl.ds((len(RIM_NODES) + t) * SUB, SUB)
+            speed, value = pace[0][t], trace[0][t]
+            own_low, give_low = -(speed + 1.0) * value, (1.0 - speed) * value
+            speed, value = pace[1][t], trace[1][t]
+            own_high, give_high = (speed - 1.0) * value, (1.0 + speed) * value
+            outside = (1.0 + self.turn_halo * self.phys_ref[tile, 1, at, :]) * self.phys_ref[
+                tile, var, at, :
+            ]
+            outside = jnp.where(self.floor, mirror * give_low, outside)
+            outside = jnp.where(self.roof, mirror * give_high, outside)
+            from_low = jnp.where(self.first_line, outside, pltpu.roll(give_high, self.cols, 0))
+            from_high = jnp.where(
+                self.first_line, pltpu.roll(give_low, SUB - self.cols, 0), outside
+            )
+            low[t] = self.weight_y * (own_low + from_low)
+            high[t] = self.weight_y * (own_high + from_high)
+        for j, one, two in ((0, low, high), (5, high, low)):
+            side = back(one, two, self.flip_y, self.flip_x)
+            for t in wanted:
+                total[t, j] = total[t, j] + side[t]
+
+    def pace_x(self, tile):
+        speed = sides_x(self.reader(tile, 0), self.flip_x, self.flip_y)
+        return [{t: self.turn_x * side[t] for t in side} for side in speed]
+
+    def faces_x(self, tile, var, pace, total, rim):
+        trace = sides_x(self.reader(tile, var), self.flip_x, self.flip_y)
+        low, high = {}, {}
+        for t in range(SIDE):
+            speed, value = pace[0][t], trace[0][t]
+            own_low, give_low = -(speed + 1.0) * value, (1.0 - speed) * value
+            speed, value = pace[1][t], trace[1][t]
+            own_high, give_high = (speed - 1.0) * value, (1.0 + speed) * value
+            from_low, from_high = pltpu.roll(give_high, 1, 0), pltpu.roll(give_low, SUB - 1, 0)
+            for line, (below, above) in enumerate(rim(t)):
+                from_low = jnp.where(self.slot == line * self.cols, below, from_low)
+                from_high = jnp.where(self.slot == (line + 1) * self.cols - 1, above, from_high)
+            low[t] = self.weight_x * (own_low + from_low)
+            high[t] = self.weight_x * (own_high + from_high)
+        for i, one, two in ((0, low, high), (5, high, low)):
+            side = back(one, two, self.flip_x, self.flip_y)
+            for t in range(SIDE):
+                total[i, t] = total[i, t] + side[t]
+
+
+def unpaired(refs, size):
+    takes = list(refs[:2])
+    for ref in refs[2:]:
+        takes += [ref.at[:size], ref.at[size:]]
+    return takes
+
+
+def store_rates(rate_ref, nodes, tile, var, count, total, q, w):
+    for place, node in enumerate(nodes):
+        i, j = divmod(node, SIDE)
+        at = pl.ds(place * SUB, SUB)
+        rate_ref[var, at, pl.ds(tile * LANES, LANES)] = total[i, j]
+        rate_ref[var, at, pl.ds(count + tile * LANES, LANES)] = q(i, j) * w(i, j)
+
+
 def rates_kernel(
-    dims, where_ref, facts_ref, there_high, there_low, high_ref, low_ref, phys_ref, *refs
+    dims, facts_ref, there_high, there_low, high_ref, low_ref, phys_ref, *refs
 ):
-    cols, _, span, num_vars, modes = dims
-    mid_ref, edge_ref, core_ref, rate_ref = refs[span:]
-    me = where_ref[0]
-    to_planes(dims, me, there_high, there_low, refs[:span], core_ref)
+    _, share, span, num_vars, modes = dims
+    half = span // 2
+    outs = refs[half + 1 : half + 1 + span]
+    core_ref, rate_ref = refs[half + 1 + span :]
+    takes = unpaired(refs[: half + 1], len(CORE_NODES) * share)
+    me = lax.axis_index("span")
+    to_planes(dims, me, there_high, there_low, takes, core_ref)
     count = span * modes
-    deriv = np.asarray(gll_matrix(), np.float32)
-    slot = lax.broadcasted_iota(jnp.int32, (SUB, LANES), 0)
-    flip_x = facts_ref[2] > 0.5
-    flip_y = facts_ref[3] > 0.5
-    scale_x = facts_ref[0]
-    scale_y = facts_ref[1]
-    turn_x = sign(scale_x) * (1.0 - 2.0 * facts_ref[2])
-    turn_y = sign(scale_y) * (1.0 - 2.0 * facts_ref[3])
-    weight_x = 7.5 * jnp.abs(scale_x)
-    weight_y = 7.5 * jnp.abs(scale_y)
-    first_col = slot % cols == 0
-    last_col = slot % cols == cols - 1
-    first_line = slot < cols
-    turn_halo = jnp.where(first_line, turn_y, -turn_y)
-    floor = jnp.logical_and(first_line, me == 0)
-    roof = jnp.logical_and(jnp.logical_not(first_line), me == span - 1)
-
+    faces = Faces(dims, facts_ref, phys_ref, core_ref)
+    wanted = tuple(range(1, SIDE - 1))
     for tile in range(count // LANES):
-
-        def reader(var, tile=tile):
-            def read(i, j):
-                node = SIDE * i + j
-                ref = phys_ref if node in RIM_NODES else core_ref
-                nodes = RIM_NODES if node in RIM_NODES else CORE_NODES
-                return ref[tile, var, pl.ds(nodes.index(node) * SUB, SUB), :]
-
-            return read
-
-        def halo(var, t, tile=tile):
-            return phys_ref[tile, var, pl.ds((len(RIM_NODES) + t) * SUB, SUB), :]
-
-        speed_x = sides_x(reader(0), flip_x, flip_y)
-        speed_y = sides_y(reader(1), flip_x, flip_y)
-        pace_x = [[turn_x * speed for speed in side] for side in speed_x]
-        pace_y = [[turn_y * speed for speed in side] for side in speed_y]
+        pace = faces.pace_y(tile, wanted)
         for var in range(num_vars):
-            q = reader(var)
-            mirror = 1.0 if var == num_vars - 1 else -1.0
-            total = {}
-            for j in range(SIDE):
-                flux = [q(i, j) * reader(0)(i, j) for i in range(SIDE)]
-                for i in range(SIDE):
-                    acc = None
-                    for s in range(SIDE):
-                        if abs(deriv[i, s]) > 1e-6:
-                            term = flux[s] * float(deriv[i, s])
-                            acc = term if acc is None else acc + term
-                    total[i, j] = -scale_x * acc
-            for i in range(SIDE):
-                flux = [q(i, j) * reader(1)(i, j) for j in range(SIDE)]
-                for j in range(SIDE):
-                    acc = None
-                    for s in range(SIDE):
-                        if abs(deriv[j, s]) > 1e-6:
-                            term = flux[s] * float(deriv[j, s])
-                            acc = term if acc is None else acc + term
-                    total[i, j] = total[i, j] - scale_y * acc
-            trace = sides_x(q, flip_x, flip_y)
-            low, high = [], []
-            for t in range(SIDE):
-                pace, value = pace_x[0][t], trace[0][t]
-                own_low, give_low = -(pace + 1.0) * value, (1.0 - pace) * value
-                pace, value = pace_x[1][t], trace[1][t]
-                own_high, give_high = (pace - 1.0) * value, (1.0 + pace) * value
-                from_low = jnp.where(first_col, 0.0, pltpu.roll(give_high, 1, 0))
-                from_high = jnp.where(last_col, 0.0, pltpu.roll(give_low, SUB - 1, 0))
-                low.append(weight_x * (own_low + from_low))
-                high.append(weight_x * (own_high + from_high))
-            for i, side in (
-                (0, back(low, high, flip_x, flip_y)),
-                (5, back(high, low, flip_x, flip_y)),
-            ):
-                for t in range(SIDE):
-                    total[i, t] = total[i, t] + side[t]
-            trace = sides_y(q, flip_x, flip_y)
-            low, high = [], []
-            for t in range(SIDE):
-                pace, value = pace_y[0][t], trace[0][t]
-                own_low, give_low = -(pace + 1.0) * value, (1.0 - pace) * value
-                pace, value = pace_y[1][t], trace[1][t]
-                own_high, give_high = (pace - 1.0) * value, (1.0 + pace) * value
-                outside = (1.0 + turn_halo * halo(1, t)) * halo(var, t)
-                outside = jnp.where(floor, mirror * give_low, outside)
-                outside = jnp.where(roof, mirror * give_high, outside)
-                from_low = jnp.where(first_line, outside, pltpu.roll(give_high, cols, 0))
-                from_high = jnp.where(first_line, pltpu.roll(give_low, SUB - cols, 0), outside)
-                low.append(weight_y * (own_low + from_low))
-                high.append(weight_y * (own_high + from_high))
-            for j, side in (
-                (0, back(low, high, flip_y, flip_x)),
-                (5, back(high, low, flip_y, flip_x)),
-            ):
-                for t in range(SIDE):
-                    total[t, j] = total[t, j] + side[t]
-            for i in range(SIDE):
-                for j in range(SIDE):
-                    if i in (0, 5):
-                        ref, node = edge_ref, i // 5 * SIDE + j
-                    else:
-                        ref, node = rate_ref, SIDE * (i - 1) + j
-                    at = pl.ds(node * SUB, SUB)
-                    ref[var, at, pl.ds(tile * LANES, LANES)] = total[i, j]
-                    ref[var, at, pl.ds(count + tile * LANES, LANES)] = q(i, j) * reader(2)(i, j)
+            total = faces.volume(tile, var, wanted)
+            faces.faces_y(tile, var, pace, wanted, total)
+            q, w = faces.reader(tile, var), faces.reader(tile, 2)
+            store_rates(rate_ref, MID_NODES, tile, var, count, total, q, w)
     parts = to_modes(dims, me, high_ref, low_ref, [rate_ref[var] for var in range(num_vars)])
     for k in range(span):
-        mid_ref[k] = parts[k]
+        outs[k][...] = parts[k]
 
 
 def edges_kernel(
-    dims, where_ref, facts_ref, high_ref, low_ref, mid_ref, edge_ref, one_ref, two_ref, *refs
+    dims, facts_ref, high_ref, low_ref, phys_ref, core_ref, one_ref, two_ref, *refs
 ):
     cols, share, span, num_vars, modes = dims
-    outs = refs[:span]
-    rate_ref = refs[span]
+    odd_ref, *evens, rate_ref = refs
     count = span * modes
     lines = share // cols
-    odd = where_ref[1] == 1
-    slot = lax.broadcasted_iota(jnp.int32, (SUB, LANES), 0)
-    flip_x = facts_ref[2] > 0.5
-    flip_y = facts_ref[3] > 0.5
-    weight = 7.5 * jnp.abs(facts_ref[0])
+    odd = lax.axis_index("elem") % 2 == 1
+    faces = Faces(dims, facts_ref, phys_ref, core_ref)
+    wanted = (0, SIDE - 1)
     for tile in range(count // LANES):
+        pace_x, pace_y = faces.pace_x(tile), faces.pace_y(tile, wanted)
         for var in range(num_vars):
-            low, high = [], []
-            for t in range(SIDE):
-                below, above = jnp.zeros((SUB, LANES)), jnp.zeros((SUB, LANES))
+
+            def rim(t, tile=tile, var=var):
+                found = []
                 for line in range(lines):
                     at = pl.ds(t * lines + line, 1)
                     one, two = one_ref[tile, var, at, :], two_ref[tile, var, at, :]
-                    below = jnp.where(slot == line * cols, jnp.where(odd, one, two), below)
-                    above = jnp.where(
-                        slot == (line + 1) * cols - 1, jnp.where(odd, two, one), above
-                    )
-                low.append(weight * below)
-                high.append(weight * above)
-            for i, side in enumerate(
-                (back(low, high, flip_x, flip_y), back(high, low, flip_x, flip_y))
-            ):
-                for t in range(SIDE):
-                    at = (pl.ds((i * SIDE + t) * SUB, SUB), pl.ds(tile * LANES, LANES))
-                    rate_ref[var, at[0], at[1]] = edge_ref[var, at[0], at[1]] + side[t]
-    rates = [
-        jnp.concatenate([rate_ref[var], edge_ref[var, :, count:]], axis=1)
-        for var in range(num_vars)
-    ]
-    parts = to_modes(dims, where_ref[0], high_ref, low_ref, rates)
-    half = SIDE * share
+                    found.append((jnp.where(odd, one, two), jnp.where(odd, two, one)))
+                return found
+
+            total = faces.volume(tile, var, wanted)
+            faces.faces_x(tile, var, pace_x, total, rim)
+            faces.faces_y(tile, var, pace_y, wanted, total)
+            q, w = faces.reader(tile, var), faces.reader(tile, 2)
+            store_rates(rate_ref, END_NODES, tile, var, count, total, q, w)
+    me = lax.axis_index("span")
+    parts = to_modes(dims, me, high_ref, low_ref, [rate_ref[var] for var in range(num_vars)])
+    size = len(END_NODES) * share
     for k in range(span):
-        outs[k][:half] = parts[k][:half]
-        outs[k][half : (NODES - SIDE) * share] = mid_ref[k]
-        outs[k][(NODES - SIDE) * share :] = parts[k][half:]
-
-
-def gather_kernel(dims, where_ref, pick_ref, state_ref, *refs):
+        if k % 2:
+            odd_ref[pl.ds(k // 2 * size, size), :] = parts[k]
+        else:
+            evens[k // 2][...] = parts[k]
+
+
+def put_back(nodes, share, elems, pick_ref, takes, flat):
+    turned = pick_ref[...].T[:elems]
+    pick = jnp.concatenate([turned] * (LANES // elems), axis=1).astype(jnp.bfloat16)
+    for at in range(0, len(nodes), 2):
+        columns = []
+        for row in (at * share, (at + 1) * share):
+            part = jnp.concatenate([take[pl.ds(row, share), :] for take in takes], axis=0)
+            columns.append(jnp.concatenate(split(part), axis=0))
+        moved = mm(pick, jnp.concatenate(columns, axis=1))
+        flat[pl.ds(nodes[at], elems, stride=NODES), :] = moved[:, :LANES]
+        flat[pl.ds(nodes[at + 1], elems, stride=NODES), :] = moved[:, LANES:]
+
+
+def collect_kernel(dims, pick_ref, *refs):
+    rows, cols, share, span, _ = dims
+    put_back(MID_NODES, share, rows * cols, pick_ref, refs[:span], refs[span])
+
+
+def finish_kernel(dims, pick_ref, state_ref, flat_in, *refs):
     rows, cols, share, span, modes = dims
-    takes = refs[:span]
-    out_any, flat, out_ref, sems = refs[span:]
+    takes = unpaired(refs[: span // 2 + 1], len(END_NODES) * share)
+    out_any, flat, out_ref, sems = refs[span // 2 + 1 :]
     elems = rows * cols
     count = span * modes
-    turned = pick_ref[...].T[:elems]
-    pick = jnp.concatenate([turned] * (LANES // elems), axis=1).astype(jnp.bfloat16)
-    for node in range(NODES):
-        part = jnp.concatenate([take[pl.ds(node * share, share), :] for take in takes], axis=0)
-        high, low = split(part)
-        flat[pl.ds(node, elems, stride=NODES), :] = mm(pick, jnp.concatenate([high, low], axis=0))
-    index = where_ref[0] * modes + lax.broadcasted_iota(jnp.int32, (LANES, 1), 0) % modes
+    put_back(END_NODES, share, elems, pick_ref, takes, flat)
+    me = lax.axis_index("span")
+    index = me * modes + lax.broadcasted_iota(jnp.int32, (LANES, 1), 0) % modes
     wave = jnp.where(index == 1, count // 2, index // 2).astype(jnp.float32)
     damping = 1.0 / (1.0 + TIME_STEP * VISCOSITY * wave * wave)
     copies = []
@@ -493,10 +569,6 @@
         copy.wait()
 
 
-def smem():
-    return pl.BlockSpec(memory_space=pltpu.SMEM)
-
-
 def in_hbm(array):
     return pltpu.with_memory_space_constraint(array, pltpu.HBM)
 
@@ -517,6 +589,17 @@
     for k in range(1, span):
         taken[k] = lax.ppermute(blocks[k], "span", [(s, s ^ k) for s in range(span)])
     return [taken[k] for k in range(span)]
+
+
+def relayed(odds, evens, span):
+    size = evens[0].shape[0]
+    passed = lax.ppermute(odds, "span", [(s, s ^ 1) for s in range(span)])
+    taken = [evens[0], passed[:size]]
+    for at in range(1, span // 2):
+        both = jnp.concatenate([evens[at], passed[at * size : (at + 1) * size]])
+        both = lax.ppermute(both, "span", [(s, s ^ (2 * at)) for s in range(span)])
+        taken.append(both)
+    return taken
 
 
 def ordered_body(state, metric, neighbour, wall, rim):
@@ -530,25 +613,25 @@
     count = modes * span
     tiles = count // LANES
     lines = share // cols
-    me = jnp.stack([lax.axis_index("span"), lax.axis_index("elem") % 2])
     flat_state = state.reshape(num_vars * modes, flat_size)
     f32 = jnp.float32
-    whole, rim_part, core_part = (
+    mid_part, end_part, rim_part, core_part = (
         jax.ShapeDtypeStruct((nodes * share, LANES), f32)
-        for nodes in (NODES, len(RIM_NODES) + SIDE, len(CORE_NODES))
+        for nodes in (len(MID_NODES), len(END_NODES), len(RIM_NODES) + SIDE, len(CORE_NODES))
     )
     chunks = flat_size // CHUNK
     first = pl.pallas_call(
         functools.partial(spread_kernel, (rows, cols, share, span)),
         out_shape=[rim_part] * span
-        + [core_part] * span
         + [
             jax.ShapeDtypeStruct((elems, LANES), f32),
             jax.ShapeDtypeStruct((4, share, LANES), f32),
+            jax.ShapeDtypeStruct((flat_size, LANES), f32),
         ],
-        in_specs=[smem()] + anywhere(5),
-        out_specs=vmem(2 * span + 2),
+        in_specs=anywhere(5),
+        out_specs=vmem(span + 3),
         scratch_shapes=[
+            pltpu.VMEM((4, elems, LANES), f32),
             pltpu.VMEM((elems, LANES), f32),
             pltpu.VMEM((2, elems, LANES), jnp.int32),
             pltpu.SMEM(neighbour.T.shape, jnp.int32),
@@ -556,15 +639,24 @@
             pltpu.SMEM(rim.shape, jnp.int32),
             pltpu.SMEM(metric.shape, f32),
             pltpu.VMEM(flat_state.shape, f32),
-            pltpu.VMEM((flat_size, LANES), f32),
             pltpu.SemaphoreType.DMA((4 + chunks,)),
         ],
         compiler_params=PARAMS,
         name="spread",
-    )(me, *[in_hbm(x) for x in (neighbour.T, wall.T, rim, metric, flat_state)])
+    )(*[in_hbm(x) for x in (neighbour.T, wall.T, rim, metric, flat_state)])
     rim_takes = exchange(first[:span], span)
-    core_takes = exchange(first[span : 2 * span], span)
-    pick, facts = first[2 * span :]
+    pick, facts, turned = first[span:]
+    spread_core = pl.pallas_call(
+        functools.partial(spread_core_kernel, share, span),
+        out_shape=[jax.ShapeDtypeStruct((span // 2 * core_part.shape[0], LANES), f32)]
+        + [core_part] * (span // 2),
+        in_specs=vmem(2),
+        out_specs=vmem(1 + span // 2),
+        compiler_params=PARAMS,
+        name="spread_core",
+    )
+    odds, *evens = spread_core(pick, turned)
+    core_takes = relayed(odds, evens, span)
 
     dims = (cols, share, span, num_vars, modes)
     forward = [jnp.asarray(t) for t in forward_tables(count)]
@@ -577,58 +669,66 @@
             line_shape,
             line_shape,
         ],
-        in_specs=[smem()] + vmem(3 + span),
+        in_specs=vmem(3 + span),
         out_specs=vmem(3),
         compiler_params=PARAMS,
         name="planes",
     )
-    phys, one, two = planes(me, facts, *forward, *rim_takes)
+    phys, one, two = planes(facts, *forward, *rim_takes)
     one = lax.ppermute(one, "elem", [(g, g ^ 1) for g in range(groups)])
     two = lax.ppermute(
         two, "elem", [(g, (g - 1 if g % 2 == 0 else g + 1) % groups) for g in range(groups)]
     )
 
-    middle = NODES - 2 * SIDE
     rates = pl.pallas_call(
         functools.partial(rates_kernel, dims),
-        out_shape=[
-            jax.ShapeDtypeStruct((span, middle * share, LANES), f32),
-            jax.ShapeDtypeStruct((num_vars, 2 * SIDE * share, 2 * count), f32),
-        ],
-        in_specs=[smem()] + vmem(6 + span),
-        out_specs=vmem(2),
-        scratch_shapes=[
-            pltpu.VMEM((tiles, num_vars, len(CORE_NODES) * share, LANES), f32),
-            pltpu.VMEM((num_vars, middle * share, 2 * count), f32),
-        ],
+        out_shape=[mid_part] * span
+        + [jax.ShapeDtypeStruct((tiles, num_vars, len(CORE_NODES) * share, LANES), f32)],
+        in_specs=vmem(7 + span // 2),
+        out_specs=vmem(span + 1),
+        scratch_shapes=[pltpu.VMEM((num_vars, len(MID_NODES) * share, 2 * count), f32)],
         compiler_params=PARAMS,
         name="rates",
     )
-    mid, edge = rates(me, facts, *forward, *backward, phys, *core_takes)
-    gains = pl.pallas_call(
+    *mids, core = rates(facts, *forward, *backward, phys, *core_takes)
+    mid_takes = exchange(mids, span)
+    edges = pl.pallas_call(
         functools.partial(edges_kernel, dims),
-        out_shape=[whole] * span,
-        in_specs=[smem()] + vmem(7),
-        out_specs=vmem(span),
-        scratch_shapes=[pltpu.VMEM((num_vars, 2 * SIDE * share, count), f32)],
+        out_shape=[jax.ShapeDtypeStruct((span // 2 * end_part.shape[0], LANES), f32)]
+        + [end_part] * (span // 2),
+        in_specs=vmem(7),
+        out_specs=vmem(1 + span // 2),
+        scratch_shapes=[pltpu.VMEM((num_vars, len(END_NODES) * share, 2 * count), f32)],
         compiler_params=PARAMS,
         name="edges",
-    )(me, facts, *backward, mid, edge, one, two)
-    takes = exchange(gains, span)
-
-    out = pl.pallas_call(
-        functools.partial(gather_kernel, (rows, cols, share, span, modes)),
-        out_shape=jax.ShapeDtypeStruct((num_vars * modes, flat_size), f32),
-        in_specs=[smem()] + vmem(2 + span),
-        out_specs=pl.BlockSpec(memory_space=pltpu.HBM),
+    )
+    odds, *evens = edges(facts, *backward, phys, core, one, two)
+    end_takes = relayed(odds, evens, span)
+
+    dims = (rows, cols, share, span, modes)
+    flat_shape = jax.ShapeDtypeStruct((flat_size, LANES), f32)
+    collect = pl.pallas_call(
+        functools.partial(collect_kernel, dims),
+        out_shape=flat_shape,
+        in_specs=vmem(1 + span),
+        out_specs=vmem(1)[0],
+        compiler_params=PARAMS,
+        name="collect",
+    )
+    flat = collect(pick, *mid_takes)
+    out, _ = pl.pallas_call(
+        functools.partial(finish_kernel, dims),
+        out_shape=[jax.ShapeDtypeStruct(flat_state.shape, f32), flat_shape],
+        in_specs=vmem(4 + span // 2),
+        out_specs=anywhere(1) + vmem(1),
         scratch_shapes=[
-            pltpu.VMEM((flat_size, LANES), f32),
             pltpu.VMEM(flat_state.shape, f32),
             pltpu.SemaphoreType.DMA((chunks,)),
         ],
+        input_output_aliases={2: 1},
         compiler_params=PARAMS,
-        name="collect",
-    )(me, pick, flat_state, *takes)
+        name="finish",
+    )(pick, flat_state, flat, *end_takes)
     return out.reshape(state.shape)
 
 

time: 56.3 us -> 52.3 us (0.929)
  Pallas kernels: 12.7 us -> 9.26 us
  starting transfers between devices: 28.4 us -> 25 us
  waiting for transfers between devices: 14.9 us -> 17.5 us
    ppermute x21 -> x14, starting transfers between devices: 24.1 us -> 12.6 us  [exchange(): lax.ppermute(blocks[k], 'span', [(s, s ^ k) for s in range(span)])]
    ppermute x0 -> x8, starting transfers between devices: none -> 8.28 us  [the longest x6 7.65 us: relayed(): both = lax.ppermute(both, 'span', [(s, s ^ 2 * at) for s in range(span)])]
    ppermute x0 -> x8, waiting for transfers between devices: none -> 5.07 us  [the longest x6 5.06 us: relayed(): both = lax.ppermute(both, 'span', [(s, s ^ 2 * at) for s in range(span)])]
    ppermute x21 -> x14, waiting for transfers between devices: 14.6 us -> 11.1 us  [exchange(): lax.ppermute(blocks[k], 'span', [(s, s ^ k) for s in range(span)])]
    pallas_call x4 -> x6, Pallas kernels: 9.07 us -> 6.58 us  [the longest x1 2.43 us: ordered_body(): *mids, core = rates(facts, *forward, *backward, phys, *core_takes)]
    ppermute x1, waiting for transfers between devices: 0.24 us -> 1.36 us  [ordered_body(): lax.ppermute(two, 'elem', [(g, (g - 1 if g % 2 == 0 else g + 1) % groups)...]
    pallas_call x1, Pallas kernels: 3.61 us -> 2.67 us  [ordered_body(): pl.pallas_call(functools.partial(spread_kernel, (rows, cols, share, span)...]
  transfers between devices with their start and end apart: 23 -> 24, of which waited for: 6 -> 7; matrix products, arithmetic and copies ran while one was open for 0% -> 0% of each run, Pallas kernels for 9% -> 7%
where the time goes in v1:
time: 52.3 us; the launch traced here: 52.1 us
  starting transfers between devices  25 us (48%)
  waiting for transfers between devices  17.5 us (33%)
  Pallas kernels  9.26 us (18%)
    ppermute x14, starting transfers between devices, exchange(): lax.ppermute(blocks[k], 'span', [(s, s ^ k) for s in range(span)])  12.6 us
    ppermute x14, waiting for transfers between devices, exchange(): lax.ppermute(blocks[k], 'span', [(s, s ^ k) for s in range(span)])  11.1 us
    ppermute x6, starting transfers between devices, relayed(): both = lax.ppermute(both, 'span', [(s, s ^ 2 * at) for s in range(span)])  7.65 us
    ppermute x6, waiting for transfers between devices, relayed(): both = lax.ppermute(both, 'span', [(s, s ^ 2 * at) for s in range(span)])  5.06 us
    pallas_call x1, Pallas kernels, ordered_body(): pl.pallas_call(functools.partial(spread_kernel, (rows, cols, share, span)...  2.67 us
    ppermute x1, starting transfers between devices, ordered_body(): lax.ppermute(two, 'elem', [(g, (g - 1 if g % 2 == 0 else g + 1) % groups)...  2.48 us
    pallas_call x1, Pallas kernels, ordered_body(): *mids, core = rates(facts, *forward, *backward, phys, *core_takes)  2.43 us
    ppermute x1, starting transfers between devices, ordered_body(): one = lax.ppermute(one, 'elem', [(g, g ^ 1) for g in range(groups)])  1.64 us
  transfers between devices with their start and end apart: 24, of which 7 were waited for; matrix products, arithmetic and copies ran while one was open for 0% of the time, Pallas kernels for 7%

profile of v1, /device:TPU:0, one launch (start us, length us, event | category | flops | bytes accessed | tf_op | source)
XLA Modules:
  0.0 52.1 jit_solution(4442509319503980987)
XLA Ops:
  0.0 2.7 %spread.1 = (f32[208,128]{1,0:T(8,128)S(1)}, f32[208,128]{1,0:T(8,128)S(1)}, f32[208,128]{1,0:T(8,128)S(1)}, f32[208,128]{1,0:T(8,128)S(1)}, f32[208,128]{1,0:T(...) custom-call(s32[4,64]{1,0:T(4,128)} %bitcast.6, ...), custom_call_target="tpu_custom_call" | custom-call | tf_op jit(solution)/shard_map/spread/pallas_call | solution.py:623
  2.7 0.0 copy-start.3
  2.7 0.0 copy-start.4
  2.7 0.2 spread_core.1
  2.9 0.6 %collective-permute-start.7 = (f32[512,128]{1,0:T(8,128)S(1)}, f32[512,128]{1,0:T(8,128)S(1)}, u32[]{:S(2)}, u32[]{:S(2)}) collective-permute-start(f32[512,128]{1,0:T(8,128)S(1)} %get-tuple-element.52), channel_id=1, source_target_pairs={{0,1},{1,0},{2,3},{3,2},{4,5},{5,4},{6,7},{7,6},{8,9},{9,8},{10,11... | collective-permute-start | bytes 786440 | tf_op jit(solution)/shard_map/ppermute | solution.py:596
  3.5 0.1 collective-permute-start
  3.6 2.9 %collective-permute-start.1 = (f32[208,128]{1,0:T(8,128)S(1)}, f32[208,128]{1,0:T(8,128)S(1)}, u32[]{:S(2)}, u32[]{:S(2)}) collective-permute-start(f32[208,128]{1,0:T(8,128)S(1)} %get-tuple-element.43), channel_id=1, source_target_pairs={{0,2},{1,3},{2,0},{3,1},{4,6},{5,7},{6,4},{7,5},{8,10},{9,11},{10,... | collective-permute-start | bytes 319496 | tf_op jit(solution)/shard_map/ppermute | solution.py:590
  6.5 0.0 collective-permute-start.2
  6.5 1.5 %collective-permute-start.3 = (f32[208,128]{1,0:T(8,128)S(1)}, f32[208,128]{1,0:T(8,128)S(1)}, u32[]{:S(2)}, u32[]{:S(2)}) collective-permute-start(f32[208,128]{1,0:T(8,128)S(1)} %get-tuple-element.45), channel_id=1, source_target_pairs={{0,4},{1,5},{2,6},{3,7},{4,0},{5,1},{6,2},{7,3},{8,12},{9,13},{10,... | collective-permute-start | bytes 319496 | tf_op jit(solution)/shard_map/ppermute | solution.py:590
  8.0 0.0 collective-permute-done.7
  8.0 0.0 copy-start.1
  8.0 0.3 collective-permute-start.4
  8.4 0.0 collective-permute-done.refs_1_
  8.4 2.7 %collective-permute-start.5 = (f32[208,128]{1,0:T(8,128)S(1)}, f32[208,128]{1,0:T(8,128)S(1)}, u32[]{:S(2)}, u32[]{:S(2)}) collective-permute-start(f32[208,128]{1,0:T(8,128)S(1)} %get-tuple-element.47), channel_id=1, source_target_pairs={{0,6},{1,7},{2,4},{3,5},{4,2},{5,3},{6,0},{7,1},{8,14},{9,15},{10,... | collective-permute-start | bytes 319496 | tf_op jit(solution)/shard_map/ppermute | solution.py:590
  11.1 0.0 collective-permute-done.1.refs_2_
  11.1 0.1 collective-permute-start.6
  11.2 0.5 collective-permute-done.2.refs_3_
  11.7 1.1 %collective-permute-start.8 = (f32[256,128]{1,0:T(8,128)S(1)}, f32[256,128]{1,0:T(8,128)S(1)}, u32[]{:S(2)}, u32[]{:S(2)}) collective-permute-start(f32[256,128]{1,0:T(8,128)S(1)} %pad_maximum_fusion), channel_id=1, source_target_pairs={{0,2},{1,3},{2,0},{3,1},{4,6},{5,7},{6,4},{7,5},{8,10},{9,11},{10,... | collective-permute-start | bytes 393224 | tf_op jit(solution)/shard_map/ppermute | solution.py:600
  12.8 0.0 collective-permute-done.3.refs_4_
  12.8 1.5 %collective-permute-start.9 = (f32[256,128]{1,0:T(8,128)S(1)}, f32[256,128]{1,0:T(8,128)S(1)}, u32[]{:S(2)}, u32[]{:S(2)}) collective-permute-start(f32[256,128]{1,0:T(8,128)S(1)} %pad_maximum_fusion.1), channel_id=1, source_target_pairs={{0,4},{1,5},{2,6},{3,7},{4,0},{5,1},{6,2},{7,3},{8,12},{9,13},{10,... | collective-permute-start | bytes 393224 | tf_op jit(solution)/shard_map/ppermute | solution.py:600
  14.3 3.9 %collective-permute-done.4.refs_5_ = f32[208,128]{1,0:T(8,128)S(1)} collective-permute-done((f32[208,128]{1,0:T(8,128)S(1)}, f32[208,128]{1,0:T(8,128)S(1)}, u32[]{:S(2)}, u32[]{:S(2)}) %collective-permute-start.4) | collective-permute-done | bytes 106528 | tf_op jit(solution)/shard_map/ppermute | solution.py:590
  18.2 2.8 %collective-permute-start.10 = (f32[256,128]{1,0:T(8,128)S(1)}, f32[256,128]{1,0:T(8,128)S(1)}, u32[]{:S(2)}, u32[]{:S(2)}) collective-permute-start(f32[256,128]{1,0:T(8,128)S(1)} %pad_maximum_fusion.2), channel_id=1, source_target_pairs={{0,6},{1,7},{2,4},{3,5},{4,2},{5,3},{6,0},{7,1},{8,14},{9,15},{10,... | collective-permute-start | bytes 393224 | tf_op jit(solution)/shard_map/ppermute | solution.py:600
  21.0 0.0 collective-permute-done.5.refs_6_
  21.0 0.0 collective-permute-done.6.refs_7_
  21.0 0.0 copy-done.3
  21.0 0.0 copy-done.4
  21.1 0.8 %planes.1 = (f32[2,4,208,128]{3,2,1,0:T(8,128)S(1)}, f32[2,4,12,128]{3,2,1,0:T(8,128)S(1)}, f32[2,4,12,128]{3,2,1,0:T(8,128)S(1)}) custom-call(f32[4,8,128]{2,1,0:T(8,128)S(1)} %get-tuple-element.40.facts_ref, bf16[256,256]{1,0:T(8,128)(2,1)S(1)} %copy-done.4, bf16[256,256]{1,0:T(8,128)(2,1)S(1)} %copy-done.3, f32[208,128]{1,0:T(8,128)S(1)} %get-tuple-element.41.refs_0_, ...), custom_call_target="tpu_custom_call" | custom-call | tf_op jit(solution)/shard_map/planes/pallas_call | solution.py:677
  21.9 1.6 %collective-permute-start.18 = (f32[2,4,12,128]{3,2,1,0:T(8,128)S(1)}, f32[2,4,12,128]{3,2,1,0:T(8,128)S(1)}, u32[]{:S(2)}, u32[]{:S(2)}) collective-permute-start(f32[2,4,12,128]{3,2,1,0:T(8,128)S(1)} %get-tuple-element.65), channel_id=1, source_target_pairs={{0,8},{8,0},{16,24},{24,16},{1,9},{9,1},{17,25},{25,17},{2,10},{10... | collective-permute-start | bytes 147464 | tf_op jit(solution)/shard_map/ppermute | solution.py:678
  23.5 2.5 %collective-permute-start.19 = (f32[2,4,12,128]{3,2,1,0:T(8,128)S(1)}, f32[2,4,12,128]{3,2,1,0:T(8,128)S(1)}, u32[]{:S(2)}, u32[]{:S(2)}) collective-permute-start(f32[2,4,12,128]{3,2,1,0:T(8,128)S(1)} %get-tuple-element.66), channel_id=1, source_target_pairs={{0,24},{8,16},{16,8},{24,0},{1,25},{9,17},{17,9},{25,1},{2,26},{10... | collective-permute-start | bytes 147464 | tf_op jit(solution)/shard_map/ppermute | solution.py:679
  26.0 0.0 collective-permute-done.8.refs_2_
  26.0 0.0 collective-permute-done.9.refs_3_
  26.0 0.0 collective-permute-done.10.refs_4_
  26.0 0.0 copy-done.1
  26.0 0.0 copy-done.2
  26.0 2.4 %rates.1 = (f32[192,128]{1,0:T(8,128)S(1)}, f32[192,128]{1,0:T(8,128)S(1)}, f32[192,128]{1,0:T(8,128)S(1)}, f32[192,128]{1,0:T(8,128)S(1)}, f32[192,128]{1,0:T(8...) custom-call(f32[4,8,128]{2,1,0:T(8,128)S(1)} %get-tuple-element.40.f, ...), custom_call_target="tpu_custom_call" | custom-call | tf_op jit(solution)/shard_map/rates/pallas_call | solution.py:693
  28.5 0.0 collective-permute-done.18.one_ref
  28.5 1.4 %collective-permute-done.19.two_ref = f32[2,4,12,128]{3,2,1,0:T(8,128)S(1)} collective-permute-done((f32[2,4,12,128]{3,2,1,0:T(8,128)S(1)}, f32[2,4,12,128]{3,2,1,0:T(8,128)S(1)}, u32[]{:S(2)}, u32[]{:S(2)}) %collective-permute-start.19) | collective-permute-done | bytes 49184 | tf_op jit(solution)/shard_map/ppermute | solution.py:679
  29.8 1.2 %edges.1 = (f32[384,128]{1,0:T(8,128)S(1)}, f32[96,128]{1,0:T(8,128)S(1)}, f32[96,128]{1,0:T(8,128)S(1)}, f32[96,128]{1,0:T(8,128)S(1)}, f32[96,128]{1,0:T(8,128)S(1)}) custom-call(f32[4,8,128]{2,1,0:T(8,128)S(1)} %get-tuple-element.40.facts_ref, bf16[256,512]{1,0:T(8,128)(2,1)S(1)} %copy-done.2, bf16[256,512]{1,0:T(8,128)(2,1)S(1)} %copy-done.1, ...), custom_call_target="tpu_custom_call" | custom-call | tf_op jit(solution)/shard_map/edges/pallas_call | solution.py:705
  31.0 0.1 collective-permute-start.20
  31.1 0.5 collective-permute-start.11
  31.6 0.6 %collective-permute-start.12 = (f32[192,128]{1,0:T(8,128)S(1)}, f32[192,128]{1,0:T(8,128)S(1)}, u32[]{:S(2)}, u32[]{:S(2)}) collective-permute-start(f32[192,128]{1,0:T(8,128)S(1)} %get-tuple-element.58), channel_id=1, source_target_pairs={{0,2},{1,3},{2,0},{3,1},{4,6},{5,7},{6,4},{7,5},{8,10},{9,11},{10,... | collective-permute-start | bytes 294920 | tf_op jit(solution)/shard_map/ppermute | solution.py:590
  32.2 0.8 %collective-permute-start.13 = (f32[192,128]{1,0:T(8,128)S(1)}, f32[192,128]{1,0:T(8,128)S(1)}, u32[]{:S(2)}, u32[]{:S(2)}) collective-permute-start(f32[192,128]{1,0:T(8,128)S(1)} %get-tuple-element.59), channel_id=1, source_target_pairs={{0,3},{1,2},{2,1},{3,0},{4,7},{5,6},{6,5},{7,4},{8,11},{9,10},{10,... | collective-permute-start | bytes 294920 | tf_op jit(solution)/shard_map/ppermute | solution.py:590
  33.0 0.5 collective-permute-start.14
  33.5 0.0 collective-permute-done.20
  33.5 1.6 %collective-permute-start.15 = (f32[192,128]{1,0:T(8,128)S(1)}, f32[192,128]{1,0:T(8,128)S(1)}, u32[]{:S(2)}, u32[]{:S(2)}) collective-permute-start(f32[192,128]{1,0:T(8,128)S(1)} %get-tuple-element.61), channel_id=1, source_target_pairs={{0,5},{1,4},{2,7},{3,6},{4,1},{5,0},{6,3},{7,2},{8,13},{9,12},{10,... | collective-permute-start | bytes 294920 | tf_op jit(solution)/shard_map/ppermute | solution.py:590
  35.1 0.0 copy-start
  35.2 0.0 collective-permute-done.11.refs_1_
  35.2 0.7 %collective-permute-start.16 = (f32[192,128]{1,0:T(8,128)S(1)}, f32[192,128]{1,0:T(8,128)S(1)}, u32[]{:S(2)}, u32[]{:S(2)}) collective-permute-start(f32[192,128]{1,0:T(8,128)S(1)} %get-tuple-element.62), channel_id=1, source_target_pairs={{0,6},{1,7},{2,4},{3,5},{4,2},{5,3},{6,0},{7,1},{8,14},{9,15},{10,... | collective-permute-start | bytes 294920 | tf_op jit(solution)/shard_map/ppermute | solution.py:590
  35.9 1.4 %collective-permute-done.12.refs_2_ = f32[192,128]{1,0:T(8,128)S(1)} collective-permute-done((f32[192,128]{1,0:T(8,128)S(1)}, f32[192,128]{1,0:T(8,128)S(1)}, u32[]{:S(2)}, u32[]{:S(2)}) %collective-permute-start.12) | collective-permute-done | bytes 98336 | tf_op jit(solution)/shard_map/ppermute | solution.py:590
  37.3 0.3 collective-permute-start.17
  37.6 0.0 collective-permute-done.13.refs_3_
  37.6 1.1 %collective-permute-start.21 = (f32[192,128]{1,0:T(8,128)S(1)}, f32[192,128]{1,0:T(8,128)S(1)}, u32[]{:S(2)}, u32[]{:S(2)}) collective-permute-start(f32[192,128]{1,0:T(8,128)S(1)} %pad_maximum_fusion.3), channel_id=1, source_target_pairs={{0,2},{1,3},{2,0},{3,1},{4,6},{5,7},{6,4},{7,5},{8,10},{9,11},{10,... | collective-permute-start | bytes 294920 | tf_op jit(solution)/shard_map/ppermute | solution.py:600
  38.7 0.0 collective-permute-done.14.refs_4_
  38.7 0.5 collective-permute-start.22
  39.2 5.3 %collective-permute-done.15.refs_5_ = f32[192,128]{1,0:T(8,128)S(1)} collective-permute-done((f32[192,128]{1,0:T(8,128)S(1)}, f32[192,128]{1,0:T(8,128)S(1)}, u32[]{:S(2)}, u32[]{:S(2)}) %collective-permute-start.15) | collective-permute-done | bytes 98336 | tf_op jit(solution)/shard_map/ppermute | solution.py:590
  44.5 0.6 %collective-permute-start.23 = (f32[192,128]{1,0:T(8,128)S(1)}, f32[192,128]{1,0:T(8,128)S(1)}, u32[]{:S(2)}, u32[]{:S(2)}) collective-permute-start(f32[192,128]{1,0:T(8,128)S(1)} %pad_maximum_fusion.5), channel_id=1, source_target_pairs={{0,6},{1,7},{2,4},{3,5},{4,2},{5,3},{6,0},{7,1},{8,14},{9,15},{10,... | collective-permute-start | bytes 294920 | tf_op jit(solution)/shard_map/ppermute | solution.py:600
  45.1 0.0 collective-permute-done.16.refs_6_
  45.1 0.0 collective-permute-done.17.refs_7_
  45.1 0.4 collect.1.flat_in
  45.5 0.0 collective-permute-done.21.refs_2_
  45.5 1.4 %collective-permute-done.22.refs_3_ = f32[192,128]{1,0:T(8,128)S(1)} collective-permute-done((f32[192,128]{1,0:T(8,128)S(1)}, f32[192,128]{1,0:T(8,128)S(1)}, u32[]{:S(2)}, u32[]{:S(2)}) %collective-permute-start.22) | collective-permute-done | bytes 98336 | tf_op jit(solution)/shard_map/ppermute | solution.py:600
  46.9 3.7 %collective-permute-done.23.refs_4_ = f32[192,128]{1,0:T(8,128)S(1)} collective-permute-done((f32[192,128]{1,0:T(8,128)S(1)}, f32[192,128]{1,0:T(8,128)S(1)}, u32[]{:S(2)}, u32[]{:S(2)}) %collective-permute-start.23) | collective-permute-done | bytes 98336 | tf_op jit(solution)/shard_map/ppermute | solution.py:600
  50.6 0.0 copy-done
  50.6 1.6 %finish.1 = (f32[128,2304]{1,0:T(8,128)}, f32[2304,128]{1,0:T(8,128)S(1)}) custom-call(f32[64,128]{1,0:T(8,128)S(1)} %get-tuple-element.39.pick_ref, f32[128,2304]{1,0:T(8,128)S(1)} %bitcast.5, f32[2304,128]{1,0:T(8,128)S(1)} %collect.1.flat_in, f32[96,128]{1,0:T(8,128)S(1)} %get-tuple-element.67.refs_0_, ...), custom_call_target="tpu_custom_call", output_to_operand_aliasing={{1}: (2, {})} | custom-call | tf_op jit(solution)/shard_map/finish/pallas_call | solution.py:719
  (9 shorter events, 0.1 us)
Async XLA Ops:
  2.7 18.4 %copy-start.3 = (bf16[256,256]{1,0:T(8,128)(2,1)S(1)}, bf16[256,256]{1,0:T(8,128)(2,1)}, u32[]{:S(2)}) copy-start(bf16[256,256]{1,0:T(8,128)(2,1)} %constant.9.clone.low_ref.there_low) | copy-start | bytes 393220
  2.7 18.4 %copy-start.4 = (bf16[256,256]{1,0:T(8,128)(2,1)S(1)}, bf16[256,256]{1,0:T(8,128)(2,1)}, u32[]{:S(2)}) copy-start(bf16[256,256]{1,0:T(8,128)(2,1)} %constant.8.clone.high_ref.there_high) | copy-start | bytes 393220
  2.9 5.1 %collective-permute-start.7 = (f32[512,128]{1,0:T(8,128)S(1)}, f32[512,128]{1,0:T(8,128)S(1)}, u32[]{:S(2)}, u32[]{:S(2)}) collective-permute-start(f32[512,128]{1,0:T(8,128)S(1)} %get-tuple-element.52), channel_id=1, source_target_pairs={{0,1},{1,0},{2,3},{3,2},{4,5},{5,4},{6,7},{7,6},{8,9},{9,8},{10,11... | collective-permute-start | bytes 786440 | tf_op jit(solution)/shard_map/ppermute | solution.py:596
  3.5 4.9 %collective-permute-start = (f32[208,128]{1,0:T(8,128)S(1)}, f32[208,128]{1,0:T(8,128)S(1)}, u32[]{:S(2)}, u32[]{:S(2)}) collective-permute-start(f32[208,128]{1,0:T(8,128)S(1)} %get-tuple-element.42), channel_id=1, source_target_pairs={{0,1},{1,0},{2,3},{3,2},{4,5},{5,4},{6,7},{7,6},{8,9},{9,8},{10,11... | collective-permute-start | bytes 319496 | tf_op jit(solution)/shard_map/ppermute | solution.py:590
  3.6 7.5 %collective-permute-start.1 = (f32[208,128]{1,0:T(8,128)S(1)}, f32[208,128]{1,0:T(8,128)S(1)}, u32[]{:S(2)}, u32[]{:S(2)}) collective-permute-start(f32[208,128]{1,0:T(8,128)S(1)} %get-tuple-element.43), channel_id=1, source_target_pairs={{0,2},{1,3},{2,0},{3,1},{4,6},{5,7},{6,4},{7,5},{8,10},{9,11},{10,... | collective-permute-start | bytes 319496 | tf_op jit(solution)/shard_map/ppermute | solution.py:590
  6.5 5.3 %collective-permute-start.2 = (f32[208,128]{1,0:T(8,128)S(1)}, f32[208,128]{1,0:T(8,128)S(1)}, u32[]{:S(2)}, u32[]{:S(2)}) collective-permute-start(f32[208,128]{1,0:T(8,128)S(1)} %get-tuple-element.44), channel_id=1, source_target_pairs={{0,3},{1,2},{2,1},{3,0},{4,7},{5,6},{6,5},{7,4},{8,11},{9,10},{10,... | collective-permute-start | bytes 319496 | tf_op jit(solution)/shard_map/ppermute | solution.py:590
  6.5 6.3 %collective-permute-start.3 = (f32[208,128]{1,0:T(8,128)S(1)}, f32[208,128]{1,0:T(8,128)S(1)}, u32[]{:S(2)}, u32[]{:S(2)}) collective-permute-start(f32[208,128]{1,0:T(8,128)S(1)} %get-tuple-element.45), channel_id=1, source_target_pairs={{0,4},{1,5},{2,6},{3,7},{4,0},{5,1},{6,2},{7,3},{8,12},{9,13},{10,... | collective-permute-start | bytes 319496 | tf_op jit(solution)/shard_map/ppermute | solution.py:590
  8.0 18.0 %copy-start.1 = (bf16[256,512]{1,0:T(8,128)(2,1)S(1)}, bf16[256,512]{1,0:T(8,128)(2,1)}, u32[]{:S(2)}) copy-start(bf16[256,512]{1,0:T(8,128)(2,1)} %constant.11.clone.low_ref) | copy-start | bytes 786436
  8.0 18.0 %copy-start.2 = (bf16[256,512]{1,0:T(8,128)(2,1)S(1)}, bf16[256,512]{1,0:T(8,128)(2,1)}, u32[]{:S(2)}) copy-start(bf16[256,512]{1,0:T(8,128)(2,1)} %constant.10.clone.high_ref) | copy-start | bytes 786436
  8.0 10.2 %collective-permute-start.4 = (f32[208,128]{1,0:T(8,128)S(1)}, f32[208,128]{1,0:T(8,128)S(1)}, u32[]{:S(2)}, u32[]{:S(2)}) collective-permute-start(f32[208,128]{1,0:T(8,128)S(1)} %get-tuple-element.46), channel_id=1, source_target_pairs={{0,5},{1,4},{2,7},{3,6},{4,1},{5,0},{6,3},{7,2},{8,13},{9,12},{10,... | collective-permute-start | bytes 319496 | tf_op jit(solution)/shard_map/ppermute | solution.py:590
  8.4 12.6 %collective-permute-start.5 = (f32[208,128]{1,0:T(8,128)S(1)}, f32[208,128]{1,0:T(8,128)S(1)}, u32[]{:S(2)}, u32[]{:S(2)}) collective-permute-start(f32[208,128]{1,0:T(8,128)S(1)} %get-tuple-element.47), channel_id=1, source_target_pairs={{0,6},{1,7},{2,4},{3,5},{4,2},{5,3},{6,0},{7,1},{8,14},{9,15},{10,... | collective-permute-start | bytes 319496 | tf_op jit(solution)/shard_map/ppermute | solution.py:590
  11.1 10.0 %collective-permute-start.6 = (f32[208,128]{1,0:T(8,128)S(1)}, f32[208,128]{1,0:T(8,128)S(1)}, u32[]{:S(2)}, u32[]{:S(2)}) collective-permute-start(f32[208,128]{1,0:T(8,128)S(1)} %get-tuple-element.48), channel_id=1, source_target_pairs={{0,7},{1,6},{2,5},{3,4},{4,3},{5,2},{6,1},{7,0},{8,15},{9,14},{10,... | collective-permute-start | bytes 319496 | tf_op jit(solution)/shard_map/ppermute | solution.py:590
  11.7 14.2 %collective-permute-start.8 = (f32[256,128]{1,0:T(8,128)S(1)}, f32[256,128]{1,0:T(8,128)S(1)}, u32[]{:S(2)}, u32[]{:S(2)}) collective-permute-start(f32[256,128]{1,0:T(8,128)S(1)} %pad_maximum_fusion), channel_id=1, source_target_pairs={{0,2},{1,3},{2,0},{3,1},{4,6},{5,7},{6,4},{7,5},{8,10},{9,11},{10,... | collective-permute-start | bytes 393224 | tf_op jit(solution)/shard_map/ppermute | solution.py:600
  12.8 13.2 %collective-permute-start.9 = (f32[256,128]{1,0:T(8,128)S(1)}, f32[256,128]{1,0:T(8,128)S(1)}, u32[]{:S(2)}, u32[]{:S(2)}) collective-permute-start(f32[256,128]{1,0:T(8,128)S(1)} %pad_maximum_fusion.1), channel_id=1, source_target_pairs={{0,4},{1,5},{2,6},{3,7},{4,0},{5,1},{6,2},{7,3},{8,12},{9,13},{10,... | collective-permute-start | bytes 393224 | tf_op jit(solution)/shard_map/ppermute | solution.py:600
  18.2 7.8 %collective-permute-start.10 = (f32[256,128]{1,0:T(8,128)S(1)}, f32[256,128]{1,0:T(8,128)S(1)}, u32[]{:S(2)}, u32[]{:S(2)}) collective-permute-start(f32[256,128]{1,0:T(8,128)S(1)} %pad_maximum_fusion.2), channel_id=1, source_target_pairs={{0,6},{1,7},{2,4},{3,5},{4,2},{5,3},{6,0},{7,1},{8,14},{9,15},{10,... | collective-permute-start | bytes 393224 | tf_op jit(solution)/shard_map/ppermute | solution.py:600
  21.9 6.6 %collective-permute-start.18 = (f32[2,4,12,128]{3,2,1,0:T(8,128)S(1)}, f32[2,4,12,128]{3,2,1,0:T(8,128)S(1)}, u32[]{:S(2)}, u32[]{:S(2)}) collective-permute-start(f32[2,4,12,128]{3,2,1,0:T(8,128)S(1)} %get-tuple-element.65), channel_id=1, source_target_pairs={{0,8},{8,0},{16,24},{24,16},{1,9},{9,1},{17,25},{25,17},{2,10},{10... | collective-permute-start | bytes 147464 | tf_op jit(solution)/shard_map/ppermute | solution.py:678
  23.5 6.3 %collective-permute-start.19 = (f32[2,4,12,128]{3,2,1,0:T(8,128)S(1)}, f32[2,4,12,128]{3,2,1,0:T(8,128)S(1)}, u32[]{:S(2)}, u32[]{:S(2)}) collective-permute-start(f32[2,4,12,128]{3,2,1,0:T(8,128)S(1)} %get-tuple-element.66), channel_id=1, source_target_pairs={{0,24},{8,16},{16,8},{24,0},{1,25},{9,17},{17,9},{25,1},{2,26},{10... | collective-permute-start | bytes 147464 | tf_op jit(solution)/shard_map/ppermute | solution.py:679
  31.0 2.5 %collective-permute-start.20 = (f32[384,128]{1,0:T(8,128)S(1)}, f32[384,128]{1,0:T(8,128)S(1)}, u32[]{:S(2)}, u32[]{:S(2)}) collective-permute-start(f32[384,128]{1,0:T(8,128)S(1)} %get-tuple-element.68), channel_id=1, source_target_pairs={{0,1},{1,0},{2,3},{3,2},{4,5},{5,4},{6,7},{7,6},{8,9},{9,8},{10,11... | collective-permute-start | bytes 589832 | tf_op jit(solution)/shard_map/ppermute | solution.py:596
  31.1 4.1 %collective-permute-start.11 = (f32[192,128]{1,0:T(8,128)S(1)}, f32[192,128]{1,0:T(8,128)S(1)}, u32[]{:S(2)}, u32[]{:S(2)}) collective-permute-start(f32[192,128]{1,0:T(8,128)S(1)} %get-tuple-element.57), channel_id=1, source_target_pairs={{0,1},{1,0},{2,3},{3,2},{4,5},{5,4},{6,7},{7,6},{8,9},{9,8},{10,11... | collective-permute-start | bytes 294920 | tf_op jit(solution)/shard_map/ppermute | solution.py:590
  31.6 5.7 %collective-permute-start.12 = (f32[192,128]{1,0:T(8,128)S(1)}, f32[192,128]{1,0:T(8,128)S(1)}, u32[]{:S(2)}, u32[]{:S(2)}) collective-permute-start(f32[192,128]{1,0:T(8,128)S(1)} %get-tuple-element.58), channel_id=1, source_target_pairs={{0,2},{1,3},{2,0},{3,1},{4,6},{5,7},{6,4},{7,5},{8,10},{9,11},{10,... | collective-permute-start | bytes 294920 | tf_op jit(solution)/shard_map/ppermute | solution.py:590
  32.2 5.4 %collective-permute-start.13 = (f32[192,128]{1,0:T(8,128)S(1)}, f32[192,128]{1,0:T(8,128)S(1)}, u32[]{:S(2)}, u32[]{:S(2)}) collective-permute-start(f32[192,128]{1,0:T(8,128)S(1)} %get-tuple-element.59), channel_id=1, source_target_pairs={{0,3},{1,2},{2,1},{3,0},{4,7},{5,6},{6,5},{7,4},{8,11},{9,10},{10,... | collective-permute-start | bytes 294920 | tf_op jit(solution)/shard_map/ppermute | solution.py:590
  33.0 5.7 %collective-permute-start.14 = (f32[192,128]{1,0:T(8,128)S(1)}, f32[192,128]{1,0:T(8,128)S(1)}, u32[]{:S(2)}, u32[]{:S(2)}) collective-permute-start(f32[192,128]{1,0:T(8,128)S(1)} %get-tuple-element.60), channel_id=1, source_target_pairs={{0,4},{1,5},{2,6},{3,7},{4,0},{5,1},{6,2},{7,3},{8,12},{9,13},{10,... | collective-permute-start | bytes 294920 | tf_op jit(solution)/shard_map/ppermute | solution.py:590
  33.5 11.0 %collective-permute-start.15 = (f32[192,128]{1,0:T(8,128)S(1)}, f32[192,128]{1,0:T(8,128)S(1)}, u32[]{:S(2)}, u32[]{:S(2)}) collective-permute-start(f32[192,128]{1,0:T(8,128)S(1)} %get-tuple-element.61), channel_id=1, source_target_pairs={{0,5},{1,4},{2,7},{3,6},{4,1},{5,0},{6,3},{7,2},{8,13},{9,12},{10,... | collective-permute-start | bytes 294920 | tf_op jit(solution)/shard_map/ppermute | solution.py:590
  35.1 15.4 %copy-start = (f32[4,32,2304]{2,1,0:T(8,128)S(1)}, f32[4,32,2304]{2,1,0:T(8,128)}, u32[]{:S(2)}) copy-start(f32[4,32,2304]{2,1,0:T(8,128)} %param.10) | copy-start | bytes 3538948
  35.2 9.9 %collective-permute-start.16 = (f32[192,128]{1,0:T(8,128)S(1)}, f32[192,128]{1,0:T(8,128)S(1)}, u32[]{:S(2)}, u32[]{:S(2)}) collective-permute-start(f32[192,128]{1,0:T(8,128)S(1)} %get-tuple-element.62), channel_id=1, source_target_pairs={{0,6},{1,7},{2,4},{3,5},{4,2},{5,3},{6,0},{7,1},{8,14},{9,15},{10,... | collective-permute-start | bytes 294920 | tf_op jit(solution)/shard_map/ppermute | solution.py:590
  37.3 7.8 %collective-permute-start.17 = (f32[192,128]{1,0:T(8,128)S(1)}, f32[192,128]{1,0:T(8,128)S(1)}, u32[]{:S(2)}, u32[]{:S(2)}) collective-permute-start(f32[192,128]{1,0:T(8,128)S(1)} %get-tuple-element.63), channel_id=1, source_target_pairs={{0,7},{1,6},{2,5},{3,4},{4,3},{5,2},{6,1},{7,0},{8,15},{9,14},{10,... | collective-permute-start | bytes 294920 | tf_op jit(solution)/shard_map/ppermute | solution.py:590
  37.6 7.9 %collective-permute-start.21 = (f32[192,128]{1,0:T(8,128)S(1)}, f32[192,128]{1,0:T(8,128)S(1)}, u32[]{:S(2)}, u32[]{:S(2)}) collective-permute-start(f32[192,128]{1,0:T(8,128)S(1)} %pad_maximum_fusion.3), channel_id=1, source_target_pairs={{0,2},{1,3},{2,0},{3,1},{4,6},{5,7},{6,4},{7,5},{8,10},{9,11},{10,... | collective-permute-start | bytes 294920 | tf_op jit(solution)/shard_map/ppermute | solution.py:600
  38.7 8.1 %collective-permute-start.22 = (f32[192,128]{1,0:T(8,128)S(1)}, f32[192,128]{1,0:T(8,128)S(1)}, u32[]{:S(2)}, u32[]{:S(2)}) collective-permute-start(f32[192,128]{1,0:T(8,128)S(1)} %pad_maximum_fusion.4), channel_id=1, source_target_pairs={{0,4},{1,5},{2,6},{3,7},{4,0},{5,1},{6,2},{7,3},{8,12},{9,13},{10,... | collective-permute-start | bytes 294920 | tf_op jit(solution)/shard_map/ppermute | solution.py:600
  44.5 6.1 %collective-permute-start.23 = (f32[192,128]{1,0:T(8,128)S(1)}, f32[192,128]{1,0:T(8,128)S(1)}, u32[]{:S(2)}, u32[]{:S(2)}) collective-permute-start(f32[192,128]{1,0:T(8,128)S(1)} %pad_maximum_fusion.5), channel_id=1, source_target_pairs={{0,6},{1,7},{2,4},{3,5},{4,2},{5,3},{6,0},{7,1},{8,14},{9,15},{10,... | collective-permute-start | bytes 294920 | tf_op jit(solution)/shard_map/ppermute | solution.py:600

commit v2 on v1

--- a/solution.py
+++ b/solution.py
@@ -174,16 +174,18 @@
             at = (place // share ^ me) * share + place % share
             chosen = jnp.where(lane == cell, 1.0, 0.0)
             pick_ref[pl.ds(at, 1), :] = chosen
-            if row % lines == lines - 1 and row + 1 < rows:
-                under = ((row // lines + 1) ^ me) * share + col
-                halo_ref[pl.ds(under, 1), :] = chosen
-                for kind, bend in enumerate((face, 1 - flip_y)):
-                    bends_ref[kind, pl.ds(under, 1), :] = jnp.full((1, LANES), bend, jnp.int32)
-            if row % lines == 0 and row > 0:
-                over = ((row // lines - 1) ^ me) * share + cols + col
-                halo_ref[pl.ds(over, 1), :] = chosen
-                for kind, bend in enumerate((face, flip_y)):
-                    bends_ref[kind, pl.ds(over, 1), :] = jnp.full((1, LANES), bend, jnp.int32)
+            block, line = divmod(row, lines)
+            if block % 2 and line == lines - 1 and block + 1 < rows // lines:
+                far, bends = (block + 1) ^ me, (face, 1 - flip_y)
+            elif block % 2 == 0 and line == 0 and block > 0:
+                far, bends = (block - 1) ^ me, (face, flip_y)
+            else:
+                far = None
+            for half in (0, cols) if far is not None else ():
+                place_at = far * share + half + col
+                halo_ref[pl.ds(place_at, 1), :] = chosen
+                for kind, bend in enumerate(bends):
+                    bends_ref[kind, pl.ds(place_at, 1), :] = jnp.full((1, LANES), bend, jnp.int32)
             facts = (
                 metric_ref[0, cell],
                 metric_ref[1, cell],
@@ -216,9 +218,11 @@
     bend_x = bends_ref[0] == 1
     bend_y = bends_ref[1] == 1
     trace = [jnp.where(bend_y, edge[t, 5], edge[t, 0]) for t in range(SIDE)]
-    for t in range(SIDE):
-        moved = jnp.where(bend_x, trace[SIDE - 1 - t], trace[t])
-        at = pl.ds((len(RIM_NODES) + t) * share, share)
+    upper = lax.broadcasted_iota(jnp.int32, (elems, LANES), 0) % share < cols
+    for t in range(0, SIDE, 2):
+        one, two = (jnp.where(bend_x, trace[SIDE - 1 - s], trace[s]) for s in (t, t + 1))
+        moved = jnp.where(upper, one, two)
+        at = pl.ds(len(RIM_NODES) * share + t * cols, share)
         for step in range(span):
             sends[step][at, :] = moved[step * share : (step + 1) * share]
 
@@ -291,16 +295,31 @@
 def planes_kernel(dims, facts_ref, high_ref, low_ref, *refs):
     cols, share, span, num_vars, modes = dims
     takes = refs[:span]
-    phys_ref, one_ref, two_ref = refs[span:]
+    phys_ref, twin_ref, one_ref, two_ref = refs[span:]
     to_planes(dims, lax.axis_index("span"), high_ref, low_ref, takes, phys_ref)
     odd = lax.axis_index("elem") % 2 == 1
     lines = share // cols
     flip_x = facts_ref[2] > 0.5
     flip_y = facts_ref[3] > 0.5
     turn_x = sign(facts_ref[0]) * (1.0 - 2.0 * facts_ref[2])
+    second = lax.axis_index("span") % 2 == 1
+    turn_y = sign(facts_ref[1]) * (1.0 - 2.0 * facts_ref[3])
+    turn_y = jnp.where(second, -turn_y, turn_y)
+    inner = jnp.where(second, 1.0 - facts_ref[3], facts_ref[3]) > 0.5
+
+    def toward_twin(value):
+        return along({t: jnp.where(inner, value(t, 0), value(t, 5)) for t in range(SIDE)}, flip_x)
+
     for tile in range(span * modes // LANES):
         speed = sides_x(rim_reader(phys_ref, tile, 0), flip_x, flip_y)
+        pace = toward_twin(rim_reader(phys_ref, tile, 1))
+        pace = {t: 1.0 + turn_y * pace[t] for t in pace}
         for var in range(num_vars):
+            trace = toward_twin(rim_reader(phys_ref, tile, var))
+            for t in range(SIDE):
+                give = pace[t] * trace[t]
+                at = pl.ds(t * cols, cols)
+                twin_ref[tile, var, at, :] = jnp.where(second, give[:cols], give[share - cols :])
             trace = sides_x(rim_reader(phys_ref, tile, var), flip_x, flip_y)
             for t in range(SIDE):
                 low_x = (1.0 - turn_x * speed[0][t]) * trace[0][t]
@@ -353,10 +372,10 @@
 
 
 class Faces:
-    def __init__(self, dims, facts_ref, phys_ref, core_ref):
+    def __init__(self, dims, facts_ref, phys_ref, core_ref, twin_ref):
         cols, share, span, self.num_vars, modes = dims
         self.cols = cols
-        self.phys_ref, self.core_ref = phys_ref, core_ref
+        self.phys_ref, self.core_ref, self.twin_ref = phys_ref, core_ref, twin_ref
         me = lax.axis_index("span")
         slot = lax.broadcasted_iota(jnp.int32, (SUB, LANES), 0)
         self.slot = slot
@@ -370,6 +389,7 @@
         self.weight_y = 7.5 * jnp.abs(facts_ref[1])
         self.first_line = slot < cols
         self.turn_halo = jnp.where(self.first_line, self.turn_y, -self.turn_y)
+        self.far = slot // cols == me % 2
         self.floor = jnp.logical_and(self.first_line, me == 0)
         self.roof = jnp.logical_and(jnp.logical_not(self.first_line), me == span - 1)
 
@@ -399,19 +419,31 @@
         speed = sides_y(self.reader(tile, 1), self.flip_x, self.flip_y, wanted)
         return [{t: self.turn_y * side[t] for t in wanted} for side in speed]
 
-    def faces_y(self, tile, var, pace, wanted, total):
+    def twice(self, ref, tile, var, at):
+        row = ref[tile, var, pl.ds(at, self.cols), :]
+        return jnp.concatenate([row] * (SUB // self.cols), axis=0)
+
+    def far_row(self, tile, var, t):
+        return self.twice(self.phys_ref, tile, var, len(RIM_NODES) * SUB + t * self.cols)
+
+    def twin_row(self, tile, var, t):
+        return self.twice(self.twin_ref, tile, var, t * self.cols)
+
+    def far_pace(self, tile, wanted):
+        return {t: 1.0 + self.turn_halo * self.far_row(tile, 1, t) for t in wanted}
+
+    def faces_y(self, tile, var, pace, far_pace, wanted, total):
         mirror = 1.0 if var == self.num_vars - 1 else -1.0
         trace = sides_y(self.reader(tile, var), self.flip_x, self.flip_y, wanted)
         low, high = {}, {}
         for t in wanted:
-            at = pl.ds((len(RIM_NODES) + t) * SUB, SUB)
             speed, value = pace[0][t], trace[0][t]
             own_low, give_low = -(speed + 1.0) * value, (1.0 - speed) * value
             speed, value = pace[1][t], trace[1][t]
             own_high, give_high = (speed - 1.0) * value, (1.0 + speed) * value
-            outside = (1.0 + self.turn_halo * self.phys_ref[tile, 1, at, :]) * self.phys_ref[
-                tile, var, at, :
-            ]
+            outside = jnp.where(
+                self.far, far_pace[t] * self.far_row(tile, var, t), self.twin_row(tile, var, t)
+            )
             outside = jnp.where(self.floor, mirror * give_low, outside)
             outside = jnp.where(self.roof, mirror * give_high, outside)
             from_low = jnp.where(self.first_line, outside, pltpu.roll(give_high, self.cols, 0))
@@ -465,7 +497,7 @@
 
 
 def rates_kernel(
-    dims, facts_ref, there_high, there_low, high_ref, low_ref, phys_ref, *refs
+    dims, facts_ref, there_high, there_low, high_ref, low_ref, phys_ref, twin_ref, *refs
 ):
     _, share, span, num_vars, modes = dims
     half = span // 2
@@ -475,13 +507,13 @@
     me = lax.axis_index("span")
     to_planes(dims, me, there_high, there_low, takes, core_ref)
     count = span * modes
-    faces = Faces(dims, facts_ref, phys_ref, core_ref)
+    faces = Faces(dims, facts_ref, phys_ref, core_ref, twin_ref)
     wanted = tuple(range(1, SIDE - 1))
     for tile in range(count // LANES):
-        pace = faces.pace_y(tile, wanted)
+        pace, far_pace = faces.pace_y(tile, wanted), faces.far_pace(tile, wanted)
         for var in range(num_vars):
             total = faces.volume(tile, var, wanted)
-            faces.faces_y(tile, var, pace, wanted, total)
+            faces.faces_y(tile, var, pace, far_pace, wanted, total)
             q, w = faces.reader(tile, var), faces.reader(tile, 2)
             store_rates(rate_ref, MID_NODES, tile, var, count, total, q, w)
     parts = to_modes(dims, me, high_ref, low_ref, [rate_ref[var] for var in range(num_vars)])
@@ -490,17 +522,18 @@
 
 
 def edges_kernel(
-    dims, facts_ref, high_ref, low_ref, phys_ref, core_ref, one_ref, two_ref, *refs
+    dims, facts_ref, high_ref, low_ref, phys_ref, core_ref, twin_ref, one_ref, two_ref, *refs
 ):
     cols, share, span, num_vars, modes = dims
     odd_ref, *evens, rate_ref = refs
     count = span * modes
     lines = share // cols
     odd = lax.axis_index("elem") % 2 == 1
-    faces = Faces(dims, facts_ref, phys_ref, core_ref)
+    faces = Faces(dims, facts_ref, phys_ref, core_ref, twin_ref)
     wanted = (0, SIDE - 1)
     for tile in range(count // LANES):
         pace_x, pace_y = faces.pace_x(tile), faces.pace_y(tile, wanted)
+        far_pace = faces.far_pace(tile, wanted)
         for var in range(num_vars):
 
             def rim(t, tile=tile, var=var):
@@ -513,7 +546,7 @@
 
             total = faces.volume(tile, var, wanted)
             faces.faces_x(tile, var, pace_x, total, rim)
-            faces.faces_y(tile, var, pace_y, wanted, total)
+            faces.faces_y(tile, var, pace_y, far_pace, wanted, total)
             q, w = faces.reader(tile, var), faces.reader(tile, 2)
             store_rates(rate_ref, END_NODES, tile, var, count, total, q, w)
     me = lax.axis_index("span")
@@ -617,7 +650,7 @@
     f32 = jnp.float32
     mid_part, end_part, rim_part, core_part = (
         jax.ShapeDtypeStruct((nodes * share, LANES), f32)
-        for nodes in (len(MID_NODES), len(END_NODES), len(RIM_NODES) + SIDE, len(CORE_NODES))
+        for nodes in (len(MID_NODES), len(END_NODES), len(RIM_NODES) + SIDE // 2, len(CORE_NODES))
     )
     chunks = flat_size // CHUNK
     first = pl.pallas_call(
@@ -665,16 +698,18 @@
     planes = pl.pallas_call(
         functools.partial(planes_kernel, dims),
         out_shape=[
-            jax.ShapeDtypeStruct((tiles, num_vars, (len(RIM_NODES) + SIDE) * share, LANES), f32),
+            jax.ShapeDtypeStruct((tiles, num_vars, rim_part.shape[0], LANES), f32),
+            jax.ShapeDtypeStruct((tiles, num_vars, SIDE * cols, LANES), f32),
             line_shape,
             line_shape,
         ],
         in_specs=vmem(3 + span),
-        out_specs=vmem(3),
+        out_specs=vmem(4),
         compiler_params=PARAMS,
         name="planes",
     )
-    phys, one, two = planes(facts, *forward, *rim_takes)
+    phys, twin, one, two = planes(facts, *forward, *rim_takes)
+    twin = lax.ppermute(twin, "span", [(s, s ^ 1) for s in range(span)])
     one = lax.ppermute(one, "elem", [(g, g ^ 1) for g in range(groups)])
     two = lax.ppermute(
         two, "elem", [(g, (g - 1 if g % 2 == 0 else g + 1) % groups) for g in range(groups)]
@@ -684,25 +719,25 @@
         functools.partial(rates_kernel, dims),
         out_shape=[mid_part] * span
         + [jax.ShapeDtypeStruct((tiles, num_vars, len(CORE_NODES) * share, LANES), f32)],
-        in_specs=vmem(7 + span // 2),
+        in_specs=vmem(8 + span // 2),
         out_specs=vmem(span + 1),
         scratch_shapes=[pltpu.VMEM((num_vars, len(MID_NODES) * share, 2 * count), f32)],
         compiler_params=PARAMS,
         name="rates",
     )
-    *mids, core = rates(facts, *forward, *backward, phys, *core_takes)
+    *mids, core = rates(facts, *forward, *backward, phys, twin, *core_takes)
     mid_takes = exchange(mids, span)
     edges = pl.pallas_call(
         functools.partial(edges_kernel, dims),
         out_shape=[jax.ShapeDtypeStruct((span // 2 * end_part.shape[0], LANES), f32)]
         + [end_part] * (span // 2),
-        in_specs=vmem(7),
+        in_specs=vmem(8),
         out_specs=vmem(1 + span // 2),
         scratch_shapes=[pltpu.VMEM((num_vars, len(END_NODES) * share, 2 * count), f32)],
         compiler_params=PARAMS,
         name="edges",
     )
-    odds, *evens = edges(facts, *backward, phys, core, one, two)
+    odds, *evens = edges(facts, *backward, phys, core, twin, one, two)
     end_takes = relayed(odds, evens, span)
 
     dims = (rows, cols, share, span, modes)

time: 52.3 us -> 53.5 us (1.023)
  starting transfers between devices: 25 us -> 28.2 us
  waiting for transfers between devices: 17.5 us -> 15.6 us
    ppermute x14, starting transfers between devices: 12.6 us -> 15.7 us  [exchange(): lax.ppermute(blocks[k], 'span', [(s, s ^ k) for s in range(span)])]
    ppermute x1, waiting for transfers between devices: 1.36 us -> 0.01 us  [ordered_body(): lax.ppermute(two, 'elem', [(g, (g - 1 if g % 2 == 0 else g + 1) % groups)...]
    ppermute x14, waiting for transfers between devices: 11.1 us -> 9.82 us  [exchange(): lax.ppermute(blocks[k], 'span', [(s, s ^ k) for s in range(span)])]
    ppermute x6, waiting for transfers between devices: 5.06 us -> 5.75 us  [relayed(): both = lax.ppermute(both, 'span', [(s, s ^ 2 * at) for s in range(span)])]
  transfers between devices with their start and end apart: 24 -> 25, of which waited for: 7 -> 10; matrix products, arithmetic and copies ran while one was open for 0% -> 0% of each run, Pallas kernels for 7% -> 7%
where the time goes in v2:
time: 53.5 us; the launch traced here: 53.3 us
  starting transfers between devices  28.2 us (53%)
  waiting for transfers between devices  15.6 us (29%)
  Pallas kernels  9.29 us (17%)
    ppermute x14, starting transfers between devices, exchange(): lax.ppermute(blocks[k], 'span', [(s, s ^ k) for s in range(span)])  15.7 us
    ppermute x14, waiting for transfers between devices, exchange(): lax.ppermute(blocks[k], 'span', [(s, s ^ k) for s in range(span)])  9.82 us
    ppermute x6, starting transfers between devices, relayed(): both = lax.ppermute(both, 'span', [(s, s ^ 2 * at) for s in range(span)])  7.76 us
    ppermute x6, waiting for transfers between devices, relayed(): both = lax.ppermute(both, 'span', [(s, s ^ 2 * at) for s in range(span)])  5.75 us
    pallas_call x1, Pallas kernels, ordered_body(): pl.pallas_call(functools.partial(spread_kernel, (rows, cols, share, span)...  2.74 us
    ppermute x1, starting transfers between devices, ordered_body(): lax.ppermute(two, 'elem', [(g, (g - 1 if g % 2 == 0 else g + 1) % groups)...  2.46 us
    pallas_call x1, Pallas kernels, ordered_body(): *mids, core = rates(facts, *forward, *backward, phys, twin, *core_takes)  2.44 us
    ppermute x1, starting transfers between devices, ordered_body(): one = lax.ppermute(one, 'elem', [(g, g ^ 1) for g in range(groups)])  1.58 us
  transfers between devices with their start and end apart: 25, of which 10 were waited for; matrix products, arithmetic and copies ran while one was open for 0% of the time, Pallas kernels for 7%

profile of v2, /device:TPU:0, one launch (start us, length us, event | category | flops | bytes accessed | tf_op | source)
XLA Modules:
  0.0 53.3 jit_solution(11361341579882934136)
XLA Ops:
  0.0 0.0 copy-start.3
  0.0 2.7 %spread.1 = (f32[184,128]{1,0:T(8,128)S(1)}, f32[184,128]{1,0:T(8,128)S(1)}, f32[184,128]{1,0:T(8,128)S(1)}, f32[184,128]{1,0:T(8,128)S(1)}, f32[184,128]{1,0:T(...) custom-call(s32[4,64]{1,0:T(4,128)} %bitcast.6, ...), custom_call_target="tpu_custom_call" | custom-call | tf_op jit(solution)/shard_map/spread/pallas_call | solution.py:656
  2.8 0.2 spread_core.1
  3.0 0.6 %collective-permute-start.8 = (f32[512,128]{1,0:T(8,128)S(1)}, f32[512,128]{1,0:T(8,128)S(1)}, u32[]{:S(2)}, u32[]{:S(2)}) collective-permute-start(f32[512,128]{1,0:T(8,128)S(1)} %get-tuple-element.54), channel_id=1, source_target_pairs={{0,1},{1,0},{2,3},{3,2},{4,5},{5,4},{6,7},{7,6},{8,9},{9,8},{10,11... | collective-permute-start | bytes 786440 | tf_op jit(solution)/shard_map/ppermute | solution.py:629
  3.5 0.1 collective-permute-start
  3.6 2.9 %collective-permute-start.1 = (f32[184,128]{1,0:T(8,128)S(1)}, f32[184,128]{1,0:T(8,128)S(1)}, u32[]{:S(2)}, u32[]{:S(2)}) collective-permute-start(f32[184,128]{1,0:T(8,128)S(1)} %get-tuple-element.44), channel_id=1, source_target_pairs={{0,2},{1,3},{2,0},{3,1},{4,6},{5,7},{6,4},{7,5},{8,10},{9,11},{10,... | collective-permute-start | bytes 282632 | tf_op jit(solution)/shard_map/ppermute | solution.py:623
  6.5 0.0 collective-permute-start.2
  6.5 1.5 %collective-permute-start.3 = (f32[184,128]{1,0:T(8,128)S(1)}, f32[184,128]{1,0:T(8,128)S(1)}, u32[]{:S(2)}, u32[]{:S(2)}) collective-permute-start(f32[184,128]{1,0:T(8,128)S(1)} %get-tuple-element.46), channel_id=1, source_target_pairs={{0,4},{1,5},{2,6},{3,7},{4,0},{5,1},{6,2},{7,3},{8,12},{9,13},{10,... | collective-permute-start | bytes 282632 | tf_op jit(solution)/shard_map/ppermute | solution.py:623
  8.0 0.0 collective-permute-done.refs_1_
  8.0 0.2 collective-permute-start.4
  8.3 1.3 %collective-permute-done.1.refs_2_ = f32[184,128]{1,0:T(8,128)S(1)} collective-permute-done((f32[184,128]{1,0:T(8,128)S(1)}, f32[184,128]{1,0:T(8,128)S(1)}, u32[]{:S(2)}, u32[]{:S(2)}) %collective-permute-start.1) | collective-permute-done | bytes 94240 | tf_op jit(solution)/shard_map/ppermute | solution.py:623
  9.6 3.4 %collective-permute-start.5 = (f32[184,128]{1,0:T(8,128)S(1)}, f32[184,128]{1,0:T(8,128)S(1)}, u32[]{:S(2)}, u32[]{:S(2)}) collective-permute-start(f32[184,128]{1,0:T(8,128)S(1)} %get-tuple-element.48), channel_id=1, source_target_pairs={{0,6},{1,7},{2,4},{3,5},{4,2},{5,3},{6,0},{7,1},{8,14},{9,15},{10,... | collective-permute-start | bytes 282632 | tf_op jit(solution)/shard_map/ppermute | solution.py:623
  13.1 0.0 collective-permute-done.2.refs_3_
  13.1 1.1 %collective-permute-start.6 = (f32[184,128]{1,0:T(8,128)S(1)}, f32[184,128]{1,0:T(8,128)S(1)}, u32[]{:S(2)}, u32[]{:S(2)}) collective-permute-start(f32[184,128]{1,0:T(8,128)S(1)} %get-tuple-element.49), channel_id=1, source_target_pairs={{0,7},{1,6},{2,5},{3,4},{4,3},{5,2},{6,1},{7,0},{8,15},{9,14},{10,... | collective-permute-start | bytes 282632 | tf_op jit(solution)/shard_map/ppermute | solution.py:623
  14.2 0.0 collective-permute-done.3.refs_4_
  14.2 0.7 %collective-permute-done.4.refs_5_ = f32[184,128]{1,0:T(8,128)S(1)} collective-permute-done((f32[184,128]{1,0:T(8,128)S(1)}, f32[184,128]{1,0:T(8,128)S(1)}, u32[]{:S(2)}, u32[]{:S(2)}) %collective-permute-start.4) | collective-permute-done | bytes 94240 | tf_op jit(solution)/shard_map/ppermute | solution.py:623
  14.9 1.0 %collective-permute-done.5.refs_6_ = f32[184,128]{1,0:T(8,128)S(1)} collective-permute-done((f32[184,128]{1,0:T(8,128)S(1)}, f32[184,128]{1,0:T(8,128)S(1)}, u32[]{:S(2)}, u32[]{:S(2)}) %collective-permute-start.5) | collective-permute-done | bytes 94240 | tf_op jit(solution)/shard_map/ppermute | solution.py:623
  15.8 2.1 %collective-permute-done.6.refs_7_ = f32[184,128]{1,0:T(8,128)S(1)} collective-permute-done((f32[184,128]{1,0:T(8,128)S(1)}, f32[184,128]{1,0:T(8,128)S(1)}, u32[]{:S(2)}, u32[]{:S(2)}) %collective-permute-start.6) | collective-permute-done | bytes 94240 | tf_op jit(solution)/shard_map/ppermute | solution.py:623
  18.0 0.0 copy-done.3
  18.0 0.0 copy-done.4
  18.0 0.8 %planes.1 = (f32[2,4,184,128]{3,2,1,0:T(8,128)S(1)}, f32[2,4,24,128]{3,2,1,0:T(8,128)S(1)}, f32[2,4,12,128]{3,2,1,0:T(8,128)S(1)}, f32[2,4,12,128]{3,2,1,0:T(8,128)S(1)}) custom-call(f32[4,8,128]{2,1,0:T(8,128)S(1)} %get-tuple-element.41.facts_ref, bf16[256,256]{1,0:T(8,128)(2,1)S(1)} %copy-done.4, bf16[256,256]{1,0:T(8,128)(2,1)S(1)} %copy-done.3, ...), custom_call_target="tpu_custom_call" | custom-call | tf_op jit(solution)/shard_map/planes/pallas_call | solution.py:711
  18.7 0.1 collective-permute-start.7
  18.8 0.0 collective-permute-done.8
  18.9 1.5 %collective-permute-start.9 = (f32[256,128]{1,0:T(8,128)S(1)}, f32[256,128]{1,0:T(8,128)S(1)}, u32[]{:S(2)}, u32[]{:S(2)}) collective-permute-start(f32[256,128]{1,0:T(8,128)S(1)} %pad_maximum_fusion), channel_id=1, source_target_pairs={{0,2},{1,3},{2,0},{3,1},{4,6},{5,7},{6,4},{7,5},{8,10},{9,11},{10,... | collective-permute-start | bytes 393224 | tf_op jit(solution)/shard_map/ppermute | solution.py:633
  20.4 1.3 %collective-permute-start.10 = (f32[256,128]{1,0:T(8,128)S(1)}, f32[256,128]{1,0:T(8,128)S(1)}, u32[]{:S(2)}, u32[]{:S(2)}) collective-permute-start(f32[256,128]{1,0:T(8,128)S(1)} %pad_maximum_fusion.1), channel_id=1, source_target_pairs={{0,4},{1,5},{2,6},{3,7},{4,0},{5,1},{6,2},{7,3},{8,12},{9,13},{10,... | collective-permute-start | bytes 393224 | tf_op jit(solution)/shard_map/ppermute | solution.py:633
  21.7 0.9 %collective-permute-start.11 = (f32[256,128]{1,0:T(8,128)S(1)}, f32[256,128]{1,0:T(8,128)S(1)}, u32[]{:S(2)}, u32[]{:S(2)}) collective-permute-start(f32[256,128]{1,0:T(8,128)S(1)} %pad_maximum_fusion.2), channel_id=1, source_target_pairs={{0,6},{1,7},{2,4},{3,5},{4,2},{5,3},{6,0},{7,1},{8,14},{9,15},{10,... | collective-permute-start | bytes 393224 | tf_op jit(solution)/shard_map/ppermute | solution.py:633
  22.6 1.6 %collective-permute-start.19 = (f32[2,4,12,128]{3,2,1,0:T(8,128)S(1)}, f32[2,4,12,128]{3,2,1,0:T(8,128)S(1)}, u32[]{:S(2)}, u32[]{:S(2)}) collective-permute-start(f32[2,4,12,128]{3,2,1,0:T(8,128)S(1)} %get-tuple-element.67), channel_id=1, source_target_pairs={{0,8},{8,0},{16,24},{24,16},{1,9},{9,1},{17,25},{25,17},{2,10},{10... | collective-permute-start | bytes 147464 | tf_op jit(solution)/shard_map/ppermute | solution.py:713
  24.2 0.0 collective-permute-done.7.twin_ref
  24.2 2.5 %collective-permute-start.20 = (f32[2,4,12,128]{3,2,1,0:T(8,128)S(1)}, f32[2,4,12,128]{3,2,1,0:T(8,128)S(1)}, u32[]{:S(2)}, u32[]{:S(2)}) collective-permute-start(f32[2,4,12,128]{3,2,1,0:T(8,128)S(1)} %get-tuple-element.68), channel_id=1, source_target_pairs={{0,24},{8,16},{16,8},{24,0},{1,25},{9,17},{17,9},{25,1},{2,26},{10... | collective-permute-start | bytes 147464 | tf_op jit(solution)/shard_map/ppermute | solution.py:714
  26.6 0.0 collective-permute-done.9.refs_2_
  26.6 0.6 %collective-permute-done.10.refs_3_ = f32[256,128]{1,0:T(8,128)S(1)} collective-permute-done((f32[256,128]{1,0:T(8,128)S(1)}, f32[256,128]{1,0:T(8,128)S(1)}, u32[]{:S(2)}, u32[]{:S(2)}) %collective-permute-start.10) | collective-permute-done | bytes 131104 | tf_op jit(solution)/shard_map/ppermute | solution.py:633
  27.2 1.2 %collective-permute-done.11.refs_4_ = f32[256,128]{1,0:T(8,128)S(1)} collective-permute-done((f32[256,128]{1,0:T(8,128)S(1)}, f32[256,128]{1,0:T(8,128)S(1)}, u32[]{:S(2)}, u32[]{:S(2)}) %collective-permute-start.11) | collective-permute-done | bytes 131104 | tf_op jit(solution)/shard_map/ppermute | solution.py:633
  28.4 0.0 copy-done.1
  28.4 0.0 copy-done.2
  28.4 2.4 %rates.1 = (f32[192,128]{1,0:T(8,128)S(1)}, f32[192,128]{1,0:T(8,128)S(1)}, f32[192,128]{1,0:T(8,128)S(1)}, f32[192,128]{1,0:T(8,128)S(1)}, f32[192,128]{1,0:T(8...) custom-call(f32[4,8,128]{2,1,0:T(8,128)S(1)} %get-tuple-element.41.f, ...), custom_call_target="tpu_custom_call" | custom-call | tf_op jit(solution)/shard_map/rates/pallas_call | solution.py:728
  30.9 0.0 collective-permute-done.19.one_ref
  30.9 0.0 collective-permute-done.20.two_ref
  30.9 1.2 %edges.1 = (f32[384,128]{1,0:T(8,128)S(1)}, f32[96,128]{1,0:T(8,128)S(1)}, f32[96,128]{1,0:T(8,128)S(1)}, f32[96,128]{1,0:T(8,128)S(1)}, f32[96,128]{1,0:T(8,128)S(1)}) custom-call(f32[4,8,128]{2,1,0:T(8,128)S(1)} %get-tuple-element.41.facts_ref, bf16[256,512]{1,0:T(8,128)(2,1)S(1)} %copy-done.2, bf16[256,512]{1,0:T(8,128)(2,1)S(1)} %copy-done.1, ...), custom_call_target="tpu_custom_call" | custom-call | tf_op jit(solution)/shard_map/edges/pallas_call | solution.py:740
  32.1 0.1 collective-permute-start.21
  32.2 0.5 collective-permute-start.12
  32.7 1.1 %collective-permute-start.13 = (f32[192,128]{1,0:T(8,128)S(1)}, f32[192,128]{1,0:T(8,128)S(1)}, u32[]{:S(2)}, u32[]{:S(2)}) collective-permute-start(f32[192,128]{1,0:T(8,128)S(1)} %get-tuple-element.60), channel_id=1, source_target_pairs={{0,2},{1,3},{2,0},{3,1},{4,6},{5,7},{6,4},{7,5},{8,10},{9,11},{10,... | collective-permute-start | bytes 294920 | tf_op jit(solution)/shard_map/ppermute | solution.py:623
  33.7 0.4 collective-permute-start.14
  34.1 1.3 %collective-permute-start.15 = (f32[192,128]{1,0:T(8,128)S(1)}, f32[192,128]{1,0:T(8,128)S(1)}, u32[]{:S(2)}, u32[]{:S(2)}) collective-permute-start(f32[192,128]{1,0:T(8,128)S(1)} %get-tuple-element.62), channel_id=1, source_target_pairs={{0,4},{1,5},{2,6},{3,7},{4,0},{5,1},{6,2},{7,3},{8,12},{9,13},{10,... | collective-permute-start | bytes 294920 | tf_op jit(solution)/shard_map/ppermute | solution.py:623
  35.4 0.0 collective-permute-done.21
  35.4 0.8 %collective-permute-start.16 = (f32[192,128]{1,0:T(8,128)S(1)}, f32[192,128]{1,0:T(8,128)S(1)}, u32[]{:S(2)}, u32[]{:S(2)}) collective-permute-start(f32[192,128]{1,0:T(8,128)S(1)} %get-tuple-element.63), channel_id=1, source_target_pairs={{0,5},{1,4},{2,7},{3,6},{4,1},{5,0},{6,3},{7,2},{8,13},{9,12},{10,... | collective-permute-start | bytes 294920 | tf_op jit(solution)/shard_map/ppermute | solution.py:623
  36.2 0.0 copy-start
  36.2 0.0 collective-permute-done.12.refs_1_
  36.3 1.9 %collective-permute-start.17 = (f32[192,128]{1,0:T(8,128)S(1)}, f32[192,128]{1,0:T(8,128)S(1)}, u32[]{:S(2)}, u32[]{:S(2)}) collective-permute-start(f32[192,128]{1,0:T(8,128)S(1)} %get-tuple-element.64), channel_id=1, source_target_pairs={{0,6},{1,7},{2,4},{3,5},{4,2},{5,3},{6,0},{7,1},{8,14},{9,15},{10,... | collective-permute-start | bytes 294920 | tf_op jit(solution)/shard_map/ppermute | solution.py:623
  38.2 0.0 collective-permute-done.13.refs_2_
  38.2 0.5 collective-permute-start.18
  38.7 0.2 collective-permute-done.14.refs_3_
  38.8 1.0 %collective-permute-start.22 = (f32[192,128]{1,0:T(8,128)S(1)}, f32[192,128]{1,0:T(8,128)S(1)}, u32[]{:S(2)}, u32[]{:S(2)}) collective-permute-start(f32[192,128]{1,0:T(8,128)S(1)} %pad_maximum_fusion.3), channel_id=1, source_target_pairs={{0,2},{1,3},{2,0},{3,1},{4,6},{5,7},{6,4},{7,5},{8,10},{9,11},{10,... | collective-permute-start | bytes 294920 | tf_op jit(solution)/shard_map/ppermute | solution.py:633
  39.8 0.0 collective-permute-done.15.refs_4_
  39.8 1.3 %collective-permute-start.23 = (f32[192,128]{1,0:T(8,128)S(1)}, f32[192,128]{1,0:T(8,128)S(1)}, u32[]{:S(2)}, u32[]{:S(2)}) collective-permute-start(f32[192,128]{1,0:T(8,128)S(1)} %pad_maximum_fusion.4), channel_id=1, source_target_pairs={{0,4},{1,5},{2,6},{3,7},{4,0},{5,1},{6,2},{7,3},{8,12},{9,13},{10,... | collective-permute-start | bytes 294920 | tf_op jit(solution)/shard_map/ppermute | solution.py:633
  41.1 4.5 %collective-permute-done.16.refs_5_ = f32[192,128]{1,0:T(8,128)S(1)} collective-permute-done((f32[192,128]{1,0:T(8,128)S(1)}, f32[192,128]{1,0:T(8,128)S(1)}, u32[]{:S(2)}, u32[]{:S(2)}) %collective-permute-start.16) | collective-permute-done | bytes 98336 | tf_op jit(solution)/shard_map/ppermute | solution.py:623
  45.6 1.8 %collective-permute-start.24 = (f32[192,128]{1,0:T(8,128)S(1)}, f32[192,128]{1,0:T(8,128)S(1)}, u32[]{:S(2)}, u32[]{:S(2)}) collective-permute-start(f32[192,128]{1,0:T(8,128)S(1)} %pad_maximum_fusion.5), channel_id=1, source_target_pairs={{0,6},{1,7},{2,4},{3,5},{4,2},{5,3},{6,0},{7,1},{8,14},{9,15},{10,... | collective-permute-start | bytes 294920 | tf_op jit(solution)/shard_map/ppermute | solution.py:633
  47.4 0.0 collective-permute-done.17.refs_6_
  47.4 0.0 collective-permute-done.18.refs_7_
  47.4 0.4 collect.1.flat_in
  47.8 0.0 collective-permute-done.22.refs_2_
  47.8 0.1 collective-permute-done.23.refs_3_
  47.9 3.8 %collective-permute-done.24.refs_4_ = f32[192,128]{1,0:T(8,128)S(1)} collective-permute-done((f32[192,128]{1,0:T(8,128)S(1)}, f32[192,128]{1,0:T(8,128)S(1)}, u32[]{:S(2)}, u32[]{:S(2)}) %collective-permute-start.24) | collective-permute-done | bytes 98336 | tf_op jit(solution)/shard_map/ppermute | solution.py:633
  51.8 0.0 copy-done
  51.8 1.6 %finish.1 = (f32[128,2304]{1,0:T(8,128)}, f32[2304,128]{1,0:T(8,128)S(1)}) custom-call(f32[64,128]{1,0:T(8,128)S(1)} %get-tuple-element.40.pick_ref, f32[128,2304]{1,0:T(8,128)S(1)} %bitcast.5, f32[2304,128]{1,0:T(8,128)S(1)} %collect.1.flat_in, f32[96,128]{1,0:T(8,128)S(1)} %get-tuple-element.69.refs_0_, ...), custom_call_target="tpu_custom_call", output_to_operand_aliasing={{1}: (2, {})} | custom-call | tf_op jit(solution)/shard_map/finish/pallas_call | solution.py:754
  (11 shorter events, 0.1 us)
Async XLA Ops:
  0.0 18.0 %copy-start.3 = (bf16[256,256]{1,0:T(8,128)(2,1)S(1)}, bf16[256,256]{1,0:T(8,128)(2,1)}, u32[]{:S(2)}) copy-start(bf16[256,256]{1,0:T(8,128)(2,1)} %constant.9.clone.low_ref.there_low) | copy-start | bytes 393220
  0.0 18.0 %copy-start.4 = (bf16[256,256]{1,0:T(8,128)(2,1)S(1)}, bf16[256,256]{1,0:T(8,128)(2,1)}, u32[]{:S(2)}) copy-start(bf16[256,256]{1,0:T(8,128)(2,1)} %constant.8.clone.high_ref.there_high) | copy-start | bytes 393220
  3.0 15.8 %collective-permute-start.8 = (f32[512,128]{1,0:T(8,128)S(1)}, f32[512,128]{1,0:T(8,128)S(1)}, u32[]{:S(2)}, u32[]{:S(2)}) collective-permute-start(f32[512,128]{1,0:T(8,128)S(1)} %get-tuple-element.54), channel_id=1, source_target_pairs={{0,1},{1,0},{2,3},{3,2},{4,5},{5,4},{6,7},{7,6},{8,9},{9,8},{10,11... | collective-permute-start | bytes 786440 | tf_op jit(solution)/shard_map/ppermute | solution.py:629
  3.5 4.5 %collective-permute-start = (f32[184,128]{1,0:T(8,128)S(1)}, f32[184,128]{1,0:T(8,128)S(1)}, u32[]{:S(2)}, u32[]{:S(2)}) collective-permute-start(f32[184,128]{1,0:T(8,128)S(1)} %get-tuple-element.43), channel_id=1, source_target_pairs={{0,1},{1,0},{2,3},{3,2},{4,5},{5,4},{6,7},{7,6},{8,9},{9,8},{10,11... | collective-permute-start | bytes 282632 | tf_op jit(solution)/shard_map/ppermute | solution.py:623
  3.6 6.0 %collective-permute-start.1 = (f32[184,128]{1,0:T(8,128)S(1)}, f32[184,128]{1,0:T(8,128)S(1)}, u32[]{:S(2)}, u32[]{:S(2)}) collective-permute-start(f32[184,128]{1,0:T(8,128)S(1)} %get-tuple-element.44), channel_id=1, source_target_pairs={{0,2},{1,3},{2,0},{3,1},{4,6},{5,7},{6,4},{7,5},{8,10},{9,11},{10,... | collective-permute-start | bytes 282632 | tf_op jit(solution)/shard_map/ppermute | solution.py:623
  6.5 6.5 %collective-permute-start.2 = (f32[184,128]{1,0:T(8,128)S(1)}, f32[184,128]{1,0:T(8,128)S(1)}, u32[]{:S(2)}, u32[]{:S(2)}) collective-permute-start(f32[184,128]{1,0:T(8,128)S(1)} %get-tuple-element.45), channel_id=1, source_target_pairs={{0,3},{1,2},{2,1},{3,0},{4,7},{5,6},{6,5},{7,4},{8,11},{9,10},{10,... | collective-permute-start | bytes 282632 | tf_op jit(solution)/shard_map/ppermute | solution.py:623
  6.5 7.6 %collective-permute-start.3 = (f32[184,128]{1,0:T(8,128)S(1)}, f32[184,128]{1,0:T(8,128)S(1)}, u32[]{:S(2)}, u32[]{:S(2)}) collective-permute-start(f32[184,128]{1,0:T(8,128)S(1)} %get-tuple-element.46), channel_id=1, source_target_pairs={{0,4},{1,5},{2,6},{3,7},{4,0},{5,1},{6,2},{7,3},{8,12},{9,13},{10,... | collective-permute-start | bytes 282632 | tf_op jit(solution)/shard_map/ppermute | solution.py:623
  8.0 6.8 %collective-permute-start.4 = (f32[184,128]{1,0:T(8,128)S(1)}, f32[184,128]{1,0:T(8,128)S(1)}, u32[]{:S(2)}, u32[]{:S(2)}) collective-permute-start(f32[184,128]{1,0:T(8,128)S(1)} %get-tuple-element.47), channel_id=1, source_target_pairs={{0,5},{1,4},{2,7},{3,6},{4,1},{5,0},{6,3},{7,2},{8,13},{9,12},{10,... | collective-permute-start | bytes 282632 | tf_op jit(solution)/shard_map/ppermute | solution.py:623
  9.6 6.2 %collective-permute-start.5 = (f32[184,128]{1,0:T(8,128)S(1)}, f32[184,128]{1,0:T(8,128)S(1)}, u32[]{:S(2)}, u32[]{:S(2)}) collective-permute-start(f32[184,128]{1,0:T(8,128)S(1)} %get-tuple-element.48), channel_id=1, source_target_pairs={{0,6},{1,7},{2,4},{3,5},{4,2},{5,3},{6,0},{7,1},{8,14},{9,15},{10,... | collective-permute-start | bytes 282632 | tf_op jit(solution)/shard_map/ppermute | solution.py:623
  13.1 4.9 %collective-permute-start.6 = (f32[184,128]{1,0:T(8,128)S(1)}, f32[184,128]{1,0:T(8,128)S(1)}, u32[]{:S(2)}, u32[]{:S(2)}) collective-permute-start(f32[184,128]{1,0:T(8,128)S(1)} %get-tuple-element.49), channel_id=1, source_target_pairs={{0,7},{1,6},{2,5},{3,4},{4,3},{5,2},{6,1},{7,0},{8,15},{9,14},{10,... | collective-permute-start | bytes 282632 | tf_op jit(solution)/shard_map/ppermute | solution.py:623
  18.0 10.5 %copy-start.1 = (bf16[256,512]{1,0:T(8,128)(2,1)S(1)}, bf16[256,512]{1,0:T(8,128)(2,1)}, u32[]{:S(2)}) copy-start(bf16[256,512]{1,0:T(8,128)(2,1)} %constant.11.clone.low_ref) | copy-start | bytes 786436
  18.0 10.5 %copy-start.2 = (bf16[256,512]{1,0:T(8,128)(2,1)S(1)}, bf16[256,512]{1,0:T(8,128)(2,1)}, u32[]{:S(2)}) copy-start(bf16[256,512]{1,0:T(8,128)(2,1)} %constant.10.clone.high_ref) | copy-start | bytes 786436
  18.7 5.4 %collective-permute-start.7 = (f32[2,4,24,128]{3,2,1,0:T(8,128)S(1)}, f32[2,4,24,128]{3,2,1,0:T(8,128)S(1)}, u32[]{:S(2)}, u32[]{:S(2)}) collective-permute-start(f32[2,4,24,128]{3,2,1,0:T(8,128)S(1)} %get-tuple-element.51), channel_id=1, source_target_pairs={{0,1},{1,0},{2,3},{3,2},{4,5},{5,4},{6,7},{7,6},{8,9},{9,8},{10,11... | collective-permute-start | bytes 294920 | tf_op jit(solution)/shard_map/ppermute | solution.py:712
  18.9 7.8 %collective-permute-start.9 = (f32[256,128]{1,0:T(8,128)S(1)}, f32[256,128]{1,0:T(8,128)S(1)}, u32[]{:S(2)}, u32[]{:S(2)}) collective-permute-start(f32[256,128]{1,0:T(8,128)S(1)} %pad_maximum_fusion), channel_id=1, source_target_pairs={{0,2},{1,3},{2,0},{3,1},{4,6},{5,7},{6,4},{7,5},{8,10},{9,11},{10,... | collective-permute-start | bytes 393224 | tf_op jit(solution)/shard_map/ppermute | solution.py:633
  20.4 6.8 %collective-permute-start.10 = (f32[256,128]{1,0:T(8,128)S(1)}, f32[256,128]{1,0:T(8,128)S(1)}, u32[]{:S(2)}, u32[]{:S(2)}) collective-permute-start(f32[256,128]{1,0:T(8,128)S(1)} %pad_maximum_fusion.1), channel_id=1, source_target_pairs={{0,4},{1,5},{2,6},{3,7},{4,0},{5,1},{6,2},{7,3},{8,12},{9,13},{10,... | collective-permute-start | bytes 393224 | tf_op jit(solution)/shard_map/ppermute | solution.py:633
  21.7 6.7 %collective-permute-start.11 = (f32[256,128]{1,0:T(8,128)S(1)}, f32[256,128]{1,0:T(8,128)S(1)}, u32[]{:S(2)}, u32[]{:S(2)}) collective-permute-start(f32[256,128]{1,0:T(8,128)S(1)} %pad_maximum_fusion.2), channel_id=1, source_target_pairs={{0,6},{1,7},{2,4},{3,5},{4,2},{5,3},{6,0},{7,1},{8,14},{9,15},{10,... | collective-permute-start | bytes 393224 | tf_op jit(solution)/shard_map/ppermute | solution.py:633
  22.6 8.3 %collective-permute-start.19 = (f32[2,4,12,128]{3,2,1,0:T(8,128)S(1)}, f32[2,4,12,128]{3,2,1,0:T(8,128)S(1)}, u32[]{:S(2)}, u32[]{:S(2)}) collective-permute-start(f32[2,4,12,128]{3,2,1,0:T(8,128)S(1)} %get-tuple-element.67), channel_id=1, source_target_pairs={{0,8},{8,0},{16,24},{24,16},{1,9},{9,1},{17,25},{25,17},{2,10},{10... | collective-permute-start | bytes 147464 | tf_op jit(solution)/shard_map/ppermute | solution.py:713
  24.2 6.7 %collective-permute-start.20 = (f32[2,4,12,128]{3,2,1,0:T(8,128)S(1)}, f32[2,4,12,128]{3,2,1,0:T(8,128)S(1)}, u32[]{:S(2)}, u32[]{:S(2)}) collective-permute-start(f32[2,4,12,128]{3,2,1,0:T(8,128)S(1)} %get-tuple-element.68), channel_id=1, source_target_pairs={{0,24},{8,16},{16,8},{24,0},{1,25},{9,17},{17,9},{25,1},{2,26},{10... | collective-permute-start | bytes 147464 | tf_op jit(solution)/shard_map/ppermute | solution.py:714
  32.1 3.3 %collective-permute-start.21 = (f32[384,128]{1,0:T(8,128)S(1)}, f32[384,128]{1,0:T(8,128)S(1)}, u32[]{:S(2)}, u32[]{:S(2)}) collective-permute-start(f32[384,128]{1,0:T(8,128)S(1)} %get-tuple-element.70), channel_id=1, source_target_pairs={{0,1},{1,0},{2,3},{3,2},{4,5},{5,4},{6,7},{7,6},{8,9},{9,8},{10,11... | collective-permute-start | bytes 589832 | tf_op jit(solution)/shard_map/ppermute | solution.py:629
  32.2 4.1 %collective-permute-start.12 = (f32[192,128]{1,0:T(8,128)S(1)}, f32[192,128]{1,0:T(8,128)S(1)}, u32[]{:S(2)}, u32[]{:S(2)}) collective-permute-start(f32[192,128]{1,0:T(8,128)S(1)} %get-tuple-element.59), channel_id=1, source_target_pairs={{0,1},{1,0},{2,3},{3,2},{4,5},{5,4},{6,7},{7,6},{8,9},{9,8},{10,11... | collective-permute-start | bytes 294920 | tf_op jit(solution)/shard_map/ppermute | solution.py:623
  32.7 5.5 %collective-permute-start.13 = (f32[192,128]{1,0:T(8,128)S(1)}, f32[192,128]{1,0:T(8,128)S(1)}, u32[]{:S(2)}, u32[]{:S(2)}) collective-permute-start(f32[192,128]{1,0:T(8,128)S(1)} %get-tuple-element.60), channel_id=1, source_target_pairs={{0,2},{1,3},{2,0},{3,1},{4,6},{5,7},{6,4},{7,5},{8,10},{9,11},{10,... | collective-permute-start | bytes 294920 | tf_op jit(solution)/shard_map/ppermute | solution.py:623
  33.7 5.1 %collective-permute-start.14 = (f32[192,128]{1,0:T(8,128)S(1)}, f32[192,128]{1,0:T(8,128)S(1)}, u32[]{:S(2)}, u32[]{:S(2)}) collective-permute-start(f32[192,128]{1,0:T(8,128)S(1)} %get-tuple-element.61), channel_id=1, source_target_pairs={{0,3},{1,2},{2,1},{3,0},{4,7},{5,6},{6,5},{7,4},{8,11},{9,10},{10,... | collective-permute-start | bytes 294920 | tf_op jit(solution)/shard_map/ppermute | solution.py:623
  34.1 5.7 %collective-permute-start.15 = (f32[192,128]{1,0:T(8,128)S(1)}, f32[192,128]{1,0:T(8,128)S(1)}, u32[]{:S(2)}, u32[]{:S(2)}) collective-permute-start(f32[192,128]{1,0:T(8,128)S(1)} %get-tuple-element.62), channel_id=1, source_target_pairs={{0,4},{1,5},{2,6},{3,7},{4,0},{5,1},{6,2},{7,3},{8,12},{9,13},{10,... | collective-permute-start | bytes 294920 | tf_op jit(solution)/shard_map/ppermute | solution.py:623
  35.4 10.2 %collective-permute-start.16 = (f32[192,128]{1,0:T(8,128)S(1)}, f32[192,128]{1,0:T(8,128)S(1)}, u32[]{:S(2)}, u32[]{:S(2)}) collective-permute-start(f32[192,128]{1,0:T(8,128)S(1)} %get-tuple-element.63), channel_id=1, source_target_pairs={{0,5},{1,4},{2,7},{3,6},{4,1},{5,0},{6,3},{7,2},{8,13},{9,12},{10,... | collective-permute-start | bytes 294920 | tf_op jit(solution)/shard_map/ppermute | solution.py:623
  36.2 15.6 %copy-start = (f32[4,32,2304]{2,1,0:T(8,128)S(1)}, f32[4,32,2304]{2,1,0:T(8,128)}, u32[]{:S(2)}) copy-start(f32[4,32,2304]{2,1,0:T(8,128)} %param.10) | copy-start | bytes 3538948
  36.3 11.2 %collective-permute-start.17 = (f32[192,128]{1,0:T(8,128)S(1)}, f32[192,128]{1,0:T(8,128)S(1)}, u32[]{:S(2)}, u32[]{:S(2)}) collective-permute-start(f32[192,128]{1,0:T(8,128)S(1)} %get-tuple-element.64), channel_id=1, source_target_pairs={{0,6},{1,7},{2,4},{3,5},{4,2},{5,3},{6,0},{7,1},{8,14},{9,15},{10,... | collective-permute-start | bytes 294920 | tf_op jit(solution)/shard_map/ppermute | solution.py:623
  38.2 9.2 %collective-permute-start.18 = (f32[192,128]{1,0:T(8,128)S(1)}, f32[192,128]{1,0:T(8,128)S(1)}, u32[]{:S(2)}, u32[]{:S(2)}) collective-permute-start(f32[192,128]{1,0:T(8,128)S(1)} %get-tuple-element.65), channel_id=1, source_target_pairs={{0,7},{1,6},{2,5},{3,4},{4,3},{5,2},{6,1},{7,0},{8,15},{9,14},{10,... | collective-permute-start | bytes 294920 | tf_op jit(solution)/shard_map/ppermute | solution.py:623
  38.8 9.0 %collective-permute-start.22 = (f32[192,128]{1,0:T(8,128)S(1)}, f32[192,128]{1,0:T(8,128)S(1)}, u32[]{:S(2)}, u32[]{:S(2)}) collective-permute-start(f32[192,128]{1,0:T(8,128)S(1)} %pad_maximum_fusion.3), channel_id=1, source_target_pairs={{0,2},{1,3},{2,0},{3,1},{4,6},{5,7},{6,4},{7,5},{8,10},{9,11},{10,... | collective-permute-start | bytes 294920 | tf_op jit(solution)/shard_map/ppermute | solution.py:633
  39.8 8.1 %collective-permute-start.23 = (f32[192,128]{1,0:T(8,128)S(1)}, f32[192,128]{1,0:T(8,128)S(1)}, u32[]{:S(2)}, u32[]{:S(2)}) collective-permute-start(f32[192,128]{1,0:T(8,128)S(1)} %pad_maximum_fusion.4), channel_id=1, source_target_pairs={{0,4},{1,5},{2,6},{3,7},{4,0},{5,1},{6,2},{7,3},{8,12},{9,13},{10,... | collective-permute-start | bytes 294920 | tf_op jit(solution)/shard_map/ppermute | solution.py:633
  45.6 6.2 %collective-permute-start.24 = (f32[192,128]{1,0:T(8,128)S(1)}, f32[192,128]{1,0:T(8,128)S(1)}, u32[]{:S(2)}, u32[]{:S(2)}) collective-permute-start(f32[192,128]{1,0:T(8,128)S(1)} %pad_maximum_fusion.5), channel_id=1, source_target_pairs={{0,6},{1,7},{2,4},{3,5},{4,2},{5,3},{6,0},{7,1},{8,14},{9,15},{10,... | collective-permute-start | bytes 294920 | tf_op jit(solution)/shard_map/ppermute | solution.py:633

commit v3 on v2

--- a/solution.py
+++ b/solution.py
@@ -19,6 +19,7 @@
 LANES = 128
 SUB = 8
 CHUNK = 3 * LANES
+FETCH = 6 * LANES
 RIM_NODES = [p for p in range(NODES) if p // SIDE in (0, 5) or p % SIDE in (0, 5)]
 CORE_NODES = [p for p in range(NODES) if p not in RIM_NODES]
 MID_NODES = [p for p in range(NODES) if p // SIDE not in (0, 5)]
@@ -145,11 +146,11 @@
     ]
     large = [
         pltpu.make_async_copy(
-            state_any.at[:, pl.ds(at, CHUNK)],
-            state_ref.at[:, pl.ds(at, CHUNK)],
-            sems.at[len(small) + at // CHUNK],
+            state_any.at[:, pl.ds(at, FETCH)],
+            state_ref.at[:, pl.ds(at, FETCH)],
+            sems.at[len(small) + at // FETCH],
         )
-        for at in range(0, width, CHUNK)
+        for at in range(0, width, FETCH)
     ]
     for copy in small + large:
         copy.start()
@@ -200,8 +201,8 @@
                 face = step & 1
         before = here
     for at in range(0, width, LANES):
-        if at % CHUNK == 0:
-            large[at // CHUNK].wait()
+        if at % FETCH == 0:
+            large[at // FETCH].wait()
         flat[pl.ds(at, LANES), :] = state_ref[:, pl.ds(at, LANES)].T
     facts_ref[...] = all_ref[:, :share]
     pick = pick_ref[...].astype(jnp.bfloat16)
@@ -332,20 +333,23 @@
                     two_ref[tile, var, at, :] = jnp.where(odd, up, down)
 
 
-def to_modes(dims, me, high_ref, low_ref, rates):
-    _, _, span, num_vars, modes = dims
+def mode_tables(dims, me, high_ref, low_ref):
+    _, _, span, _, modes = dims
+    return [
+        jnp.concatenate([ref[pl.ds((me ^ k) * modes, modes), :] for k in range(span)], axis=0)
+        for ref in (high_ref, low_ref)
+    ]
+
+
+def to_modes(tables, rate):
+    high, low = split(rate)
+    return mm_nt(high, tables[0]) + mm_nt(low, tables[0]) + mm_nt(high, tables[1])
+
+
+def by_target(dims, gains):
     lane = lax.broadcasted_iota(jnp.int32, (1, LANES), 1)
-    tables = []
-    for ref in (high_ref, low_ref):
-        tables.append(
-            jnp.concatenate([ref[pl.ds((me ^ k) * modes, modes), :] for k in range(span)], axis=0)
-        )
-    size = rates[0].shape[0]
-    high, low = split(jnp.concatenate(rates, axis=0))
-    gain = mm_nt(high, tables[0]) + mm_nt(low, tables[0]) + mm_nt(high, tables[1])
-    gains = [gain[var * size : (var + 1) * size] for var in range(num_vars)]
     out = []
-    for group in range(span // 4):
+    for group in range(dims[2] // 4):
         at = slice(group * LANES, (group + 1) * LANES)
         out += regroup([gain[:, at] for gain in gains], lane)
     return out
@@ -509,16 +513,20 @@
     count = span * modes
     faces = Faces(dims, facts_ref, phys_ref, core_ref, twin_ref)
     wanted = tuple(range(1, SIDE - 1))
-    for tile in range(count // LANES):
-        pace, far_pace = faces.pace_y(tile, wanted), faces.far_pace(tile, wanted)
-        for var in range(num_vars):
+    paces = [
+        (faces.pace_y(tile, wanted), faces.far_pace(tile, wanted)) for tile in range(count // LANES)
+    ]
+    tables = mode_tables(dims, me, high_ref, low_ref)
+    gains = []
+    for var in range(num_vars):
+        for tile in range(count // LANES):
             total = faces.volume(tile, var, wanted)
-            faces.faces_y(tile, var, pace, far_pace, wanted, total)
+            faces.faces_y(tile, var, *paces[tile], wanted, total)
             q, w = faces.reader(tile, var), faces.reader(tile, 2)
             store_rates(rate_ref, MID_NODES, tile, var, count, total, q, w)
-    parts = to_modes(dims, me, high_ref, low_ref, [rate_ref[var] for var in range(num_vars)])
-    for k in range(span):
-        outs[k][...] = parts[k]
+        gains.append(to_modes(tables, rate_ref[var]))
+    for k, part in enumerate(by_target(dims, gains)):
+        outs[k][...] = part
 
 
 def edges_kernel(
@@ -549,8 +557,10 @@
             faces.faces_y(tile, var, pace_y, far_pace, wanted, total)
             q, w = faces.reader(tile, var), faces.reader(tile, 2)
             store_rates(rate_ref, END_NODES, tile, var, count, total, q, w)
-    me = lax.axis_index("span")
-    parts = to_modes(dims, me, high_ref, low_ref, [rate_ref[var] for var in range(num_vars)])
+    tables = mode_tables(dims, lax.axis_index("span"), high_ref, low_ref)
+    rows = len(END_NODES) * share
+    gain = to_modes(tables, jnp.concatenate([rate_ref[var] for var in range(num_vars)], axis=0))
+    parts = by_target(dims, [gain[var * rows : (var + 1) * rows] for var in range(num_vars)])
     size = len(END_NODES) * share
     for k in range(span):
         if k % 2:
@@ -672,7 +682,7 @@
             pltpu.SMEM(rim.shape, jnp.int32),
             pltpu.SMEM(metric.shape, f32),
             pltpu.VMEM(flat_state.shape, f32),
-            pltpu.SemaphoreType.DMA((4 + chunks,)),
+            pltpu.SemaphoreType.DMA((4 + flat_size // FETCH,)),
         ],
         compiler_params=PARAMS,
         name="spread",
@@ -1002,6 +1012,7 @@
         and elems % rows == 0
         and SUB % (elems // rows) == 0
         and flat_size % CHUNK == 0
+        and flat_size % FETCH == 0
     )
     if not fits:
         return plain_body(state, metric, neighbour, orient, wall, rim)

time: 53.5 us -> 52.9 us (0.989)
  Pallas kernels: 9.29 us -> 8.74 us
  transfers between devices with their start and end apart: 25 -> 25, of which waited for: 10 -> 10; matrix products, arithmetic and copies ran while one was open for 0% -> 0% of each run, Pallas kernels for 7% -> 6%
where the time goes in v3:
time: 52.9 us; the launch traced here: 52.8 us
  starting transfers between devices  28.1 us (53%)
  waiting for transfers between devices  15.6 us (29%)
  Pallas kernels  8.74 us (17%)
    ppermute x14, starting transfers between devices, exchange(): lax.ppermute(blocks[k], 'span', [(s, s ^ k) for s in range(span)])  15.6 us
    ppermute x14, waiting for transfers between devices, exchange(): lax.ppermute(blocks[k], 'span', [(s, s ^ k) for s in range(span)])  9.83 us
    ppermute x6, starting transfers between devices, relayed(): both = lax.ppermute(both, 'span', [(s, s ^ 2 * at) for s in range(span)])  7.73 us
    ppermute x6, waiting for transfers between devices, relayed(): both = lax.ppermute(both, 'span', [(s, s ^ 2 * at) for s in range(span)])  5.76 us
    ppermute x1, starting transfers between devices, ordered_body(): lax.ppermute(two, 'elem', [(g, (g - 1 if g % 2 == 0 else g + 1) % groups)...  2.48 us
    pallas_call x1, Pallas kernels, ordered_body(): pl.pallas_call(functools.partial(spread_kernel, (rows, cols, share, span)...  2.41 us
    pallas_call x1, Pallas kernels, ordered_body(): *mids, core = rates(facts, *forward, *backward, phys, twin, *core_takes)  2.21 us
    ppermute x1, starting transfers between devices, ordered_body(): one = lax.ppermute(one, 'elem', [(g, g ^ 1) for g in range(groups)])  1.58 us
  transfers between devices with their start and end apart: 25, of which 10 were waited for; matrix products, arithmetic and copies ran while one was open for 0% of the time, Pallas kernels for 6%

profile of v3, /device:TPU:0, one launch (start us, length us, event | category | flops | bytes accessed | tf_op | source)
XLA Modules:
  0.0 52.8 jit_solution(1652911039384126627)
XLA Ops:
  0.0 0.0 copy-start.3
  0.0 2.4 %spread.1 = (f32[184,128]{1,0:T(8,128)S(1)}, f32[184,128]{1,0:T(8,128)S(1)}, f32[184,128]{1,0:T(8,128)S(1)}, f32[184,128]{1,0:T(8,128)S(1)}, f32[184,128]{1,0:T(...) custom-call(s32[4,64]{1,0:T(4,128)} %bitcast.6, ...), custom_call_target="tpu_custom_call" | custom-call | tf_op jit(solution)/shard_map/spread/pallas_call | solution.py:666
  2.4 0.2 spread_core.1
  2.6 0.6 %collective-permute-start.8 = (f32[512,128]{1,0:T(8,128)S(1)}, f32[512,128]{1,0:T(8,128)S(1)}, u32[]{:S(2)}, u32[]{:S(2)}) collective-permute-start(f32[512,128]{1,0:T(8,128)S(1)} %get-tuple-element.54), channel_id=1, source_target_pairs={{0,1},{1,0},{2,3},{3,2},{4,5},{5,4},{6,7},{7,6},{8,9},{9,8},{10,11... | collective-permute-start | bytes 786440 | tf_op jit(solution)/shard_map/ppermute | solution.py:639
  3.2 0.1 collective-permute-start
  3.3 2.9 %collective-permute-start.1 = (f32[184,128]{1,0:T(8,128)S(1)}, f32[184,128]{1,0:T(8,128)S(1)}, u32[]{:S(2)}, u32[]{:S(2)}) collective-permute-start(f32[184,128]{1,0:T(8,128)S(1)} %get-tuple-element.44), channel_id=1, source_target_pairs={{0,2},{1,3},{2,0},{3,1},{4,6},{5,7},{6,4},{7,5},{8,10},{9,11},{10,... | collective-permute-start | bytes 282632 | tf_op jit(solution)/shard_map/ppermute | solution.py:633
  6.2 0.0 collective-permute-start.2
  6.2 1.5 %collective-permute-start.3 = (f32[184,128]{1,0:T(8,128)S(1)}, f32[184,128]{1,0:T(8,128)S(1)}, u32[]{:S(2)}, u32[]{:S(2)}) collective-permute-start(f32[184,128]{1,0:T(8,128)S(1)} %get-tuple-element.46), channel_id=1, source_target_pairs={{0,4},{1,5},{2,6},{3,7},{4,0},{5,1},{6,2},{7,3},{8,12},{9,13},{10,... | collective-permute-start | bytes 282632 | tf_op jit(solution)/shard_map/ppermute | solution.py:633
  7.7 0.0 collective-permute-done.refs_1_
  7.7 0.3 collective-permute-start.4
  8.0 1.3 %collective-permute-done.1.refs_2_ = f32[184,128]{1,0:T(8,128)S(1)} collective-permute-done((f32[184,128]{1,0:T(8,128)S(1)}, f32[184,128]{1,0:T(8,128)S(1)}, u32[]{:S(2)}, u32[]{:S(2)}) %collective-permute-start.1) | collective-permute-done | bytes 94240 | tf_op jit(solution)/shard_map/ppermute | solution.py:633
  9.3 3.4 %collective-permute-start.5 = (f32[184,128]{1,0:T(8,128)S(1)}, f32[184,128]{1,0:T(8,128)S(1)}, u32[]{:S(2)}, u32[]{:S(2)}) collective-permute-start(f32[184,128]{1,0:T(8,128)S(1)} %get-tuple-element.48), channel_id=1, source_target_pairs={{0,6},{1,7},{2,4},{3,5},{4,2},{5,3},{6,0},{7,1},{8,14},{9,15},{10,... | collective-permute-start | bytes 282632 | tf_op jit(solution)/shard_map/ppermute | solution.py:633
  12.7 0.0 collective-permute-done.2.refs_3_
  12.7 1.1 %collective-permute-start.6 = (f32[184,128]{1,0:T(8,128)S(1)}, f32[184,128]{1,0:T(8,128)S(1)}, u32[]{:S(2)}, u32[]{:S(2)}) collective-permute-start(f32[184,128]{1,0:T(8,128)S(1)} %get-tuple-element.49), channel_id=1, source_target_pairs={{0,7},{1,6},{2,5},{3,4},{4,3},{5,2},{6,1},{7,0},{8,15},{9,14},{10,... | collective-permute-start | bytes 282632 | tf_op jit(solution)/shard_map/ppermute | solution.py:633
  13.8 0.0 collective-permute-done.3.refs_4_
  13.8 0.7 %collective-permute-done.4.refs_5_ = f32[184,128]{1,0:T(8,128)S(1)} collective-permute-done((f32[184,128]{1,0:T(8,128)S(1)}, f32[184,128]{1,0:T(8,128)S(1)}, u32[]{:S(2)}, u32[]{:S(2)}) %collective-permute-start.4) | collective-permute-done | bytes 94240 | tf_op jit(solution)/shard_map/ppermute | solution.py:633
  14.6 0.9 %collective-permute-done.5.refs_6_ = f32[184,128]{1,0:T(8,128)S(1)} collective-permute-done((f32[184,128]{1,0:T(8,128)S(1)}, f32[184,128]{1,0:T(8,128)S(1)}, u32[]{:S(2)}, u32[]{:S(2)}) %collective-permute-start.5) | collective-permute-done | bytes 94240 | tf_op jit(solution)/shard_map/ppermute | solution.py:633
  15.5 2.1 %collective-permute-done.6.refs_7_ = f32[184,128]{1,0:T(8,128)S(1)} collective-permute-done((f32[184,128]{1,0:T(8,128)S(1)}, f32[184,128]{1,0:T(8,128)S(1)}, u32[]{:S(2)}, u32[]{:S(2)}) %collective-permute-start.6) | collective-permute-done | bytes 94240 | tf_op jit(solution)/shard_map/ppermute | solution.py:633
  17.6 0.0 copy-done.3
  17.6 0.0 copy-done.4
  17.6 0.8 %planes.1 = (f32[2,4,184,128]{3,2,1,0:T(8,128)S(1)}, f32[2,4,24,128]{3,2,1,0:T(8,128)S(1)}, f32[2,4,12,128]{3,2,1,0:T(8,128)S(1)}, f32[2,4,12,128]{3,2,1,0:T(8,128)S(1)}) custom-call(f32[4,8,128]{2,1,0:T(8,128)S(1)} %get-tuple-element.41.facts_ref, bf16[256,256]{1,0:T(8,128)(2,1)S(1)} %copy-done.4, bf16[256,256]{1,0:T(8,128)(2,1)S(1)} %copy-done.3, ...), custom_call_target="tpu_custom_call" | custom-call | tf_op jit(solution)/shard_map/planes/pallas_call | solution.py:721
  18.4 0.1 collective-permute-start.7
  18.5 0.0 collective-permute-done.8
  18.5 1.5 %collective-permute-start.9 = (f32[256,128]{1,0:T(8,128)S(1)}, f32[256,128]{1,0:T(8,128)S(1)}, u32[]{:S(2)}, u32[]{:S(2)}) collective-permute-start(f32[256,128]{1,0:T(8,128)S(1)} %pad_maximum_fusion), channel_id=1, source_target_pairs={{0,2},{1,3},{2,0},{3,1},{4,6},{5,7},{6,4},{7,5},{8,10},{9,11},{10,... | collective-permute-start | bytes 393224 | tf_op jit(solution)/shard_map/ppermute | solution.py:643
  20.1 1.3 %collective-permute-start.10 = (f32[256,128]{1,0:T(8,128)S(1)}, f32[256,128]{1,0:T(8,128)S(1)}, u32[]{:S(2)}, u32[]{:S(2)}) collective-permute-start(f32[256,128]{1,0:T(8,128)S(1)} %pad_maximum_fusion.1), channel_id=1, source_target_pairs={{0,4},{1,5},{2,6},{3,7},{4,0},{5,1},{6,2},{7,3},{8,12},{9,13},{10,... | collective-permute-start | bytes 393224 | tf_op jit(solution)/shard_map/ppermute | solution.py:643
  21.4 0.9 %collective-permute-start.11 = (f32[256,128]{1,0:T(8,128)S(1)}, f32[256,128]{1,0:T(8,128)S(1)}, u32[]{:S(2)}, u32[]{:S(2)}) collective-permute-start(f32[256,128]{1,0:T(8,128)S(1)} %pad_maximum_fusion.2), channel_id=1, source_target_pairs={{0,6},{1,7},{2,4},{3,5},{4,2},{5,3},{6,0},{7,1},{8,14},{9,15},{10,... | collective-permute-start | bytes 393224 | tf_op jit(solution)/shard_map/ppermute | solution.py:643
  22.3 1.6 %collective-permute-start.19 = (f32[2,4,12,128]{3,2,1,0:T(8,128)S(1)}, f32[2,4,12,128]{3,2,1,0:T(8,128)S(1)}, u32[]{:S(2)}, u32[]{:S(2)}) collective-permute-start(f32[2,4,12,128]{3,2,1,0:T(8,128)S(1)} %get-tuple-element.67), channel_id=1, source_target_pairs={{0,8},{8,0},{16,24},{24,16},{1,9},{9,1},{17,25},{25,17},{2,10},{10... | collective-permute-start | bytes 147464 | tf_op jit(solution)/shard_map/ppermute | solution.py:723
  23.8 0.0 collective-permute-done.7.twin_ref
  23.8 2.5 %collective-permute-start.20 = (f32[2,4,12,128]{3,2,1,0:T(8,128)S(1)}, f32[2,4,12,128]{3,2,1,0:T(8,128)S(1)}, u32[]{:S(2)}, u32[]{:S(2)}) collective-permute-start(f32[2,4,12,128]{3,2,1,0:T(8,128)S(1)} %get-tuple-element.68), channel_id=1, source_target_pairs={{0,24},{8,16},{16,8},{24,0},{1,25},{9,17},{17,9},{25,1},{2,26},{10... | collective-permute-start | bytes 147464 | tf_op jit(solution)/shard_map/ppermute | solution.py:724
  26.3 0.0 collective-permute-done.9.refs_2_
  26.3 0.6 %collective-permute-done.10.refs_3_ = f32[256,128]{1,0:T(8,128)S(1)} collective-permute-done((f32[256,128]{1,0:T(8,128)S(1)}, f32[256,128]{1,0:T(8,128)S(1)}, u32[]{:S(2)}, u32[]{:S(2)}) %collective-permute-start.10) | collective-permute-done | bytes 131104 | tf_op jit(solution)/shard_map/ppermute | solution.py:643
  26.9 1.2 %collective-permute-done.11.refs_4_ = f32[256,128]{1,0:T(8,128)S(1)} collective-permute-done((f32[256,128]{1,0:T(8,128)S(1)}, f32[256,128]{1,0:T(8,128)S(1)}, u32[]{:S(2)}, u32[]{:S(2)}) %collective-permute-start.11) | collective-permute-done | bytes 131104 | tf_op jit(solution)/shard_map/ppermute | solution.py:643
  28.1 0.0 copy-done.1
  28.1 0.0 copy-done.2
  28.1 2.2 %rates.1 = (f32[192,128]{1,0:T(8,128)S(1)}, f32[192,128]{1,0:T(8,128)S(1)}, f32[192,128]{1,0:T(8,128)S(1)}, f32[192,128]{1,0:T(8,128)S(1)}, f32[192,128]{1,0:T(8...) custom-call(f32[4,8,128]{2,1,0:T(8,128)S(1)} %get-tuple-element.41.f, ...), custom_call_target="tpu_custom_call" | custom-call | tf_op jit(solution)/shard_map/rates/pallas_call | solution.py:738
  30.3 0.0 collective-permute-done.19.one_ref
  30.3 0.0 collective-permute-done.20.two_ref
  30.3 1.2 %edges.1 = (f32[384,128]{1,0:T(8,128)S(1)}, f32[96,128]{1,0:T(8,128)S(1)}, f32[96,128]{1,0:T(8,128)S(1)}, f32[96,128]{1,0:T(8,128)S(1)}, f32[96,128]{1,0:T(8,128)S(1)}) custom-call(f32[4,8,128]{2,1,0:T(8,128)S(1)} %get-tuple-element.41.facts_ref, bf16[256,512]{1,0:T(8,128)(2,1)S(1)} %copy-done.2, bf16[256,512]{1,0:T(8,128)(2,1)S(1)} %copy-done.1, ...), custom_call_target="tpu_custom_call" | custom-call | tf_op jit(solution)/shard_map/edges/pallas_call | solution.py:750
  31.5 0.1 collective-permute-start.21
  31.6 0.5 collective-permute-start.12
  32.1 1.1 %collective-permute-start.13 = (f32[192,128]{1,0:T(8,128)S(1)}, f32[192,128]{1,0:T(8,128)S(1)}, u32[]{:S(2)}, u32[]{:S(2)}) collective-permute-start(f32[192,128]{1,0:T(8,128)S(1)} %get-tuple-element.60), channel_id=1, source_target_pairs={{0,2},{1,3},{2,0},{3,1},{4,6},{5,7},{6,4},{7,5},{8,10},{9,11},{10,... | collective-permute-start | bytes 294920 | tf_op jit(solution)/shard_map/ppermute | solution.py:633
  33.2 0.4 collective-permute-start.14
  33.5 1.3 %collective-permute-start.15 = (f32[192,128]{1,0:T(8,128)S(1)}, f32[192,128]{1,0:T(8,128)S(1)}, u32[]{:S(2)}, u32[]{:S(2)}) collective-permute-start(f32[192,128]{1,0:T(8,128)S(1)} %get-tuple-element.62), channel_id=1, source_target_pairs={{0,4},{1,5},{2,6},{3,7},{4,0},{5,1},{6,2},{7,3},{8,12},{9,13},{10,... | collective-permute-start | bytes 294920 | tf_op jit(solution)/shard_map/ppermute | solution.py:633
  34.8 0.0 collective-permute-done.21
  34.8 0.8 %collective-permute-start.16 = (f32[192,128]{1,0:T(8,128)S(1)}, f32[192,128]{1,0:T(8,128)S(1)}, u32[]{:S(2)}, u32[]{:S(2)}) collective-permute-start(f32[192,128]{1,0:T(8,128)S(1)} %get-tuple-element.63), channel_id=1, source_target_pairs={{0,5},{1,4},{2,7},{3,6},{4,1},{5,0},{6,3},{7,2},{8,13},{9,12},{10,... | collective-permute-start | bytes 294920 | tf_op jit(solution)/shard_map/ppermute | solution.py:633
  35.6 0.0 copy-start
  35.7 0.0 collective-permute-done.12.refs_1_
  35.7 1.9 %collective-permute-start.17 = (f32[192,128]{1,0:T(8,128)S(1)}, f32[192,128]{1,0:T(8,128)S(1)}, u32[]{:S(2)}, u32[]{:S(2)}) collective-permute-start(f32[192,128]{1,0:T(8,128)S(1)} %get-tuple-element.64), channel_id=1, source_target_pairs={{0,6},{1,7},{2,4},{3,5},{4,2},{5,3},{6,0},{7,1},{8,14},{9,15},{10,... | collective-permute-start | bytes 294920 | tf_op jit(solution)/shard_map/ppermute | solution.py:633
  37.6 0.0 collective-permute-done.13.refs_2_
  37.6 0.5 collective-permute-start.18
  38.1 0.2 collective-permute-done.14.refs_3_
  38.2 1.0 %collective-permute-start.22 = (f32[192,128]{1,0:T(8,128)S(1)}, f32[192,128]{1,0:T(8,128)S(1)}, u32[]{:S(2)}, u32[]{:S(2)}) collective-permute-start(f32[192,128]{1,0:T(8,128)S(1)} %pad_maximum_fusion.3), channel_id=1, source_target_pairs={{0,2},{1,3},{2,0},{3,1},{4,6},{5,7},{6,4},{7,5},{8,10},{9,11},{10,... | collective-permute-start | bytes 294920 | tf_op jit(solution)/shard_map/ppermute | solution.py:643
  39.2 0.0 collective-permute-done.15.refs_4_
  39.2 1.3 %collective-permute-start.23 = (f32[192,128]{1,0:T(8,128)S(1)}, f32[192,128]{1,0:T(8,128)S(1)}, u32[]{:S(2)}, u32[]{:S(2)}) collective-permute-start(f32[192,128]{1,0:T(8,128)S(1)} %pad_maximum_fusion.4), channel_id=1, source_target_pairs={{0,4},{1,5},{2,6},{3,7},{4,0},{5,1},{6,2},{7,3},{8,12},{9,13},{10,... | collective-permute-start | bytes 294920 | tf_op jit(solution)/shard_map/ppermute | solution.py:643
  40.5 4.5 %collective-permute-done.16.refs_5_ = f32[192,128]{1,0:T(8,128)S(1)} collective-permute-done((f32[192,128]{1,0:T(8,128)S(1)}, f32[192,128]{1,0:T(8,128)S(1)}, u32[]{:S(2)}, u32[]{:S(2)}) %collective-permute-start.16) | collective-permute-done | bytes 98336 | tf_op jit(solution)/shard_map/ppermute | solution.py:633
  45.0 1.8 %collective-permute-start.24 = (f32[192,128]{1,0:T(8,128)S(1)}, f32[192,128]{1,0:T(8,128)S(1)}, u32[]{:S(2)}, u32[]{:S(2)}) collective-permute-start(f32[192,128]{1,0:T(8,128)S(1)} %pad_maximum_fusion.5), channel_id=1, source_target_pairs={{0,6},{1,7},{2,4},{3,5},{4,2},{5,3},{6,0},{7,1},{8,14},{9,15},{10,... | collective-permute-start | bytes 294920 | tf_op jit(solution)/shard_map/ppermute | solution.py:643
  46.8 0.0 collective-permute-done.17.refs_6_
  46.8 0.0 collective-permute-done.18.refs_7_
  46.8 0.4 collect.1.flat_in
  47.2 0.0 collective-permute-done.22.refs_2_
  47.2 0.2 collective-permute-done.23.refs_3_
  47.4 3.8 %collective-permute-done.24.refs_4_ = f32[192,128]{1,0:T(8,128)S(1)} collective-permute-done((f32[192,128]{1,0:T(8,128)S(1)}, f32[192,128]{1,0:T(8,128)S(1)}, u32[]{:S(2)}, u32[]{:S(2)}) %collective-permute-start.24) | collective-permute-done | bytes 98336 | tf_op jit(solution)/shard_map/ppermute | solution.py:643
  51.2 0.0 copy-done
  51.2 1.6 %finish.1 = (f32[128,2304]{1,0:T(8,128)}, f32[2304,128]{1,0:T(8,128)S(1)}) custom-call(f32[64,128]{1,0:T(8,128)S(1)} %get-tuple-element.40.pick_ref, f32[128,2304]{1,0:T(8,128)S(1)} %bitcast.5, f32[2304,128]{1,0:T(8,128)S(1)} %collect.1.flat_in, f32[96,128]{1,0:T(8,128)S(1)} %get-tuple-element.69.refs_0_, ...), custom_call_target="tpu_custom_call", output_to_operand_aliasing={{1}: (2, {})} | custom-call | tf_op jit(solution)/shard_map/finish/pallas_call | solution.py:764
  (11 shorter events, 0.1 us)
Async XLA Ops:
  0.0 17.6 %copy-start.3 = (bf16[256,256]{1,0:T(8,128)(2,1)S(1)}, bf16[256,256]{1,0:T(8,128)(2,1)}, u32[]{:S(2)}) copy-start(bf16[256,256]{1,0:T(8,128)(2,1)} %constant.9.clone.low_ref.there_low) | copy-start | bytes 393220
  0.0 17.6 %copy-start.4 = (bf16[256,256]{1,0:T(8,128)(2,1)S(1)}, bf16[256,256]{1,0:T(8,128)(2,1)}, u32[]{:S(2)}) copy-start(bf16[256,256]{1,0:T(8,128)(2,1)} %constant.8.clone.high_ref.there_high) | copy-start | bytes 393220
  2.6 15.8 %collective-permute-start.8 = (f32[512,128]{1,0:T(8,128)S(1)}, f32[512,128]{1,0:T(8,128)S(1)}, u32[]{:S(2)}, u32[]{:S(2)}) collective-permute-start(f32[512,128]{1,0:T(8,128)S(1)} %get-tuple-element.54), channel_id=1, source_target_pairs={{0,1},{1,0},{2,3},{3,2},{4,5},{5,4},{6,7},{7,6},{8,9},{9,8},{10,11... | collective-permute-start | bytes 786440 | tf_op jit(solution)/shard_map/ppermute | solution.py:639
  3.2 4.5 %collective-permute-start = (f32[184,128]{1,0:T(8,128)S(1)}, f32[184,128]{1,0:T(8,128)S(1)}, u32[]{:S(2)}, u32[]{:S(2)}) collective-permute-start(f32[184,128]{1,0:T(8,128)S(1)} %get-tuple-element.43), channel_id=1, source_target_pairs={{0,1},{1,0},{2,3},{3,2},{4,5},{5,4},{6,7},{7,6},{8,9},{9,8},{10,11... | collective-permute-start | bytes 282632 | tf_op jit(solution)/shard_map/ppermute | solution.py:633
  3.3 6.0 %collective-permute-start.1 = (f32[184,128]{1,0:T(8,128)S(1)}, f32[184,128]{1,0:T(8,128)S(1)}, u32[]{:S(2)}, u32[]{:S(2)}) collective-permute-start(f32[184,128]{1,0:T(8,128)S(1)} %get-tuple-element.44), channel_id=1, source_target_pairs={{0,2},{1,3},{2,0},{3,1},{4,6},{5,7},{6,4},{7,5},{8,10},{9,11},{10,... | collective-permute-start | bytes 282632 | tf_op jit(solution)/shard_map/ppermute | solution.py:633
  6.2 6.5 %collective-permute-start.2 = (f32[184,128]{1,0:T(8,128)S(1)}, f32[184,128]{1,0:T(8,128)S(1)}, u32[]{:S(2)}, u32[]{:S(2)}) collective-permute-start(f32[184,128]{1,0:T(8,128)S(1)} %get-tuple-element.45), channel_id=1, source_target_pairs={{0,3},{1,2},{2,1},{3,0},{4,7},{5,6},{6,5},{7,4},{8,11},{9,10},{10,... | collective-permute-start | bytes 282632 | tf_op jit(solution)/shard_map/ppermute | solution.py:633
  6.2 7.6 %collective-permute-start.3 = (f32[184,128]{1,0:T(8,128)S(1)}, f32[184,128]{1,0:T(8,128)S(1)}, u32[]{:S(2)}, u32[]{:S(2)}) collective-permute-start(f32[184,128]{1,0:T(8,128)S(1)} %get-tuple-element.46), channel_id=1, source_target_pairs={{0,4},{1,5},{2,6},{3,7},{4,0},{5,1},{6,2},{7,3},{8,12},{9,13},{10,... | collective-permute-start | bytes 282632 | tf_op jit(solution)/shard_map/ppermute | solution.py:633
  7.7 6.9 %collective-permute-start.4 = (f32[184,128]{1,0:T(8,128)S(1)}, f32[184,128]{1,0:T(8,128)S(1)}, u32[]{:S(2)}, u32[]{:S(2)}) collective-permute-start(f32[184,128]{1,0:T(8,128)S(1)} %get-tuple-element.47), channel_id=1, source_target_pairs={{0,5},{1,4},{2,7},{3,6},{4,1},{5,0},{6,3},{7,2},{8,13},{9,12},{10,... | collective-permute-start | bytes 282632 | tf_op jit(solution)/shard_map/ppermute | solution.py:633
  9.3 6.2 %collective-permute-start.5 = (f32[184,128]{1,0:T(8,128)S(1)}, f32[184,128]{1,0:T(8,128)S(1)}, u32[]{:S(2)}, u32[]{:S(2)}) collective-permute-start(f32[184,128]{1,0:T(8,128)S(1)} %get-tuple-element.48), channel_id=1, source_target_pairs={{0,6},{1,7},{2,4},{3,5},{4,2},{5,3},{6,0},{7,1},{8,14},{9,15},{10,... | collective-permute-start | bytes 282632 | tf_op jit(solution)/shard_map/ppermute | solution.py:633
  12.7 4.9 %collective-permute-start.6 = (f32[184,128]{1,0:T(8,128)S(1)}, f32[184,128]{1,0:T(8,128)S(1)}, u32[]{:S(2)}, u32[]{:S(2)}) collective-permute-start(f32[184,128]{1,0:T(8,128)S(1)} %get-tuple-element.49), channel_id=1, source_target_pairs={{0,7},{1,6},{2,5},{3,4},{4,3},{5,2},{6,1},{7,0},{8,15},{9,14},{10,... | collective-permute-start | bytes 282632 | tf_op jit(solution)/shard_map/ppermute | solution.py:633
  17.6 10.5 %copy-start.1 = (bf16[256,512]{1,0:T(8,128)(2,1)S(1)}, bf16[256,512]{1,0:T(8,128)(2,1)}, u32[]{:S(2)}) copy-start(bf16[256,512]{1,0:T(8,128)(2,1)} %constant.11.clone.low_ref) | copy-start | bytes 786436
  17.6 10.5 %copy-start.2 = (bf16[256,512]{1,0:T(8,128)(2,1)S(1)}, bf16[256,512]{1,0:T(8,128)(2,1)}, u32[]{:S(2)}) copy-start(bf16[256,512]{1,0:T(8,128)(2,1)} %constant.10.clone.high_ref) | copy-start | bytes 786436
  18.4 5.4 %collective-permute-start.7 = (f32[2,4,24,128]{3,2,1,0:T(8,128)S(1)}, f32[2,4,24,128]{3,2,1,0:T(8,128)S(1)}, u32[]{:S(2)}, u32[]{:S(2)}) collective-permute-start(f32[2,4,24,128]{3,2,1,0:T(8,128)S(1)} %get-tuple-element.51), channel_id=1, source_target_pairs={{0,1},{1,0},{2,3},{3,2},{4,5},{5,4},{6,7},{7,6},{8,9},{9,8},{10,11... | collective-permute-start | bytes 294920 | tf_op jit(solution)/shard_map/ppermute | solution.py:722
  18.5 7.8 %collective-permute-start.9 = (f32[256,128]{1,0:T(8,128)S(1)}, f32[256,128]{1,0:T(8,128)S(1)}, u32[]{:S(2)}, u32[]{:S(2)}) collective-permute-start(f32[256,128]{1,0:T(8,128)S(1)} %pad_maximum_fusion), channel_id=1, source_target_pairs={{0,2},{1,3},{2,0},{3,1},{4,6},{5,7},{6,4},{7,5},{8,10},{9,11},{10,... | collective-permute-start | bytes 393224 | tf_op jit(solution)/shard_map/ppermute | solution.py:643
  20.1 6.8 %collective-permute-start.10 = (f32[256,128]{1,0:T(8,128)S(1)}, f32[256,128]{1,0:T(8,128)S(1)}, u32[]{:S(2)}, u32[]{:S(2)}) collective-permute-start(f32[256,128]{1,0:T(8,128)S(1)} %pad_maximum_fusion.1), channel_id=1, source_target_pairs={{0,4},{1,5},{2,6},{3,7},{4,0},{5,1},{6,2},{7,3},{8,12},{9,13},{10,... | collective-permute-start | bytes 393224 | tf_op jit(solution)/shard_map/ppermute | solution.py:643
  21.4 6.7 %collective-permute-start.11 = (f32[256,128]{1,0:T(8,128)S(1)}, f32[256,128]{1,0:T(8,128)S(1)}, u32[]{:S(2)}, u32[]{:S(2)}) collective-permute-start(f32[256,128]{1,0:T(8,128)S(1)} %pad_maximum_fusion.2), channel_id=1, source_target_pairs={{0,6},{1,7},{2,4},{3,5},{4,2},{5,3},{6,0},{7,1},{8,14},{9,15},{10,... | collective-permute-start | bytes 393224 | tf_op jit(solution)/shard_map/ppermute | solution.py:643
  22.3 8.0 %collective-permute-start.19 = (f32[2,4,12,128]{3,2,1,0:T(8,128)S(1)}, f32[2,4,12,128]{3,2,1,0:T(8,128)S(1)}, u32[]{:S(2)}, u32[]{:S(2)}) collective-permute-start(f32[2,4,12,128]{3,2,1,0:T(8,128)S(1)} %get-tuple-element.67), channel_id=1, source_target_pairs={{0,8},{8,0},{16,24},{24,16},{1,9},{9,1},{17,25},{25,17},{2,10},{10... | collective-permute-start | bytes 147464 | tf_op jit(solution)/shard_map/ppermute | solution.py:723
  23.8 6.5 %collective-permute-start.20 = (f32[2,4,12,128]{3,2,1,0:T(8,128)S(1)}, f32[2,4,12,128]{3,2,1,0:T(8,128)S(1)}, u32[]{:S(2)}, u32[]{:S(2)}) collective-permute-start(f32[2,4,12,128]{3,2,1,0:T(8,128)S(1)} %get-tuple-element.68), channel_id=1, source_target_pairs={{0,24},{8,16},{16,8},{24,0},{1,25},{9,17},{17,9},{25,1},{2,26},{10... | collective-permute-start | bytes 147464 | tf_op jit(solution)/shard_map/ppermute | solution.py:724
  31.5 3.3 %collective-permute-start.21 = (f32[384,128]{1,0:T(8,128)S(1)}, f32[384,128]{1,0:T(8,128)S(1)}, u32[]{:S(2)}, u32[]{:S(2)}) collective-permute-start(f32[384,128]{1,0:T(8,128)S(1)} %get-tuple-element.70), channel_id=1, source_target_pairs={{0,1},{1,0},{2,3},{3,2},{4,5},{5,4},{6,7},{7,6},{8,9},{9,8},{10,11... | collective-permute-start | bytes 589832 | tf_op jit(solution)/shard_map/ppermute | solution.py:639
  31.6 4.1 %collective-permute-start.12 = (f32[192,128]{1,0:T(8,128)S(1)}, f32[192,128]{1,0:T(8,128)S(1)}, u32[]{:S(2)}, u32[]{:S(2)}) collective-permute-start(f32[192,128]{1,0:T(8,128)S(1)} %get-tuple-element.59), channel_id=1, source_target_pairs={{0,1},{1,0},{2,3},{3,2},{4,5},{5,4},{6,7},{7,6},{8,9},{9,8},{10,11... | collective-permute-start | bytes 294920 | tf_op jit(solution)/shard_map/ppermute | solution.py:633
  32.1 5.5 %collective-permute-start.13 = (f32[192,128]{1,0:T(8,128)S(1)}, f32[192,128]{1,0:T(8,128)S(1)}, u32[]{:S(2)}, u32[]{:S(2)}) collective-permute-start(f32[192,128]{1,0:T(8,128)S(1)} %get-tuple-element.60), channel_id=1, source_target_pairs={{0,2},{1,3},{2,0},{3,1},{4,6},{5,7},{6,4},{7,5},{8,10},{9,11},{10,... | collective-permute-start | bytes 294920 | tf_op jit(solution)/shard_map/ppermute | solution.py:633
  33.2 5.1 %collective-permute-start.14 = (f32[192,128]{1,0:T(8,128)S(1)}, f32[192,128]{1,0:T(8,128)S(1)}, u32[]{:S(2)}, u32[]{:S(2)}) collective-permute-start(f32[192,128]{1,0:T(8,128)S(1)} %get-tuple-element.61), channel_id=1, source_target_pairs={{0,3},{1,2},{2,1},{3,0},{4,7},{5,6},{6,5},{7,4},{8,11},{9,10},{10,... | collective-permute-start | bytes 294920 | tf_op jit(solution)/shard_map/ppermute | solution.py:633
  33.5 5.7 %collective-permute-start.15 = (f32[192,128]{1,0:T(8,128)S(1)}, f32[192,128]{1,0:T(8,128)S(1)}, u32[]{:S(2)}, u32[]{:S(2)}) collective-permute-start(f32[192,128]{1,0:T(8,128)S(1)} %get-tuple-element.62), channel_id=1, source_target_pairs={{0,4},{1,5},{2,6},{3,7},{4,0},{5,1},{6,2},{7,3},{8,12},{9,13},{10,... | collective-permute-start | bytes 294920 | tf_op jit(solution)/shard_map/ppermute | solution.py:633
  34.8 10.2 %collective-permute-start.16 = (f32[192,128]{1,0:T(8,128)S(1)}, f32[192,128]{1,0:T(8,128)S(1)}, u32[]{:S(2)}, u32[]{:S(2)}) collective-permute-start(f32[192,128]{1,0:T(8,128)S(1)} %get-tuple-element.63), channel_id=1, source_target_pairs={{0,5},{1,4},{2,7},{3,6},{4,1},{5,0},{6,3},{7,2},{8,13},{9,12},{10,... | collective-permute-start | bytes 294920 | tf_op jit(solution)/shard_map/ppermute | solution.py:633
  35.6 15.6 %copy-start = (f32[4,32,2304]{2,1,0:T(8,128)S(1)}, f32[4,32,2304]{2,1,0:T(8,128)}, u32[]{:S(2)}) copy-start(f32[4,32,2304]{2,1,0:T(8,128)} %param.10) | copy-start | bytes 3538948
  35.7 11.1 %collective-permute-start.17 = (f32[192,128]{1,0:T(8,128)S(1)}, f32[192,128]{1,0:T(8,128)S(1)}, u32[]{:S(2)}, u32[]{:S(2)}) collective-permute-start(f32[192,128]{1,0:T(8,128)S(1)} %get-tuple-element.64), channel_id=1, source_target_pairs={{0,6},{1,7},{2,4},{3,5},{4,2},{5,3},{6,0},{7,1},{8,14},{9,15},{10,... | collective-permute-start | bytes 294920 | tf_op jit(solution)/shard_map/ppermute | solution.py:633
  37.6 9.2 %collective-permute-start.18 = (f32[192,128]{1,0:T(8,128)S(1)}, f32[192,128]{1,0:T(8,128)S(1)}, u32[]{:S(2)}, u32[]{:S(2)}) collective-permute-start(f32[192,128]{1,0:T(8,128)S(1)} %get-tuple-element.65), channel_id=1, source_target_pairs={{0,7},{1,6},{2,5},{3,4},{4,3},{5,2},{6,1},{7,0},{8,15},{9,14},{10,... | collective-permute-start | bytes 294920 | tf_op jit(solution)/shard_map/ppermute | solution.py:633
  38.2 9.0 %collective-permute-start.22 = (f32[192,128]{1,0:T(8,128)S(1)}, f32[192,128]{1,0:T(8,128)S(1)}, u32[]{:S(2)}, u32[]{:S(2)}) collective-permute-start(f32[192,128]{1,0:T(8,128)S(1)} %pad_maximum_fusion.3), channel_id=1, source_target_pairs={{0,2},{1,3},{2,0},{3,1},{4,6},{5,7},{6,4},{7,5},{8,10},{9,11},{10,... | collective-permute-start | bytes 294920 | tf_op jit(solution)/shard_map/ppermute | solution.py:643
  39.2 8.1 %collective-permute-start.23 = (f32[192,128]{1,0:T(8,128)S(1)}, f32[192,128]{1,0:T(8,128)S(1)}, u32[]{:S(2)}, u32[]{:S(2)}) collective-permute-start(f32[192,128]{1,0:T(8,128)S(1)} %pad_maximum_fusion.4), channel_id=1, source_target_pairs={{0,4},{1,5},{2,6},{3,7},{4,0},{5,1},{6,2},{7,3},{8,12},{9,13},{10,... | collective-permute-start | bytes 294920 | tf_op jit(solution)/shard_map/ppermute | solution.py:643
  45.0 6.2 %collective-permute-start.24 = (f32[192,128]{1,0:T(8,128)S(1)}, f32[192,128]{1,0:T(8,128)S(1)}, u32[]{:S(2)}, u32[]{:S(2)}) collective-permute-start(f32[192,128]{1,0:T(8,128)S(1)} %pad_maximum_fusion.5), channel_id=1, source_target_pairs={{0,6},{1,7},{2,4},{3,5},{4,2},{5,3},{6,0},{7,1},{8,14},{9,15},{10,... | collective-permute-start | bytes 294920 | tf_op jit(solution)/shard_map/ppermute | solution.py:643
